TPU v7x, 32 devices: a whole 2x2x4 slice. The times are simulated.
32 devices in a mesh: view: 8 (over z, x), head: 4 (over y, core).
Axes of the slice: x: 2, y: 2, z: 4, core: 2. Of those that a mesh axis runs over, the one named last changes fastest.
Arguments:
- features: bfloat16 [16384, 1024], P(('view', 'head')), may hold values from -6 to 6
- attend_weight: bfloat16 [2, 3, 1024, 1024], P(None, None, 'view', 'head'), may hold values from -0.1875 to 0.1875
- output_weight: bfloat16 [2, 1024, 1024], P(None, 'view'), may hold values from -0.1875 to 0.1875
- fast_init: bfloat16 [2, 16, 3, 64, 512], P(None, 'head', None, None, 'view'), may hold values from -0.75 to 0.75
- update_mask: int32 [8, 2048], P('view'), may hold values 0 or 1
Outputs:
- refined: bfloat16 [16384, 1024], P(('view', 'head'))
All inputs are finite; a program needn't handle non-finite values. No bound on the sum of `update_mask` on one device may be relied on, other than what follows from the above.
Results may differ from a plain program's by a relative error of at most 0.035.
Values may be sent and summed in bfloat16 or wider, within the bound.
No kernel may reach another device: no remote copies, remote signals or barrier semaphores. Data moves between devices by JAX's collectives and lax.ppermute only.
A program may use at most 64 MiB of HBM per device.

v0:
```python
import functools
import math

import jax
import jax.numpy as jnp
from jax import lax
from jax.experimental import pallas as pl
from jax.experimental.pallas import tpu as pltpu
from jax.sharding import PartitionSpec as P


NS_STEPS = 5

newton_coeffs = (3.4445, -4.775, 2.0315)
learn_rate = 1.0
score_scale = 0.25
log2_e = math.log2(math.e)

F32, BF16 = jnp.float32, jnp.bfloat16
SMEM = pl.BlockSpec(memory_space=pltpu.SMEM)

FRONT_TILE, FRONT_WIDTH, FRONT_UNROLL, FRONT_TYPE = 256, 512, 4, F32
APPLY_TILE, APPLY_TYPE = 512, F32
VMEM_MIB = 32
ATTEND_TILE, ATTEND_WIDTH, ATTEND_UNROLL = 256, 1024, False


def mm(a, b, ca, cb, precision=None):
    return lax.dot_general(
        a, b, (((ca,), (cb,)), ((), ())), preferred_element_type=F32, precision=precision
    )


def whole(shape):
    return pl.BlockSpec(tuple(shape), lambda i: (0,) * len(shape))


def cost(flops, nbytes, trans=0):
    return pl.CostEstimate(flops=int(flops), bytes_accessed=int(nbytes), transcendentals=int(trans))


def sigmoid(x):
    return 0.5 * jnp.tanh(0.5 * x) + 0.5


def unit(part, axis):
    return part * lax.rsqrt(jnp.mean(part * part, axis=axis, keepdims=True) + 1e-05)


LIMIT = pltpu.CompilerParams(vmem_limit_bytes=VMEM_MIB * 2**20)
ANY = pl.BlockSpec(memory_space=pl.ANY)


def pack_kernel(wide, ids_ref, w_ref, f_ref, o_ref, *outs):
    blocks, _, d_slab, cols = w_ref.shape
    heads = f_ref.shape[1]
    f_slab = f_ref.shape[4]
    rows = o_ref.shape[1]
    for b in range(blocks):
        at = 3 * d_slab
        for j in range(3):
            outs[b][j * d_slab : (j + 1) * d_slab] = w_ref[b, j]
            parts = [f_ref[b, h, j].astype(F32).T for h in range(heads)]
            outs[b][at : at + f_slab] = jnp.concatenate(parts, axis=1).astype(BF16)
            at += f_slab
        for i in range(blocks if b == 1 else 0):
            for c in range(0, wide, cols):
                place = pl.multiple_of((ids_ref[1] & 1) * wide + c, cols)
                outs[b][at : at + rows] = o_ref[i, :, pl.ds(place, cols)]
                at += rows


def pack(ids, weight, fast, output):
    blocks, _, d_slab, cols = weight.shape
    f_slab = fast.shape[4]
    rows, wide = output.shape[1], output.shape[2] // 2
    shapes = [(3 * (d_slab + f_slab), cols) for _ in range(blocks)]
    shapes[1] = (shapes[1][0] + blocks * rows * (wide // cols), cols)
    return pl.pallas_call(
        functools.partial(pack_kernel, wide),
        grid=(1,),
        in_specs=[SMEM, whole(weight.shape), whole(fast.shape), whole(output.shape)],
        out_specs=[whole(s) for s in shapes],
        out_shape=[jax.ShapeDtypeStruct(s, BF16) for s in shapes],
        cost_estimate=cost(0, 2 * 2**20),
        compiler_params=LIMIT,
        name="pack",
    )(ids, weight, fast, output)


def prepare_kernel(count, d_slab, f_slab, heads, dim, outs, o_rows, o_parts, ids_ref, *refs):
    slabs, refs = refs[:count], refs[count:]
    w_ref, ft_ref = refs[:2]
    f_all = refs[-1]
    units = count * f_slab
    cols = heads * dim
    for k in range(count):
        source = ids_ref[0] ^ k
        for j in range(3):
            w_ref[pl.ds(pl.multiple_of(source * d_slab, d_slab), d_slab), j * cols : (j + 1) * cols] = slabs[k][
                j * d_slab : (j + 1) * d_slab
            ]
            f_all[j, pl.ds(pl.multiple_of(source * f_slab, f_slab), f_slab)] = slabs[k][
                3 * d_slab + j * f_slab : 3 * d_slab + (j + 1) * f_slab
            ]
        at = 3 * (d_slab + f_slab)
        for b in range(outs):
            for c in range(o_parts):
                place = b * count * o_rows + source * o_rows
                refs[2][pl.ds(pl.multiple_of(place, o_rows), o_rows), c * cols : (c + 1) * cols] = slabs[k][
                    at : at + o_rows
                ]
                at += o_rows
    blank = jnp.zeros((units, dim), BF16)
    for j in range(3):
        for h in range(heads):
            part = f_all[j, :, h * dim : (h + 1) * dim]
            ft_ref[h, j] = jnp.concatenate([blank, part] if j == 2 else [part, blank], axis=1)


def prepare(ids, slabs, d_slab, f_slab, heads, dim, outs=0, o_rows=0, o_parts=0):
    count = len(slabs)
    cols = heads * dim
    depth, units = count * d_slab, count * f_slab
    shapes = [(depth, 3 * cols), (heads, 3, units, 2 * dim)]
    if outs:
        shapes.append((outs * count * o_rows, o_parts * cols))
    return pl.pallas_call(
        functools.partial(prepare_kernel, count, d_slab, f_slab, heads, dim, outs, o_rows, o_parts),
        grid=(1,),
        in_specs=[SMEM] + [whole(s.shape) for s in slabs],
        out_specs=[whole(s) for s in shapes],
        out_shape=[jax.ShapeDtypeStruct(s, BF16) for s in shapes],
        scratch_shapes=[pltpu.VMEM((3, units, cols), BF16)],
        cost_estimate=cost(0, 8 * 2**20),
        compiler_params=LIMIT,
        name="prepare",
    )(ids, *slabs)


def front_kernel(heads, dim, chunks, steps, base, tokens, last, ids_ref, mask_ref, w_ref, ft_ref, *refs):
    x_refs, refs = refs[:chunks], refs[chunks:]
    if last:
        prev_ref, refs = refs[0], refs[4:]
        slots = refs[3 : 3 + heads]
        turn_ref = refs[-1]
    else:
        grad_ref = refs[3]
    q_ref, k_ref, v_ref = refs[:3]
    acc_ref, flip_ref, both_ref = refs[3 + heads : 6 + heads] if last else refs[4:7]
    step = pl.program_id(0)
    tile = q_ref.shape[0]
    cols = heads * dim
    units = ft_ref.shape[2]

    @pl.when(step == 0)
    def _():
        acc_ref[...] = jnp.zeros_like(acc_ref)

    x = x_refs[0][...]
    for c in range(1, chunks):
        x = jnp.where(step >= c * steps, x_refs[c][...], x)
    packed = mm(x, w_ref[...], 1, 0).astype(BF16)
    place = ((base + step // steps) ^ ids_ref[1]) * tokens + (step % steps) * tile
    mask = -(mask_ref[:, pl.ds(pl.multiple_of(place, tile), tile)].astype(F32))
    mask = jnp.broadcast_to(mask, (8, tile)).T[:, :1]
    side = lax.broadcasted_iota(jnp.int32, (cols, cols), 0) // dim
    same = side == lax.broadcasted_iota(jnp.int32, (cols, cols), 1) // dim
    spread = jnp.where(same, 1.0 / dim, 0.0).astype(BF16)

    def norm(part):
        part = part.astype(F32)
        return (part * lax.rsqrt(mm((part * part).astype(BF16), spread, 1, 0) + 1e-05)).astype(BF16)

    q_ref[...] = norm(packed[:, :cols])
    keys = norm(packed[:, cols : 2 * cols])
    values = packed[:, 2 * cols :]
    targets = (values.astype(F32) * mask).astype(BF16)
    ones = jnp.ones((tile, dim), BF16)
    for h in range(heads):
        rows = slice(h * dim, (h + 1) * dim)
        v_ref[h] = jnp.concatenate([values[:, rows], ones], axis=1)
        both = jnp.concatenate([keys[:, rows], targets[:, rows]], axis=1)
        flip_ref[h] = both
        both = both.T
        both_ref[h] = both
        k_ref[rows] = both[:dim]
    width = min(FRONT_WIDTH, units)

    def gradient(h, carry):
        both, flip = both_ref[h], flip_ref[h]
        for c in range(0, units, width):
            part = slice(c, c + width)
            first = mm(ft_ref[h, 0, part], both, 1, 0).astype(FRONT_TYPE)
            third = mm(ft_ref[h, 1, part], both, 1, 0).astype(FRONT_TYPE)
            back = mm(ft_ref[h, 2, part], both, 1, 0).astype(FRONT_TYPE)
            sigma = sigmoid(first)
            silu = first * sigma
            hidden = (silu * third).astype(BF16)
            d_third = (back * silu).astype(BF16)
            d_first = (back * third * (sigma + silu * (1.0 - sigma))).astype(BF16)
            acc_ref[h, 0, part] += mm(d_first, flip, 1, 0)
            acc_ref[h, 1, part] += mm(d_third, flip, 1, 0)
            acc_ref[h, 2, part] += mm(hidden, flip, 1, 0)
        return carry

    lax.fori_loop(0, heads, gradient, 0, unroll=FRONT_UNROLL)

    @pl.when(step == pl.num_programs(0) - 1)
    def _():
        def finish(h, carry):
            for j in range(3):
                rows = slice(j * dim, (j + 1) * dim)
                total = acc_ref[h, j].T[dim if j == 2 else 0 :][:dim]
                if last:
                    slot = h ^ lax.rem(ids_ref[0] >> 1, heads)
                    turn_ref[slot, rows] = (total + prev_ref[h, rows]).astype(BF16)
                else:
                    grad_ref[h, rows] = total
            return carry

        lax.fori_loop(0, heads, finish, 0)
        if last:
            for i in range(heads):
                slots[i][...] = turn_ref[i]


def front(ids, xs, base, wt, ft, mask, parts, before=None):
    tokens, depth = xs[0].shape
    heads, _, units, dim = ft.shape
    dim //= 2
    cols = heads * dim
    tile = min(FRONT_TILE, tokens)
    steps = tokens // tile
    chunks = len(xs)
    total = parts * tokens
    first = base * steps
    last = before is not None

    def pick(c):
        return lambda i: (jnp.clip(i - c * steps, 0, steps - 1), 0)

    in_specs = [SMEM, whole(mask.shape), whole(wt.shape), whole(ft.shape)]
    in_specs += [pl.BlockSpec((tile, depth), pick(c)) for c in range(chunks)]
    out_specs = [
        pl.BlockSpec((tile, cols), lambda i: (first + i, 0)),
        pl.BlockSpec((cols, tile), lambda i: (0, first + i)),
        pl.BlockSpec((heads, tile, 2 * dim), lambda i: (0, first + i, 0)),
    ]
    out_shape = [
        jax.ShapeDtypeStruct((total, cols), BF16),
        jax.ShapeDtypeStruct((cols, total), BF16),
        jax.ShapeDtypeStruct((heads, total, 2 * dim), BF16),
    ]
    args = [ids, mask, wt, ft, *xs]
    scratch = [
        pltpu.VMEM((heads, 3, units, 2 * dim), F32),
        pltpu.VMEM((heads, tile, 2 * dim), BF16),
        pltpu.VMEM((heads, 2 * dim, tile), BF16),
    ]
    aliases = {}
    if last:
        in_specs += [whole(before[3].shape)] + [ANY] * 3
        aliases = {len(args) + 1 + i: i for i in range(3)}
        args += [before[3], *before[:3]]
        out_specs += [whole((3 * dim, units))] * heads
        out_shape += [jax.ShapeDtypeStruct((3 * dim, units), BF16)] * heads
        scratch.append(pltpu.VMEM((heads, 3 * dim, units), BF16))
    else:
        out_specs.append(whole((heads, 3 * dim, units)))
        out_shape.append(jax.ShapeDtypeStruct((heads, 3 * dim, units), F32))
    here = chunks * tokens
    return pl.pallas_call(
        functools.partial(front_kernel, heads, dim, chunks, steps, base, tokens, last),
        grid=(chunks * steps,),
        in_specs=in_specs,
        out_specs=out_specs,
        out_shape=out_shape,
        scratch_shapes=scratch,
        input_output_aliases=aliases,
        cost_estimate=cost(4 * here * cols * 2 * (3 * depth + 6 * units), 6 * 2**20),
        compiler_params=LIMIT,
        name="front",
    )(*args)


def attend_kernel(heads, dim, q_ref, k_ref, v_ref, *refs):
    o_ref = refs[-1]
    span = k_ref.shape[1]
    width = min(ATTEND_WIDTH, span)

    def pair(p, carry):
        at = pl.ds(pl.multiple_of(p * 2 * dim, 2 * dim), 2 * dim)
        both = q_ref[:, at]
        keys = k_ref[at]
        outs = []
        for i in range(2):
            total = None
            for c in range(0, span, width):
                scores = mm(both[:, i * dim : (i + 1) * dim], keys[i * dim : (i + 1) * dim, c : c + width], 1, 0)
                probs = jnp.exp2(scores * (score_scale * log2_e)).astype(BF16)
                part = mm(probs, v_ref[2 * p + i, c : c + width], 1, 0)
                total = part if total is None else total + part
            outs.append(total[:, :dim] / total[:, dim:])
        o_ref[:, at] = jnp.concatenate(outs, axis=1).astype(BF16)
        return carry

    lax.fori_loop(0, heads // 2, pair, 0, unroll=ATTEND_UNROLL)


def attend(q, k, v, start, count, before=None):
    total, cols = q.shape
    heads, _, twice = v.shape
    tile = min(ATTEND_TILE, count)
    first = start // tile
    extra = [] if before is None else [before]
    return pl.pallas_call(
        functools.partial(attend_kernel, heads, twice // 2),
        grid=(count // tile,),
        in_specs=[pl.BlockSpec((tile, cols), lambda i: (first + i, 0)), whole(k.shape), whole(v.shape)]
        + [ANY] * len(extra),
        out_specs=pl.BlockSpec((tile, cols), lambda i: (first + i, 0)),
        out_shape=jax.ShapeDtypeStruct((total, cols), BF16),
        input_output_aliases={3: 0} if extra else {},
        cost_estimate=cost(4 * 4 * count * total * cols, 4 * 2**20),
        compiler_params=LIMIT,
        name="attend",
    )(q, k, v, *extra)


def split(x):
    high = x.astype(BF16)
    return high, (x - high.astype(F32)).astype(BF16)


def mm_split(a, b, ca, cb):
    return mm(a[0], b[0], ca, cb) + (mm(a[0], b[1], ca, cb) + mm(a[1], b[0], ca, cb))


def newton_kernel(ids_ref, ft_ref, own_ref, got_ref, o_ref):
    dim = ft_ref.shape[3] // 2
    summed = own_ref[...].astype(F32) + got_ref[...].astype(F32)
    scaled = []
    for j in range(3):
        total = summed[j * dim : (j + 1) * dim]
        scaled.append(total * lax.rsqrt(jnp.sum(total * total, keepdims=True) + 1e-06))
    current = jnp.concatenate(scaled, axis=0)
    side = lax.broadcasted_iota(jnp.int32, (3 * dim, 3 * dim), 0) // dim
    same = side == lax.broadcasted_iota(jnp.int32, (3 * dim, 3 * dim), 1) // dim

    halves = split(current)
    cross = mm(halves[0], halves[1], 1, 1)
    gram = jnp.where(same, mm(halves[0], halves[0], 1, 1) + (cross + cross.T), 0.0)
    eye = lax.broadcasted_iota(jnp.int32, gram.shape, 0) == lax.broadcasted_iota(jnp.int32, gram.shape, 1)
    identity = jnp.where(eye, 1.0, 0.0)

    def advance(_, state):
        gram, factor = state
        parts = split(gram)
        squared = mm_split(parts, parts, 1, 0)
        polynomial = newton_coeffs[0] * identity + newton_coeffs[1] * gram + newton_coeffs[2] * squared
        step = split(polynomial)
        factor = mm_split(step, split(factor), 1, 0)
        gram = mm_split(step, split(mm_split(parts, step, 1, 0)), 1, 0)
        return gram, factor

    _, factor = lax.fori_loop(0, NS_STEPS, advance, (gram, identity))
    current = mm_split(split(factor), halves, 1, 0)
    for j in range(3):
        rows = slice(j * dim, (j + 1) * dim)
        initial = ft_ref[0, j].astype(F32).T[dim if j == 2 else 0 :][:dim]
        o_ref[rows] = (initial - learn_rate * current[rows]).astype(BF16)


def newton(ids, ft, own, got):
    heads, _, units, twice = ft.shape
    fixed = lambda i, ids: (0, 0)
    return pl.pallas_call(
        newton_kernel,
        grid_spec=pltpu.PrefetchScalarGridSpec(
            num_scalar_prefetch=1,
            grid=(1,),
            in_specs=[
                pl.BlockSpec((1, 3, units, twice), lambda i, ids: (lax.rem(ids[0] >> 1, heads), 0, 0, 0)),
                pl.BlockSpec(own.shape, fixed),
                pl.BlockSpec(got.shape, fixed),
            ],
            out_specs=pl.BlockSpec(own.shape, fixed),
        ),
        out_shape=jax.ShapeDtypeStruct(own.shape, BF16),
        cost_estimate=cost(2**30, 2 * 2**20),
        compiler_params=LIMIT,
        name="newton",
    )(ids, ft, own, got)


def apply_kernel(heads, dim, group, stage, first_k, count, ids_ref, q_ref, a_ref, *refs):
    early_ref, refs = (refs[0], refs[1:]) if stage == "late" else (None, refs)
    units_refs, o_refs, fast_ref = refs[:count], refs[count:-1], refs[-1]
    step = pl.program_id(0)
    place = ids_ref[0] >> 1
    mine = lax.rem(place, heads) // group
    side = 1 - mine if stage == "late" else mine
    span = group * dim
    if stage == "all":
        at = slice(None)
    else:
        at = pl.ds(pl.multiple_of(side * span, span), span)

    @pl.when(step == 0)
    def _():
        for k in range(count):
            head = place ^ (first_k + k)
            if stage != "all":
                fast_ref[lax.rem(head, group)] = units_refs[k][...]
                continue

            @pl.when(head < heads)
            def _():
                fast_ref[head] = units_refs[k][...]

    queries = q_ref[:, at]
    outs = []
    for h in range(group):
        query = queries[:, h * dim : (h + 1) * dim]
        first = mm(query, fast_ref[h, :dim], 1, 0).astype(APPLY_TYPE)
        third = mm(query, fast_ref[h, dim : 2 * dim], 1, 0).astype(APPLY_TYPE)
        hidden = (first * sigmoid(first) * third).astype(BF16)
        outs.append(unit(mm(hidden, fast_ref[h, 2 * dim :], 1, 1), 1))
    mixed = (jnp.concatenate(outs, axis=1) + a_ref[:, at].astype(F32)).astype(BF16)
    if stage == "early":
        o_refs[0][...] = mixed
        return
    steps = o_refs[0].shape[0] // mixed.shape[0]
    for c, o_ref in enumerate(o_refs):

        @pl.when(step // steps == c)
        def _():
            rows = pl.ds(pl.multiple_of((step % steps) * mixed.shape[0], mixed.shape[0]), mixed.shape[0])
            if stage == "late":
                o_ref[rows, at] = mixed
                o_ref[rows, pl.ds(pl.multiple_of(mine * span, span), span)] = early_ref[...]
            else:
                o_ref[rows] = mixed


def apply_fast(ids, q, attended, fast, heads, stage, tokens, start, chunks, early=None):
    total, cols = q.shape
    dim = cols // heads
    units = fast[0].shape[1]
    group = heads if stage == "all" else heads // 2
    first_k = 0
    if stage != "all":
        first_k = 0 if stage == "early" else group
        fast = fast[first_k : first_k + group]
    tile = min(APPLY_TILE, tokens)
    first = start // tile
    rows = pl.BlockSpec((tile, cols), lambda i: (first + i, 0))
    args, in_specs = [ids, q, attended], [SMEM, rows, rows]
    if stage == "late":
        args.append(early)
        in_specs.append(pl.BlockSpec((tile, group * dim), lambda i: (first + i, 0)))
    if stage == "early":
        out_specs = pl.BlockSpec((tile, group * dim), lambda i: (first + i, 0))
        out_shape = jax.ShapeDtypeStruct((total, group * dim), BF16)
    else:
        out_specs = [whole((tokens, cols))] * chunks
        out_shape = [jax.ShapeDtypeStruct((tokens, cols), BF16)] * chunks
    here = chunks * tokens
    return pl.pallas_call(
        functools.partial(apply_kernel, heads, dim, group, stage, first_k, len(fast)),
        grid=(here // tile,),
        in_specs=in_specs + [whole(a.shape) for a in fast],
        out_specs=out_specs,
        out_shape=out_shape,
        scratch_shapes=[pltpu.VMEM((group, 3 * dim, units), BF16)],
        cost_estimate=cost(4 * 2 * here * group * dim * units * 3, 2 * 2**20),
        compiler_params=LIMIT,
    )(*args, *fast)


def project_kernel(count, more, ids_ref, s_ref, own_ref, pair_ref, *refs):
    parts, outs = refs[:count], refs[count:]
    cols = parts[0].shape[1]
    half = own_ref.shape[1]
    low = ids_ref[1] & 1
    for which, w_ref in ((low, own_ref), (1 - low, pair_ref)):
        projected = None
        for k in range(count):
            place = pl.multiple_of((ids_ref[1] ^ k) * cols, cols)
            part = mm(parts[k][...], w_ref[pl.ds(place, cols)], 1, 0)
            projected = part if projected is None else projected + part
        here = pl.ds(pl.multiple_of(which * half, half), half)
        outs[0][:, here] = (s_ref[:, here].astype(F32) + projected).astype(BF16)
    if more:
        outs[1][...] = unit(outs[0][...].astype(F32), 1).astype(BF16)


def project(ids, stream, own, pair, layer, parts, more):
    tokens, depth = stream.shape
    tile = min(256, tokens)
    cols = parts[0].shape[1]
    count = 2 if more else 1
    weight = pl.BlockSpec((depth, own.shape[1]), lambda i: (layer, 0))
    return pl.pallas_call(
        functools.partial(project_kernel, len(parts), more),
        grid=(tokens // tile,),
        in_specs=[SMEM, pl.BlockSpec((tile, depth), lambda i: (i, 0)), weight, weight]
        + [pl.BlockSpec((tile, cols), lambda i: (i, 0))] * len(parts),
        out_specs=[pl.BlockSpec((tile, depth), lambda i: (i, 0))] * count,
        out_shape=[jax.ShapeDtypeStruct((tokens, depth), BF16)] * count,
        cost_estimate=cost(2 * tokens * depth * depth, 6 * 2**20),
        compiler_params=LIMIT,
        name="project",
    )(ids, stream, own, pair, *parts)


def solution(mesh):
    views, parts = mesh.shape["view"], mesh.shape["head"]

    def swap(x, axis, k, keep=None):
        pairs = [(i, i ^ k) for i in range(mesh.shape[axis])]
        if keep is not None:
            pairs = [p for p in pairs if keep(*p)]
        return lax.ppermute(x, axis, pairs)

    def gather_view(block):
        slabs = {0: block}
        for k in range(2, views, 2):
            slabs[k] = swap(block, "view", k)
        for k in range(0, views, 2):
            slabs[k + 1] = swap(slabs[k], "view", 1)
        return [slabs[k] for k in range(views)]

    def shards(features, attend_weight, output_weight, fast_init, update_mask):
        blocks, _, d_slab, cols = attend_weight.shape
        heads, dim, f_slab = fast_init.shape[1], fast_init.shape[3], fast_init.shape[4]
        tokens = features.shape[0]
        half = parts // 2
        staged = views // 2 == heads and heads % 4 == 0
        ids = jnp.stack([lax.axis_index("view"), lax.axis_index("head")]).astype(jnp.int32)
        o_rows, o_parts = output_weight.shape[1], output_weight.shape[2] // 2 // cols
        payloads = pack(ids, attend_weight, fast_init, output_weight)

        stream = features
        normed = unit(features.astype(F32), 1).astype(BF16)
        for layer in range(blocks):
            xs = [normed]
            for k in range(1, parts):
                high = 1 << (k.bit_length() - 1)
                from_k, hop = (0, k) if high == k else (high, k ^ high)
                xs.append(swap(xs[from_k], "head", hop))
            if layer == 0:
                slabs = gather_view(payloads[0])
                wt, ft = prepare(ids, slabs, d_slab, f_slab, heads, dim)
                later = []
                for b, block in enumerate(payloads[1:], 1):
                    slabs = gather_view(block)
                    shape = (blocks, o_rows, o_parts) if b == 1 else ()
                    later.append(prepare(ids, slabs, d_slab, f_slab, heads, dim, *shape))
                out_own = later[0][2]
                out_pair = swap(out_own, "head", 1)
            else:
                wt, ft = later[layer - 1][:2]
            front_a = front(ids, xs[:half], 0, wt, ft, update_mask, parts)
            q, k, v, *grads = front(ids, xs[half:], half, wt, ft, update_mask, parts, front_a)
            near = grads[0].astype(F32)
            for i in range(1, views // 2):
                part = swap(grads[i % heads], "view", 2 * i, lambda _, o: (o >> 1) < heads)
                near = near + part.astype(F32)
            near = near.astype(BF16)
            got = swap(near, "view", 1)
            count = half * tokens
            attended = None
            least = count // 2
            for start, n in ((least, 2 * count - least), (0, least)):
                attended = attend(q, k, v, start, n, attended)
            fresh = newton(ids, ft, near, got)
            fast = [fresh] + [swap(fresh, "view", 2 * i, lambda i, o: (i >> 1) < heads) for i in range(1, views // 2)]
            stage, early = "all", None
            if staged:
                stage = "late"
                early = apply_fast(ids, q, attended, fast, heads, "early", tokens, 0, parts)
            mixed_b = apply_fast(ids, q, attended, fast, heads, stage, tokens, count, half, early)
            mixed_a = apply_fast(ids, q, attended, fast, heads, stage, tokens, 0, half, early)
            mixed = [*mixed_a, *mixed_b]
            received = [mixed[0]] + [swap(mixed[i], "head", i) for i in range(1, parts)]
            more = layer + 1 < blocks
            result = project(ids, stream, out_own, out_pair, layer, received, more)
            stream = result[0]
            normed = result[-1]
        return stream


    return jax.shard_map(
        shards,
        mesh=mesh,
        in_specs=(
            P(("view", "head"), None),
            P(None, None, "view", "head"),
            P(None, "view", None),
            P(None, "head", None, None, "view"),
            P("view", None),
        ),
        out_specs=P(("view", "head"), None),
        check_vma=False,
    )
```

profile of v0, /device:TPU:0, one launch (start us, length us, event | category | flops | bytes accessed | tf_op | source)
XLA Modules:
  0.0 346.4 jit_solution(17862874310400149962)
XLA Ops:
  0.1 1.1 copy-done.1
  1.2 1.0 copy-done.2
  2.2 1.0 copy-done.3
  4.0 3.1 collective-permute-start.9
  7.1 2.6 collective-permute-start.11
  9.7 1.7 collective-permute-start.8
  11.4 1.5 fusion
  13.3 6.4 %collective-permute-done.9.refs_2_ = bf16[576,256]{1,0:T(8,128)(2,1)S(1)} collective-permute-done((bf16[576,256]{1,0:T(8,128)(2,1)S(1)}, bf16[576,256]{1,0:T(8,128)(2,1)S(1)}, u32[]{:S(2)}, u32[]{:S(2)}) %collective-permute-start.9) | collective-permute-done | bytes 294944 | tf_op jit(solution)/shard_map/ppermute | solution.py:525
  19.7 1.7 collective-permute-start.15
  21.4 9.2 %collective-permute-done.11.refs_4_ = bf16[576,256]{1,0:T(8,128)(2,1)S(1)} collective-permute-done((bf16[576,256]{1,0:T(8,128)(2,1)S(1)}, bf16[576,256]{1,0:T(8,128)(2,1)S(1)}, u32[]{:S(2)}, u32[]{:S(2)}) %collective-permute-start.11) | collective-permute-done | bytes 294944 | tf_op jit(solution)/shard_map/ppermute | solution.py:525
  30.5 1.5 collective-permute-start.10
  32.6 1.5 collective-permute-start.14
  34.1 6.0 %collective-permute-done.10.refs_3_ = bf16[576,256]{1,0:T(8,128)(2,1)S(1)} collective-permute-done((bf16[576,256]{1,0:T(8,128)(2,1)S(1)}, bf16[576,256]{1,0:T(8,128)(2,1)S(1)}, u32[]{:S(2)}, u32[]{:S(2)}) %collective-permute-start.10) | collective-permute-done | bytes 294944 | tf_op jit(solution)/shard_map/ppermute | solution.py:525
  40.1 3.2 collective-permute-done.12.refs_5_
  43.2 3.7 %collective-permute-start.3 = (bf16[1088,256]{1,0:T(8,128)(2,1)S(1)}, bf16[1088,256]{1,0:T(8,128)(2,1)S(1)}, u32[]{:S(2)}, u32[]{:S(2)}) collective-permute-start(bf16[1088,256]{1,0:T(8,128)(2,1)S(1)} %get-tuple-element.44.refs_0_), channel_id=1, source_target_pairs={{0,16},{4,20},{8,24},{12,28},{16,0},{20,4},{24,8},{28,12},{1,17},{... | collective-permute-start | bytes 1671176 | tf_op jit(solution)/shard_map/ppermute | solution.py:525
  47.0 1.4 collective-permute-start.5
  48.3 1.1 prepare.3
  49.4 7.7 %collective-permute-done.1.refs_2_ = bf16[1088,256]{1,0:T(8,128)(2,1)S(1)} collective-permute-done((bf16[1088,256]{1,0:T(8,128)(2,1)S(1)}, bf16[1088,256]{1,0:T(8,128)(2,1)S(1)}, u32[]{:S(2)}, u32[]{:S(2)}) %collective-permute-start.1) | collective-permute-done | bytes 557088 | tf_op jit(solution)/shard_map/ppermute | solution.py:525
  57.1 1.5 collective-permute-start
  58.6 25.3 %collective-permute-done.3.refs_4_ = bf16[1088,256]{1,0:T(8,128)(2,1)S(1)} collective-permute-done((bf16[1088,256]{1,0:T(8,128)(2,1)S(1)}, bf16[1088,256]{1,0:T(8,128)(2,1)S(1)}, u32[]{:S(2)}, u32[]{:S(2)}) %collective-permute-start.3) | collective-permute-done | bytes 557088 | tf_op jit(solution)/shard_map/ppermute | solution.py:525
  83.9 1.5 collective-permute-start.2
  85.9 1.5 collective-permute-start.6
  87.4 13.4 %front.4 = (bf16[2048,256]{1,0:T(8,128)(2,1)S(1)}, bf16[256,2048]{1,0:T(8,128)(2,1)S(1)}, bf16[4,2048,128]{2,1,0:T(8,128)(2,1)S(1)}, f32[4,192,512]{2,1,0:T(8,128)S(1)}) custom-call(s32[2]{0:T(128)S(1)} %pad_add_fusion.ids_ref, s32[1,2048]{1,0:T(1,128)S(1)} %copy-done.4, bf16[1024,768]{1,0:T(8,128)(2,1)S(1)} %get-tuple-element.47.w_ref, ...), custom_call_target="tpu_custom_call" | custom-call | flops 12884901888 | bytes 6291456 | tf_op jit(solution)/shard_map/front/pallas_call | solution.py:273
  100.8 13.4 %front.5 = (bf16[2048,256]{1,0:T(8,128)(2,1)S(1)}, bf16[256,2048]{1,0:T(8,128)(2,1)S(1)}, bf16[4,2048,128]{2,1,0:T(8,128)(2,1)S(1)}, bf16[192,512]{1,0:T(8,128)(...) custom-call(s32[2]{0:T(128)S(1)} %pad_add_fusion.ids_ref, ...), custom_call_target="tpu_custom_call", output_to_operand_aliasing={{0}: (7, {}), {1}: (8, {}), {2}: (9, {})} | custom-call | flops 12884901888 | bytes 6291456 | tf_op jit(solution)/shard_map/front/pallas_call | solution.py:273
  114.2 6.5 %collective-permute-start.18 = (bf16[192,512]{1,0:T(8,128)(2,1)S(1)}, bf16[192,512]{1,0:T(8,128)(2,1)S(1)}, u32[]{:S(2)}, u32[]{:S(2)}) collective-permute-start(bf16[192,512]{1,0:T(8,128)(2,1)S(1)} %get-tuple-element.57), channel_id=1, source_target_pairs={{0,8},{4,12},{8,0},{12,4},{16,24},{20,28},{24,16},{28,20},{1,9},{5... | collective-permute-start | bytes 589832 | tf_op jit(solution)/shard_map/ppermute | solution.py:525
  120.8 2.4 collective-permute-start.20
  123.2 1.3 prepare.2
  124.6 4.5 %collective-permute-done.18 = bf16[192,512]{1,0:T(8,128)(2,1)S(1)} collective-permute-done((bf16[192,512]{1,0:T(8,128)(2,1)S(1)}, bf16[192,512]{1,0:T(8,128)(2,1)S(1)}, u32[]{:S(2)}, u32[]{:S(2)}) %collective-permute-start.18) | collective-permute-done | bytes 196640 | tf_op jit(solution)/shard_map/ppermute | solution.py:525
  129.1 8.8 %collective-permute-done.19 = bf16[192,512]{1,0:T(8,128)(2,1)S(1)} collective-permute-done((bf16[192,512]{1,0:T(8,128)(2,1)S(1)}, bf16[192,512]{1,0:T(8,128)(2,1)S(1)}, u32[]{:S(2)}, u32[]{:S(2)}) %collective-permute-start.19) | collective-permute-done | bytes 196640 | tf_op jit(solution)/shard_map/ppermute | solution.py:525
  138.0 1.6 collective-permute-start.21
  139.6 16.7 %attend.4.refs_0_ = bf16[2048,256]{1,0:T(8,128)(2,1)S(1)} custom-call(bf16[2048,256]{1,0:T(8,128)(2,1)S(1)} %get-tuple-element.53.q_ref, bf16[256,2048]{1,0:T(8,128)(2,1)S(1)} %get-tuple-element.54.k_ref, bf16[4,2048,128]{2,1,0:T(8,128)(2,1)S(1)} %get-tuple-element.55.v_ref), custom_call_target="tpu_custom_call" | custom-call | flops 12884901888 | bytes 4194304 | tf_op jit(solution)/shard_map/attend/pallas_call | solution.py:317
  156.3 5.6 %newton.2.refs_0_ = bf16[192,512]{1,0:T(8,128)(2,1)S(1)} custom-call(s32[2]{0:T(128)S(1)} %pad_add_fusion.ids_ref, bf16[4,3,512,128]{3,2,1,0:T(8,128)(2,1)S(1)} %get-tuple-element.48.ft_ref, bf16[192,512]{1,0:T(8,128)(2,1)S(1)} %add_convert_fusion.1.own_ref, bf16[192,512]{1,0:T(8,128)(2,1)S(1)} %collective-permute-done.21.got_ref), custom_call_target="tpu_custom_call" | custom-call | flops 1073741824 | bytes 2097152 | tf_op jit(solution)/shard_map/newton/pallas_call | solution.py:378
  161.9 3.9 %collective-permute-start.22 = (bf16[192,512]{1,0:T(8,128)(2,1)S(1)}, bf16[192,512]{1,0:T(8,128)(2,1)S(1)}, u32[]{:S(2)}, u32[]{:S(2)}) collective-permute-start(bf16[192,512]{1,0:T(8,128)(2,1)S(1)} %newton.2.refs_0_), channel_id=1, source_target_pairs={{0,8},{4,12},{8,0},{12,4},{16,24},{20,28},{24,16},{28,20},{1,9},{5... | collective-permute-start | bytes 589832 | tf_op jit(solution)/shard_map/ppermute | solution.py:525
  165.8 5.6 %attend.5.a_ref = bf16[2048,256]{1,0:T(8,128)(2,1)S(1)} custom-call(bf16[2048,256]{1,0:T(8,128)(2,1)S(1)} %get-tuple-element.53.q_ref, bf16[256,2048]{1,0:T(8,128)(2,1)S(1)} %get-tuple-element.54.k_ref, bf16[4,2048,128]{2,1,0:T(8,128)(2,1)S(1)} %get-tuple-element.55.v_ref, bf16[2048,256]{1,0:T(8,128)(2,1)S(1)} %attend.4.refs_0_), custom_call_target="tpu_custom_call", output_to_operand_aliasing={{}: (3, {})} | custom-call | flops 4294967296 | bytes 4194304 | tf_op jit(solution)/shard_map/attend/pallas_call | solution.py:317
  171.5 2.4 collective-permute-start.24
  173.9 6.7 %shard_map.55.refs_0_ = bf16[2048,128]{1,0:T(8,128)(2,1)S(1)} custom-call(s32[2]{0:T(128)S(1)} %pad_add_fusion.ids_ref, bf16[2048,256]{1,0:T(8,128)(2,1)S(1)} %get-tuple-element.53.q_ref, bf16[2048,256]{1,0:T(8,128)(2,1)S(1)} %attend.5.a_ref, bf16[192,512]{1,0:T(8,128)(2,1)S(1)} %newton.2.refs_0_, bf16[192,512]{1,0:T(8,128)(2,1)S(1)} %collective-permute-done.22.refs_1_), custom_call_target="tpu_custom_call" | custom-call | flops 3221225472 | bytes 2097152 | tf_op jit(solution)/shard_map/pallas_call | solution.py:470
  180.6 5.5 %collective-permute-done.23.refs_1_ = bf16[192,512]{1,0:T(8,128)(2,1)S(1)} collective-permute-done((bf16[192,512]{1,0:T(8,128)(2,1)S(1)}, bf16[192,512]{1,0:T(8,128)(2,1)S(1)}, u32[]{:S(2)}, u32[]{:S(2)}) %collective-permute-start.23) | collective-permute-done | bytes 196640 | tf_op jit(solution)/shard_map/ppermute | solution.py:525
  186.1 3.7 %shard_map.57 = (bf16[512,256]{1,0:T(8,128)(2,1)S(1)}, bf16[512,256]{1,0:T(8,128)(2,1)S(1)}) custom-call(s32[2]{0:T(128)S(1)} %pad_add_fusion.ids_ref, bf16[2048,256]{1,0:T(8,128)(2,1)S(1)} %get-tuple-element.53.q_ref, bf16[2048,256]{1,0:T(8,128)(2,1)S(1)} %attend.5.a_ref, bf16[2048,128]{1,0:T(8,128)(2,1)S(1)} %shard_map.55.refs_0_, ...), custom_call_target="tpu_custom_call" | custom-call | flops 1610612736 | bytes 2097152 | tf_op jit(solution)/shard_map/pallas_call | solution.py:470
  189.8 1.6 collective-permute-start.26
  191.4 3.7 %shard_map.56 = (bf16[512,256]{1,0:T(8,128)(2,1)S(1)}, bf16[512,256]{1,0:T(8,128)(2,1)S(1)}) custom-call(s32[2]{0:T(128)S(1)} %pad_add_fusion.ids_ref, bf16[2048,256]{1,0:T(8,128)(2,1)S(1)} %get-tuple-element.53.q_ref, bf16[2048,256]{1,0:T(8,128)(2,1)S(1)} %attend.5.a_ref, bf16[2048,128]{1,0:T(8,128)(2,1)S(1)} %shard_map.55.refs_0_, ...), custom_call_target="tpu_custom_call" | custom-call | flops 1610612736 | bytes 2097152 | tf_op jit(solution)/shard_map/pallas_call | solution.py:470
  195.8 3.2 collective-permute-done.26.refs_2_
  199.1 3.6 %collective-permute-done.27.refs_3_ = bf16[512,256]{1,0:T(8,128)(2,1)S(1)} collective-permute-done((bf16[512,256]{1,0:T(8,128)(2,1)S(1)}, bf16[512,256]{1,0:T(8,128)(2,1)S(1)}, u32[]{:S(2)}, u32[]{:S(2)}) %collective-permute-start.27) | collective-permute-done | bytes 262176 | tf_op jit(solution)/shard_map/ppermute | solution.py:525
  202.6 2.4 project.2
  205.0 1.5 collective-permute-start.28
  207.1 23.8 %collective-permute-done.28.refs_0_ = bf16[512,1024]{1,0:T(8,128)(2,1)S(1)} collective-permute-done((bf16[512,1024]{1,0:T(8,128)(2,1)S(1)}, bf16[512,1024]{1,0:T(8,128)(2,1)S(1)}, u32[]{:S(2)}, u32[]{:S(2)}) %collective-permute-start.28) | collective-permute-done | bytes 1048608 | tf_op jit(solution)/shard_map/ppermute | solution.py:525
  231.0 13.2 %front.6 = (bf16[2048,256]{1,0:T(8,128)(2,1)S(1)}, bf16[256,2048]{1,0:T(8,128)(2,1)S(1)}, bf16[4,2048,128]{2,1,0:T(8,128)(2,1)S(1)}, f32[4,192,512]{2,1,0:T(8,128)S(1)}) custom-call(s32[2]{0:T(128)S(1)} %pad_add_fusion.ids_ref, s32[1,2048]{1,0:T(1,128)S(1)} %copy-done.4, bf16[1024,768]{1,0:T(8,128)(2,1)S(1)} %get-tuple-element.65.w_ref, ...), custom_call_target="tpu_custom_call" | custom-call | flops 12884901888 | bytes 6291456 | tf_op jit(solution)/shard_map/front/pallas_call | solution.py:273
  244.2 13.3 %front.7 = (bf16[2048,256]{1,0:T(8,128)(2,1)S(1)}, bf16[256,2048]{1,0:T(8,128)(2,1)S(1)}, bf16[4,2048,128]{2,1,0:T(8,128)(2,1)S(1)}, bf16[192,512]{1,0:T(8,128)(...) custom-call(s32[2]{0:T(128)S(1)} %pad_add_fusion.ids_ref, ...), custom_call_target="tpu_custom_call", output_to_operand_aliasing={{0}: (7, {}), {1}: (8, {}), {2}: (9, {})} | custom-call | flops 12884901888 | bytes 6291456 | tf_op jit(solution)/shard_map/front/pallas_call | solution.py:273
  257.5 4.8 %collective-permute-start.31 = (bf16[192,512]{1,0:T(8,128)(2,1)S(1)}, bf16[192,512]{1,0:T(8,128)(2,1)S(1)}, u32[]{:S(2)}, u32[]{:S(2)}) collective-permute-start(bf16[192,512]{1,0:T(8,128)(2,1)S(1)} %get-tuple-element.76), channel_id=1, source_target_pairs={{0,8},{4,12},{8,0},{12,4},{16,24},{20,28},{24,16},{28,20},{1,9},{5... | collective-permute-start | bytes 589832 | tf_op jit(solution)/shard_map/ppermute | solution.py:525
  262.4 2.4 collective-permute-start.33
  264.8 6.2 %collective-permute-done.31 = bf16[192,512]{1,0:T(8,128)(2,1)S(1)} collective-permute-done((bf16[192,512]{1,0:T(8,128)(2,1)S(1)}, bf16[192,512]{1,0:T(8,128)(2,1)S(1)}, u32[]{:S(2)}, u32[]{:S(2)}) %collective-permute-start.31) | collective-permute-done | bytes 196640 | tf_op jit(solution)/shard_map/ppermute | solution.py:525
  271.0 8.5 %collective-permute-done.32 = bf16[192,512]{1,0:T(8,128)(2,1)S(1)} collective-permute-done((bf16[192,512]{1,0:T(8,128)(2,1)S(1)}, bf16[192,512]{1,0:T(8,128)(2,1)S(1)}, u32[]{:S(2)}, u32[]{:S(2)}) %collective-permute-start.32) | collective-permute-done | bytes 196640 | tf_op jit(solution)/shard_map/ppermute | solution.py:525
  280.2 16.6 %attend.6.refs_0_ = bf16[2048,256]{1,0:T(8,128)(2,1)S(1)} custom-call(bf16[2048,256]{1,0:T(8,128)(2,1)S(1)} %get-tuple-element.72.q_ref, bf16[256,2048]{1,0:T(8,128)(2,1)S(1)} %get-tuple-element.73.k_ref, bf16[4,2048,128]{2,1,0:T(8,128)(2,1)S(1)} %get-tuple-element.74.v_ref), custom_call_target="tpu_custom_call" | custom-call | flops 12884901888 | bytes 4194304 | tf_op jit(solution)/shard_map/attend/pallas_call | solution.py:317
  296.8 5.6 %newton.3.refs_0_ = bf16[192,512]{1,0:T(8,128)(2,1)S(1)} custom-call(s32[2]{0:T(128)S(1)} %pad_add_fusion.ids_ref, bf16[4,3,512,128]{3,2,1,0:T(8,128)(2,1)S(1)} %get-tuple-element.66.ft_ref, bf16[192,512]{1,0:T(8,128)(2,1)S(1)} %add_convert_fusion.own_ref, bf16[192,512]{1,0:T(8,128)(2,1)S(1)} %collective-permute-done.34.got_ref), custom_call_target="tpu_custom_call" | custom-call | flops 1073741824 | bytes 2097152 | tf_op jit(solution)/shard_map/newton/pallas_call | solution.py:378
  302.5 4.1 %collective-permute-start.35 = (bf16[192,512]{1,0:T(8,128)(2,1)S(1)}, bf16[192,512]{1,0:T(8,128)(2,1)S(1)}, u32[]{:S(2)}, u32[]{:S(2)}) collective-permute-start(bf16[192,512]{1,0:T(8,128)(2,1)S(1)} %newton.3.refs_0_), channel_id=1, source_target_pairs={{0,8},{4,12},{8,0},{12,4},{16,24},{20,28},{24,16},{28,20},{1,9},{5... | collective-permute-start | bytes 589832 | tf_op jit(solution)/shard_map/ppermute | solution.py:525
  306.6 5.5 %attend.7.a_ref = bf16[2048,256]{1,0:T(8,128)(2,1)S(1)} custom-call(bf16[2048,256]{1,0:T(8,128)(2,1)S(1)} %get-tuple-element.72.q_ref, bf16[256,2048]{1,0:T(8,128)(2,1)S(1)} %get-tuple-element.73.k_ref, bf16[4,2048,128]{2,1,0:T(8,128)(2,1)S(1)} %get-tuple-element.74.v_ref, bf16[2048,256]{1,0:T(8,128)(2,1)S(1)} %attend.6.refs_0_), custom_call_target="tpu_custom_call", output_to_operand_aliasing={{}: (3, {})} | custom-call | flops 4294967296 | bytes 4194304 | tf_op jit(solution)/shard_map/attend/pallas_call | solution.py:317
  312.2 2.4 collective-permute-start.37
  314.6 6.7 %shard_map.58.refs_0_ = bf16[2048,128]{1,0:T(8,128)(2,1)S(1)} custom-call(s32[2]{0:T(128)S(1)} %pad_add_fusion.ids_ref, bf16[2048,256]{1,0:T(8,128)(2,1)S(1)} %get-tuple-element.72.q_ref, bf16[2048,256]{1,0:T(8,128)(2,1)S(1)} %attend.7.a_ref, bf16[192,512]{1,0:T(8,128)(2,1)S(1)} %newton.3.refs_0_, bf16[192,512]{1,0:T(8,128)(2,1)S(1)} %collective-permute-done.35.refs_1_), custom_call_target="tpu_custom_call" | custom-call | flops 3221225472 | bytes 2097152 | tf_op jit(solution)/shard_map/pallas_call | solution.py:470
  321.3 5.7 %collective-permute-done.36.refs_1_ = bf16[192,512]{1,0:T(8,128)(2,1)S(1)} collective-permute-done((bf16[192,512]{1,0:T(8,128)(2,1)S(1)}, bf16[192,512]{1,0:T(8,128)(2,1)S(1)}, u32[]{:S(2)}, u32[]{:S(2)}) %collective-permute-start.36) | collective-permute-done | bytes 196640 | tf_op jit(solution)/shard_map/ppermute | solution.py:525
  327.0 3.7 %shard_map.60 = (bf16[512,256]{1,0:T(8,128)(2,1)S(1)}, bf16[512,256]{1,0:T(8,128)(2,1)S(1)}) custom-call(s32[2]{0:T(128)S(1)} %pad_add_fusion.ids_ref, bf16[2048,256]{1,0:T(8,128)(2,1)S(1)} %get-tuple-element.72.q_ref, bf16[2048,256]{1,0:T(8,128)(2,1)S(1)} %attend.7.a_ref, bf16[2048,128]{1,0:T(8,128)(2,1)S(1)} %shard_map.58.refs_0_, ...), custom_call_target="tpu_custom_call" | custom-call | flops 1610612736 | bytes 2097152 | tf_op jit(solution)/shard_map/pallas_call | solution.py:470
  330.8 1.6 collective-permute-start.39
  332.3 3.7 %shard_map.59 = (bf16[512,256]{1,0:T(8,128)(2,1)S(1)}, bf16[512,256]{1,0:T(8,128)(2,1)S(1)}) custom-call(s32[2]{0:T(128)S(1)} %pad_add_fusion.ids_ref, bf16[2048,256]{1,0:T(8,128)(2,1)S(1)} %get-tuple-element.72.q_ref, bf16[2048,256]{1,0:T(8,128)(2,1)S(1)} %attend.7.a_ref, bf16[2048,128]{1,0:T(8,128)(2,1)S(1)} %shard_map.58.refs_0_, ...), custom_call_target="tpu_custom_call" | custom-call | flops 1610612736 | bytes 2097152 | tf_op jit(solution)/shard_map/pallas_call | solution.py:470
  336.8 3.2 collective-permute-done.39.refs_2_
  340.0 3.6 %collective-permute-done.40.refs_3_ = bf16[512,256]{1,0:T(8,128)(2,1)S(1)} collective-permute-done((bf16[512,256]{1,0:T(8,128)(2,1)S(1)}, bf16[512,256]{1,0:T(8,128)(2,1)S(1)}, u32[]{:S(2)}, u32[]{:S(2)}) %collective-permute-start.40) | collective-permute-done | bytes 262176 | tf_op jit(solution)/shard_map/ppermute | solution.py:525
  343.6 2.8 project.3
  (55 shorter events, 5.4 us)
Async XLA Ops:
  0.0 12.9 %copy-start = (bf16[512,1024]{1,0:T(8,128)(2,1)S(1)}, bf16[512,1024]{1,0:T(8,128)(2,1)}, u32[]{:S(2)}) copy-start(bf16[512,1024]{1,0:T(8,128)(2,1)} %s_ref.1) | copy-start | bytes 3145732
  0.1 1.1 copy-start.1
  1.2 1.0 copy-start.2
  2.2 1.0 copy-start.3
  4.0 15.7 %collective-permute-start.9 = (bf16[576,256]{1,0:T(8,128)(2,1)S(1)}, bf16[576,256]{1,0:T(8,128)(2,1)S(1)}, u32[]{:S(2)}, u32[]{:S(2)}) collective-permute-start(bf16[576,256]{1,0:T(8,128)(2,1)S(1)} %get-tuple-element.46.refs_0_), channel_id=1, source_target_pairs={{0,8},{4,12},{8,0},{12,4},{16,24},{20,28},{24,16},{28,20},{1,9},{5... | collective-permute-start | bytes 884744 | tf_op jit(solution)/shard_map/ppermute | solution.py:525
  7.1 23.4 %collective-permute-start.11 = (bf16[576,256]{1,0:T(8,128)(2,1)S(1)}, bf16[576,256]{1,0:T(8,128)(2,1)S(1)}, u32[]{:S(2)}, u32[]{:S(2)}) collective-permute-start(bf16[576,256]{1,0:T(8,128)(2,1)S(1)} %get-tuple-element.46.refs_0_), channel_id=1, source_target_pairs={{0,16},{4,20},{8,24},{12,28},{16,0},{20,4},{24,8},{28,12},{1,17},{... | collective-permute-start | bytes 884744 | tf_op jit(solution)/shard_map/ppermute | solution.py:525
  9.7 22.3 %collective-permute-start.13 = (bf16[576,256]{1,0:T(8,128)(2,1)S(1)}, bf16[576,256]{1,0:T(8,128)(2,1)S(1)}, u32[]{:S(2)}, u32[]{:S(2)}) collective-permute-start(bf16[576,256]{1,0:T(8,128)(2,1)S(1)} %get-tuple-element.46.refs_0_), channel_id=1, source_target_pairs={{0,24},{4,28},{8,16},{12,20},{16,8},{20,12},{24,0},{28,4},{1,25},{... | collective-permute-start | bytes 884744 | tf_op jit(solution)/shard_map/ppermute | solution.py:525
  9.7 22.9 %collective-permute-start.8 = (bf16[576,256]{1,0:T(8,128)(2,1)S(1)}, bf16[576,256]{1,0:T(8,128)(2,1)S(1)}, u32[]{:S(2)}, u32[]{:S(2)}) collective-permute-start(bf16[576,256]{1,0:T(8,128)(2,1)S(1)} %get-tuple-element.46.refs_0_), channel_id=1, source_target_pairs={{0,4},{4,0},{8,12},{12,8},{16,20},{20,16},{24,28},{28,24},{1,5},{5... | collective-permute-start | bytes 884744 | tf_op jit(solution)/shard_map/ppermute | solution.py:525
  13.0 74.5 %copy-start.4 = (s32[1,2048]{1,0:T(1,128)S(1)}, s32[1,2048]{1,0:T(1,128)}, u32[]{:S(2)}) copy-start(s32[1,2048]{1,0:T(1,128)} %mask_ref.7) | copy-start | bytes 24580
  13.2 72.7 %collective-permute-start.17 = (bf16[512,1024]{1,0:T(8,128)(2,1)S(1)}, bf16[512,1024]{1,0:T(8,128)(2,1)S(1)}, u32[]{:S(2)}, u32[]{:S(2)}) collective-permute-start(bf16[512,1024]{1,0:T(8,128)(2,1)S(1)} %fusion.1.refs_0_), channel_id=1, source_target_pairs={{0,1},{1,0},{2,3},{3,2},{4,5},{5,4},{6,7},{7,6},{8,9},{9,8},{10,11... | collective-permute-start | bytes 3145736 | tf_op jit(solution)/shard_map/ppermute | solution.py:525
  19.7 67.7 %collective-permute-start.15 = (bf16[512,1024]{1,0:T(8,128)(2,1)S(1)}, bf16[512,1024]{1,0:T(8,128)(2,1)S(1)}, u32[]{:S(2)}, u32[]{:S(2)}) collective-permute-start(bf16[512,1024]{1,0:T(8,128)(2,1)S(1)} %fusion.1.refs_0_), channel_id=1, source_target_pairs={{0,2},{1,3},{2,0},{3,1},{4,6},{5,7},{6,4},{7,5},{8,10},{9,11},{10,... | collective-permute-start | bytes 3145736 | tf_op jit(solution)/shard_map/ppermute | solution.py:525
  30.5 9.5 %collective-permute-start.10 = (bf16[576,256]{1,0:T(8,128)(2,1)S(1)}, bf16[576,256]{1,0:T(8,128)(2,1)S(1)}, u32[]{:S(2)}, u32[]{:S(2)}) collective-permute-start(bf16[576,256]{1,0:T(8,128)(2,1)S(1)} %collective-permute-done.9.refs_2_), channel_id=1, source_target_pairs={{0,4},{4,0},{8,12},{12,8},{16,20},{20,16},{24,28},{28,24},{1,5},{5... | collective-permute-start | bytes 884744 | tf_op jit(solution)/shard_map/ppermute | solution.py:525
  32.0 11.2 %collective-permute-start.12 = (bf16[576,256]{1,0:T(8,128)(2,1)S(1)}, bf16[576,256]{1,0:T(8,128)(2,1)S(1)}, u32[]{:S(2)}, u32[]{:S(2)}) collective-permute-start(bf16[576,256]{1,0:T(8,128)(2,1)S(1)} %collective-permute-done.11.refs_4_), channel_id=1, source_target_pairs={{0,4},{4,0},{8,12},{12,8},{16,20},{20,16},{24,28},{28,24},{1,5},{5... | collective-permute-start | bytes 884744 | tf_op jit(solution)/shard_map/ppermute | solution.py:525
  32.6 14.4 %collective-permute-start.14 = (bf16[576,256]{1,0:T(8,128)(2,1)S(1)}, bf16[576,256]{1,0:T(8,128)(2,1)S(1)}, u32[]{:S(2)}, u32[]{:S(2)}) collective-permute-start(bf16[576,256]{1,0:T(8,128)(2,1)S(1)} %collective-permute-done.13.refs_6_), channel_id=1, source_target_pairs={{0,4},{4,0},{8,12},{12,8},{16,20},{20,16},{24,28},{28,24},{1,5},{5... | collective-permute-start | bytes 884744 | tf_op jit(solution)/shard_map/ppermute | solution.py:525
  40.1 17.0 %collective-permute-start.1 = (bf16[1088,256]{1,0:T(8,128)(2,1)S(1)}, bf16[1088,256]{1,0:T(8,128)(2,1)S(1)}, u32[]{:S(2)}, u32[]{:S(2)}) collective-permute-start(bf16[1088,256]{1,0:T(8,128)(2,1)S(1)} %get-tuple-element.44.refs_0_), channel_id=1, source_target_pairs={{0,8},{4,12},{8,0},{12,4},{16,24},{20,28},{24,16},{28,20},{1,9},{5... | collective-permute-start | bytes 1671176 | tf_op jit(solution)/shard_map/ppermute | solution.py:525
  43.2 40.6 %collective-permute-start.3 = (bf16[1088,256]{1,0:T(8,128)(2,1)S(1)}, bf16[1088,256]{1,0:T(8,128)(2,1)S(1)}, u32[]{:S(2)}, u32[]{:S(2)}) collective-permute-start(bf16[1088,256]{1,0:T(8,128)(2,1)S(1)} %get-tuple-element.44.refs_0_), channel_id=1, source_target_pairs={{0,16},{4,20},{8,24},{12,28},{16,0},{20,4},{24,8},{28,12},{1,17},{... | collective-permute-start | bytes 1671176 | tf_op jit(solution)/shard_map/ppermute | solution.py:525
  47.0 38.4 %collective-permute-start.5 = (bf16[1088,256]{1,0:T(8,128)(2,1)S(1)}, bf16[1088,256]{1,0:T(8,128)(2,1)S(1)}, u32[]{:S(2)}, u32[]{:S(2)}) collective-permute-start(bf16[1088,256]{1,0:T(8,128)(2,1)S(1)} %get-tuple-element.44.refs_0_), channel_id=1, source_target_pairs={{0,24},{4,28},{8,16},{12,20},{16,8},{20,12},{24,0},{28,4},{1,25},{... | collective-permute-start | bytes 1671176 | tf_op jit(solution)/shard_map/ppermute | solution.py:525
  57.1 63.7 %collective-permute-start = (bf16[1088,256]{1,0:T(8,128)(2,1)S(1)}, bf16[1088,256]{1,0:T(8,128)(2,1)S(1)}, u32[]{:S(2)}, u32[]{:S(2)}) collective-permute-start(bf16[1088,256]{1,0:T(8,128)(2,1)S(1)} %get-tuple-element.44.refs_0_), channel_id=1, source_target_pairs={{0,4},{4,0},{8,12},{12,8},{16,20},{20,16},{24,28},{28,24},{1,5},{5... | collective-permute-start | bytes 1671176 | tf_op jit(solution)/shard_map/ppermute | solution.py:525
  83.9 36.9 %collective-permute-start.2 = (bf16[1088,256]{1,0:T(8,128)(2,1)S(1)}, bf16[1088,256]{1,0:T(8,128)(2,1)S(1)}, u32[]{:S(2)}, u32[]{:S(2)}) collective-permute-start(bf16[1088,256]{1,0:T(8,128)(2,1)S(1)} %collective-permute-done.1.refs_2_), channel_id=1, source_target_pairs={{0,4},{4,0},{8,12},{12,8},{16,20},{20,16},{24,28},{28,24},{1,5},{5... | collective-permute-start | bytes 1671176 | tf_op jit(solution)/shard_map/ppermute | solution.py:525
  85.4 37.9 %collective-permute-start.4 = (bf16[1088,256]{1,0:T(8,128)(2,1)S(1)}, bf16[1088,256]{1,0:T(8,128)(2,1)S(1)}, u32[]{:S(2)}, u32[]{:S(2)}) collective-permute-start(bf16[1088,256]{1,0:T(8,128)(2,1)S(1)} %collective-permute-done.3.refs_4_), channel_id=1, source_target_pairs={{0,4},{4,0},{8,12},{12,8},{16,20},{20,16},{24,28},{28,24},{1,5},{5... | collective-permute-start | bytes 1671176 | tf_op jit(solution)/shard_map/ppermute | solution.py:525
  85.9 37.3 %collective-permute-start.6 = (bf16[1088,256]{1,0:T(8,128)(2,1)S(1)}, bf16[1088,256]{1,0:T(8,128)(2,1)S(1)}, u32[]{:S(2)}, u32[]{:S(2)}) collective-permute-start(bf16[1088,256]{1,0:T(8,128)(2,1)S(1)} %collective-permute-done.5.refs_6_), channel_id=1, source_target_pairs={{0,4},{4,0},{8,12},{12,8},{16,20},{20,16},{24,28},{28,24},{1,5},{5... | collective-permute-start | bytes 1671176 | tf_op jit(solution)/shard_map/ppermute | solution.py:525
  87.4 13.4 %collective-permute-start.16 = (bf16[512,1024]{1,0:T(8,128)(2,1)S(1)}, bf16[512,1024]{1,0:T(8,128)(2,1)S(1)}, u32[]{:S(2)}, u32[]{:S(2)}) collective-permute-start(bf16[512,1024]{1,0:T(8,128)(2,1)S(1)} %collective-permute-done.15.refs_0_), channel_id=1, source_target_pairs={{0,1},{1,0},{2,3},{3,2},{4,5},{5,4},{6,7},{7,6},{8,9},{9,8},{10,11... | collective-permute-start | bytes 3145736 | tf_op jit(solution)/shard_map/ppermute | solution.py:525
  114.2 14.9 %collective-permute-start.18 = (bf16[192,512]{1,0:T(8,128)(2,1)S(1)}, bf16[192,512]{1,0:T(8,128)(2,1)S(1)}, u32[]{:S(2)}, u32[]{:S(2)}) collective-permute-start(bf16[192,512]{1,0:T(8,128)(2,1)S(1)} %get-tuple-element.57), channel_id=1, source_target_pairs={{0,8},{4,12},{8,0},{12,4},{16,24},{20,28},{24,16},{28,20},{1,9},{5... | collective-permute-start | bytes 589832 | tf_op jit(solution)/shard_map/ppermute | solution.py:525
  120.8 17.1 %collective-permute-start.19 = (bf16[192,512]{1,0:T(8,128)(2,1)S(1)}, bf16[192,512]{1,0:T(8,128)(2,1)S(1)}, u32[]{:S(2)}, u32[]{:S(2)}) collective-permute-start(bf16[192,512]{1,0:T(8,128)(2,1)S(1)} %get-tuple-element.58), channel_id=1, source_target_pairs={{0,16},{4,20},{8,24},{12,28},{16,0},{20,4},{24,8},{28,12},{1,17},{... | collective-permute-start | bytes 589832 | tf_op jit(solution)/shard_map/ppermute | solution.py:525
  120.8 17.1 %collective-permute-start.20 = (bf16[192,512]{1,0:T(8,128)(2,1)S(1)}, bf16[192,512]{1,0:T(8,128)(2,1)S(1)}, u32[]{:S(2)}, u32[]{:S(2)}) collective-permute-start(bf16[192,512]{1,0:T(8,128)(2,1)S(1)} %get-tuple-element.59), channel_id=1, source_target_pairs={{0,24},{4,28},{8,16},{12,20},{16,8},{20,12},{24,0},{28,4},{1,25},{... | collective-permute-start | bytes 589832 | tf_op jit(solution)/shard_map/ppermute | solution.py:525
  124.5 78.1 %collective-permute-start.7 = (bf16[2048,512]{1,0:T(8,128)(2,1)S(1)}, bf16[2048,512]{1,0:T(8,128)(2,1)S(1)}, u32[]{:S(2)}, u32[]{:S(2)}) collective-permute-start(bf16[2048,512]{1,0:T(8,128)(2,1)S(1)} %get-tuple-element.45.own_ref), channel_id=1, source_target_pairs={{0,1},{1,0},{2,3},{3,2},{4,5},{5,4},{6,7},{7,6},{8,9},{9,8},{10,11... | collective-permute-start | bytes 6291464 | tf_op jit(solution)/shard_map/ppermute | solution.py:525
  138.0 18.3 %collective-permute-start.21 = (bf16[192,512]{1,0:T(8,128)(2,1)S(1)}, bf16[192,512]{1,0:T(8,128)(2,1)S(1)}, u32[]{:S(2)}, u32[]{:S(2)}) collective-permute-start(bf16[192,512]{1,0:T(8,128)(2,1)S(1)} %add_convert_fusion.1.own_ref), channel_id=1, source_target_pairs={{0,4},{4,0},{8,12},{12,8},{16,20},{20,16},{24,28},{28,24},{1,5},{5... | collective-permute-start | bytes 589832 | tf_op jit(solution)/shard_map/ppermute | solution.py:525
  161.9 11.9 %collective-permute-start.22 = (bf16[192,512]{1,0:T(8,128)(2,1)S(1)}, bf16[192,512]{1,0:T(8,128)(2,1)S(1)}, u32[]{:S(2)}, u32[]{:S(2)}) collective-permute-start(bf16[192,512]{1,0:T(8,128)(2,1)S(1)} %newton.2.refs_0_), channel_id=1, source_target_pairs={{0,8},{4,12},{8,0},{12,4},{16,24},{20,28},{24,16},{28,20},{1,9},{5... | collective-permute-start | bytes 589832 | tf_op jit(solution)/shard_map/ppermute | solution.py:525
  171.4 14.6 %collective-permute-start.23 = (bf16[192,512]{1,0:T(8,128)(2,1)S(1)}, bf16[192,512]{1,0:T(8,128)(2,1)S(1)}, u32[]{:S(2)}, u32[]{:S(2)}) collective-permute-start(bf16[192,512]{1,0:T(8,128)(2,1)S(1)} %newton.2.refs_0_), channel_id=1, source_target_pairs={{0,16},{4,20},{8,24},{12,28},{16,0},{20,4},{24,8},{28,12},{1,17},{... | collective-permute-start | bytes 589832 | tf_op jit(solution)/shard_map/ppermute | solution.py:525
  171.5 14.6 %collective-permute-start.24 = (bf16[192,512]{1,0:T(8,128)(2,1)S(1)}, bf16[192,512]{1,0:T(8,128)(2,1)S(1)}, u32[]{:S(2)}, u32[]{:S(2)}) collective-permute-start(bf16[192,512]{1,0:T(8,128)(2,1)S(1)} %newton.2.refs_0_), channel_id=1, source_target_pairs={{0,24},{4,28},{8,16},{12,20},{16,8},{20,12},{24,0},{28,4},{1,25},{... | collective-permute-start | bytes 589832 | tf_op jit(solution)/shard_map/ppermute | solution.py:525
  189.8 9.2 %collective-permute-start.26 = (bf16[512,256]{1,0:T(8,128)(2,1)S(1)}, bf16[512,256]{1,0:T(8,128)(2,1)S(1)}, u32[]{:S(2)}, u32[]{:S(2)}) collective-permute-start(bf16[512,256]{1,0:T(8,128)(2,1)S(1)} %get-tuple-element.62), channel_id=1, source_target_pairs={{0,2},{1,3},{2,0},{3,1},{4,6},{5,7},{6,4},{7,5},{8,10},{9,11},{10,... | collective-permute-start | bytes 786440 | tf_op jit(solution)/shard_map/ppermute | solution.py:525
  191.4 11.3 %collective-permute-start.27 = (bf16[512,256]{1,0:T(8,128)(2,1)S(1)}, bf16[512,256]{1,0:T(8,128)(2,1)S(1)}, u32[]{:S(2)}, u32[]{:S(2)}) collective-permute-start(bf16[512,256]{1,0:T(8,128)(2,1)S(1)} %get-tuple-element.63), channel_id=1, source_target_pairs={{0,3},{1,2},{2,1},{3,0},{4,7},{5,6},{6,5},{7,4},{8,11},{9,10},{10,... | collective-permute-start | bytes 786440 | tf_op jit(solution)/shard_map/ppermute | solution.py:525
  195.1 7.5 %collective-permute-start.25 = (bf16[512,256]{1,0:T(8,128)(2,1)S(1)}, bf16[512,256]{1,0:T(8,128)(2,1)S(1)}, u32[]{:S(2)}, u32[]{:S(2)}) collective-permute-start(bf16[512,256]{1,0:T(8,128)(2,1)S(1)} %get-tuple-element.61), channel_id=1, source_target_pairs={{0,1},{1,0},{2,3},{3,2},{4,5},{5,4},{6,7},{7,6},{8,9},{9,8},{10,11... | collective-permute-start | bytes 786440 | tf_op jit(solution)/shard_map/ppermute | solution.py:525
  205.0 25.9 %collective-permute-start.28 = (bf16[512,1024]{1,0:T(8,128)(2,1)S(1)}, bf16[512,1024]{1,0:T(8,128)(2,1)S(1)}, u32[]{:S(2)}, u32[]{:S(2)}) collective-permute-start(bf16[512,1024]{1,0:T(8,128)(2,1)S(1)} %get-tuple-element.67.refs_0_), channel_id=1, source_target_pairs={{0,2},{1,3},{2,0},{3,1},{4,6},{5,7},{6,4},{7,5},{8,10},{9,11},{10,... | collective-permute-start | bytes 3145736 | tf_op jit(solution)/shard_map/ppermute | solution.py:525
  206.5 24.4 %collective-permute-start.30 = (bf16[512,1024]{1,0:T(8,128)(2,1)S(1)}, bf16[512,1024]{1,0:T(8,128)(2,1)S(1)}, u32[]{:S(2)}, u32[]{:S(2)}) collective-permute-start(bf16[512,1024]{1,0:T(8,128)(2,1)S(1)} %get-tuple-element.67.refs_0_), channel_id=1, source_target_pairs={{0,1},{1,0},{2,3},{3,2},{4,5},{5,4},{6,7},{7,6},{8,9},{9,8},{10,11... | collective-permute-start | bytes 3145736 | tf_op jit(solution)/shard_map/ppermute | solution.py:525
  231.0 13.2 %collective-permute-start.29 = (bf16[512,1024]{1,0:T(8,128)(2,1)S(1)}, bf16[512,1024]{1,0:T(8,128)(2,1)S(1)}, u32[]{:S(2)}, u32[]{:S(2)}) collective-permute-start(bf16[512,1024]{1,0:T(8,128)(2,1)S(1)} %collective-permute-done.28.refs_0_), channel_id=1, source_target_pairs={{0,1},{1,0},{2,3},{3,2},{4,5},{5,4},{6,7},{7,6},{8,9},{9,8},{10,11... | collective-permute-start | bytes 3145736 | tf_op jit(solution)/shard_map/ppermute | solution.py:525
  257.5 13.5 %collective-permute-start.31 = (bf16[192,512]{1,0:T(8,128)(2,1)S(1)}, bf16[192,512]{1,0:T(8,128)(2,1)S(1)}, u32[]{:S(2)}, u32[]{:S(2)}) collective-permute-start(bf16[192,512]{1,0:T(8,128)(2,1)S(1)} %get-tuple-element.76), channel_id=1, source_target_pairs={{0,8},{4,12},{8,0},{12,4},{16,24},{20,28},{24,16},{28,20},{1,9},{5... | collective-permute-start | bytes 589832 | tf_op jit(solution)/shard_map/ppermute | solution.py:525
  262.4 17.1 %collective-permute-start.32 = (bf16[192,512]{1,0:T(8,128)(2,1)S(1)}, bf16[192,512]{1,0:T(8,128)(2,1)S(1)}, u32[]{:S(2)}, u32[]{:S(2)}) collective-permute-start(bf16[192,512]{1,0:T(8,128)(2,1)S(1)} %get-tuple-element.77), channel_id=1, source_target_pairs={{0,16},{4,20},{8,24},{12,28},{16,0},{20,4},{24,8},{28,12},{1,17},{... | collective-permute-start | bytes 589832 | tf_op jit(solution)/shard_map/ppermute | solution.py:525
  262.4 17.1 %collective-permute-start.33 = (bf16[192,512]{1,0:T(8,128)(2,1)S(1)}, bf16[192,512]{1,0:T(8,128)(2,1)S(1)}, u32[]{:S(2)}, u32[]{:S(2)}) collective-permute-start(bf16[192,512]{1,0:T(8,128)(2,1)S(1)} %get-tuple-element.78), channel_id=1, source_target_pairs={{0,24},{4,28},{8,16},{12,20},{16,8},{20,12},{24,0},{28,4},{1,25},{... | collective-permute-start | bytes 589832 | tf_op jit(solution)/shard_map/ppermute | solution.py:525
  279.6 17.2 %collective-permute-start.34 = (bf16[192,512]{1,0:T(8,128)(2,1)S(1)}, bf16[192,512]{1,0:T(8,128)(2,1)S(1)}, u32[]{:S(2)}, u32[]{:S(2)}) collective-permute-start(bf16[192,512]{1,0:T(8,128)(2,1)S(1)} %add_convert_fusion.own_ref), channel_id=1, source_target_pairs={{0,4},{4,0},{8,12},{12,8},{16,20},{20,16},{24,28},{28,24},{1,5},{5... | collective-permute-start | bytes 589832 | tf_op jit(solution)/shard_map/ppermute | solution.py:525
  302.5 12.1 %collective-permute-start.35 = (bf16[192,512]{1,0:T(8,128)(2,1)S(1)}, bf16[192,512]{1,0:T(8,128)(2,1)S(1)}, u32[]{:S(2)}, u32[]{:S(2)}) collective-permute-start(bf16[192,512]{1,0:T(8,128)(2,1)S(1)} %newton.3.refs_0_), channel_id=1, source_target_pairs={{0,8},{4,12},{8,0},{12,4},{16,24},{20,28},{24,16},{28,20},{1,9},{5... | collective-permute-start | bytes 589832 | tf_op jit(solution)/shard_map/ppermute | solution.py:525
  312.1 14.9 %collective-permute-start.36 = (bf16[192,512]{1,0:T(8,128)(2,1)S(1)}, bf16[192,512]{1,0:T(8,128)(2,1)S(1)}, u32[]{:S(2)}, u32[]{:S(2)}) collective-permute-start(bf16[192,512]{1,0:T(8,128)(2,1)S(1)} %newton.3.refs_0_), channel_id=1, source_target_pairs={{0,16},{4,20},{8,24},{12,28},{16,0},{20,4},{24,8},{28,12},{1,17},{... | collective-permute-start | bytes 589832 | tf_op jit(solution)/shard_map/ppermute | solution.py:525
  312.2 14.8 %collective-permute-start.37 = (bf16[192,512]{1,0:T(8,128)(2,1)S(1)}, bf16[192,512]{1,0:T(8,128)(2,1)S(1)}, u32[]{:S(2)}, u32[]{:S(2)}) collective-permute-start(bf16[192,512]{1,0:T(8,128)(2,1)S(1)} %newton.3.refs_0_), channel_id=1, source_target_pairs={{0,24},{4,28},{8,16},{12,20},{16,8},{20,12},{24,0},{28,4},{1,25},{... | collective-permute-start | bytes 589832 | tf_op jit(solution)/shard_map/ppermute | solution.py:525
  330.8 9.2 %collective-permute-start.39 = (bf16[512,256]{1,0:T(8,128)(2,1)S(1)}, bf16[512,256]{1,0:T(8,128)(2,1)S(1)}, u32[]{:S(2)}, u32[]{:S(2)}) collective-permute-start(bf16[512,256]{1,0:T(8,128)(2,1)S(1)} %get-tuple-element.81), channel_id=1, source_target_pairs={{0,2},{1,3},{2,0},{3,1},{4,6},{5,7},{6,4},{7,5},{8,10},{9,11},{10,... | collective-permute-start | bytes 786440 | tf_op jit(solution)/shard_map/ppermute | solution.py:525
  332.3 11.3 %collective-permute-start.40 = (bf16[512,256]{1,0:T(8,128)(2,1)S(1)}, bf16[512,256]{1,0:T(8,128)(2,1)S(1)}, u32[]{:S(2)}, u32[]{:S(2)}) collective-permute-start(bf16[512,256]{1,0:T(8,128)(2,1)S(1)} %get-tuple-element.82), channel_id=1, source_target_pairs={{0,3},{1,2},{2,1},{3,0},{4,7},{5,6},{6,5},{7,4},{8,11},{9,10},{10,... | collective-permute-start | bytes 786440 | tf_op jit(solution)/shard_map/ppermute | solution.py:525
  336.1 7.5 %collective-permute-start.38 = (bf16[512,256]{1,0:T(8,128)(2,1)S(1)}, bf16[512,256]{1,0:T(8,128)(2,1)S(1)}, u32[]{:S(2)}, u32[]{:S(2)}) collective-permute-start(bf16[512,256]{1,0:T(8,128)(2,1)S(1)} %get-tuple-element.80), channel_id=1, source_target_pairs={{0,1},{1,0},{2,3},{3,2},{4,5},{5,4},{6,7},{7,6},{8,9},{9,8},{10,11... | collective-permute-start | bytes 786440 | tf_op jit(solution)/shard_map/ppermute | solution.py:525
where the time goes:
time: 349 us; the launch traced here: 346 us
  Pallas kernels  146 us (42%)
  waiting for transfers between devices  134 us (38%)
  starting transfers between devices  60.8 us (17%)
    ppermute x41, waiting for transfers between devices, swap(): return lax.ppermute(x, axis, pairs)  134 us
    ppermute x41, starting transfers between devices, swap(): return lax.ppermute(x, axis, pairs)  60.8 us
    pallas_call x4, Pallas kernels, front(): pl.pallas_call(functools.partial(front_kernel, heads, dim, chunks, steps,...  53.3 us
    pallas_call x4, Pallas kernels, attend(): pl.pallas_call(functools.partial(attend_kernel, heads, twice // 2), grid=...  44.5 us
    pallas_call x6, Pallas kernels, apply_fast(): pl.pallas_call(functools.partial(apply_kernel, heads, dim, group, stage,...  28.4 us
    pallas_call x2, Pallas kernels, newton(): pl.pallas_call(newton_kernel, grid_spec=pltpu.PrefetchScalarGridSpec(num_...  11.3 us
  transfers between devices with their start and end apart: 41, of which 17 were waited for; matrix products, arithmetic and copies ran while one was open for 1% of the time, Pallas kernels for 34%

commit v1 on v0

--- a/solution.py
+++ b/solution.py
@@ -20,7 +20,7 @@
 SMEM = pl.BlockSpec(memory_space=pltpu.SMEM)
 
 FRONT_TILE, FRONT_WIDTH, FRONT_UNROLL, FRONT_TYPE = 256, 512, 4, F32
-APPLY_TILE, APPLY_TYPE = 512, F32
+APPLY_TILE, APPLY_TYPE = 256, F32
 VMEM_MIB = 32
 ATTEND_TILE, ATTEND_WIDTH, ATTEND_UNROLL = 256, 1024, False
 
@@ -51,41 +51,46 @@
 ANY = pl.BlockSpec(memory_space=pl.ANY)
 
 
-def pack_kernel(wide, ids_ref, w_ref, f_ref, o_ref, *outs):
-    blocks, _, d_slab, cols = w_ref.shape
-    heads = f_ref.shape[1]
-    f_slab = f_ref.shape[4]
+def pack_kernel(outs, wide, *refs):
+    w_ref, f_ref, p_ref = refs[-3 - (outs > 0)], refs[-2 - (outs > 0)], refs[-1]
+    _, _, d_slab, cols = w_ref.shape
+    heads, f_slab = f_ref.shape[1], f_ref.shape[4]
+    at = 3 * d_slab
+    for j in range(3):
+        p_ref[j * d_slab : (j + 1) * d_slab] = w_ref[0, j]
+        parts = [f_ref[0, h, j].astype(F32).T for h in range(heads)]
+        p_ref[at : at + f_slab] = jnp.concatenate(parts, axis=1).astype(BF16)
+        at += f_slab
+    if not outs:
+        return
+    ids_ref, o_ref = refs[0], refs[3]
     rows = o_ref.shape[1]
-    for b in range(blocks):
-        at = 3 * d_slab
-        for j in range(3):
-            outs[b][j * d_slab : (j + 1) * d_slab] = w_ref[b, j]
-            parts = [f_ref[b, h, j].astype(F32).T for h in range(heads)]
-            outs[b][at : at + f_slab] = jnp.concatenate(parts, axis=1).astype(BF16)
-            at += f_slab
-        for i in range(blocks if b == 1 else 0):
-            for c in range(0, wide, cols):
-                place = pl.multiple_of((ids_ref[1] & 1) * wide + c, cols)
-                outs[b][at : at + rows] = o_ref[i, :, pl.ds(place, cols)]
-                at += rows
-
-
-def pack(ids, weight, fast, output):
-    blocks, _, d_slab, cols = weight.shape
-    f_slab = fast.shape[4]
-    rows, wide = output.shape[1], output.shape[2] // 2
-    shapes = [(3 * (d_slab + f_slab), cols) for _ in range(blocks)]
-    shapes[1] = (shapes[1][0] + blocks * rows * (wide // cols), cols)
+    for i in range(outs):
+        for c in range(0, wide, cols):
+            place = pl.multiple_of((ids_ref[1] & 1) * wide + c, cols)
+            p_ref[at : at + rows] = o_ref[i, :, pl.ds(place, cols)]
+            at += rows
+
+
+def pack(block, weight, fast, ids=None, output=None):
+    _, _, d_slab, cols = weight.shape
+    rows, outs, wide = 3 * (d_slab + fast.shape[4]), 0, 0
+    args = [weight, fast]
+    in_specs = [pl.BlockSpec((1, *a.shape[1:]), lambda i, n=a.ndim: (block,) + (0,) * (n - 1)) for a in args]
+    if output is not None:
+        outs, wide = output.shape[0], output.shape[2] // 2
+        rows += outs * output.shape[1] * (wide // cols)
+        args = [ids, *args, output]
+        in_specs = [SMEM, *in_specs, whole(output.shape)]
     return pl.pallas_call(
-        functools.partial(pack_kernel, wide),
+        functools.partial(pack_kernel, outs, wide),
         grid=(1,),
-        in_specs=[SMEM, whole(weight.shape), whole(fast.shape), whole(output.shape)],
-        out_specs=[whole(s) for s in shapes],
-        out_shape=[jax.ShapeDtypeStruct(s, BF16) for s in shapes],
+        in_specs=in_specs,
+        out_specs=whole((rows, cols)),
+        out_shape=jax.ShapeDtypeStruct((rows, cols), BF16),
         cost_estimate=cost(0, 2 * 2**20),
-        compiler_params=LIMIT,
         name="pack",
-    )(ids, weight, fast, output)
+    )(*args)
 
 
 def prepare_kernel(count, d_slab, f_slab, heads, dim, outs, o_rows, o_parts, ids_ref, *refs):
@@ -138,10 +143,11 @@
     )(ids, *slabs)
 
 
-def front_kernel(heads, dim, chunks, steps, base, tokens, last, ids_ref, mask_ref, w_ref, ft_ref, *refs):
+def front_kernel(heads, dim, chunks, steps, base, offset, tokens, more, last, ids_ref, mask_ref, w_ref, ft_ref, *refs):
     x_refs, refs = refs[:chunks], refs[chunks:]
+    if more:
+        prev_ref, refs = refs[0], refs[4:]
     if last:
-        prev_ref, refs = refs[0], refs[4:]
         slots = refs[3 : 3 + heads]
         turn_ref = refs[-1]
     else:
@@ -161,7 +167,7 @@
     for c in range(1, chunks):
         x = jnp.where(step >= c * steps, x_refs[c][...], x)
     packed = mm(x, w_ref[...], 1, 0).astype(BF16)
-    place = ((base + step // steps) ^ ids_ref[1]) * tokens + (step % steps) * tile
+    place = ((base + step // steps) ^ ids_ref[1]) * tokens + offset + (step % steps) * tile
     mask = -(mask_ref[:, pl.ds(pl.multiple_of(place, tile), tile)].astype(F32))
     mask = jnp.broadcast_to(mask, (8, tile)).T[:, :1]
     side = lax.broadcasted_iota(jnp.int32, (cols, cols), 0) // dim
@@ -212,9 +218,11 @@
             for j in range(3):
                 rows = slice(j * dim, (j + 1) * dim)
                 total = acc_ref[h, j].T[dim if j == 2 else 0 :][:dim]
+                if more:
+                    total += prev_ref[h, rows]
                 if last:
                     slot = h ^ lax.rem(ids_ref[0] >> 1, heads)
-                    turn_ref[slot, rows] = (total + prev_ref[h, rows]).astype(BF16)
+                    turn_ref[slot, rows] = total.astype(BF16)
                 else:
                     grad_ref[h, rows] = total
             return carry
@@ -225,17 +233,19 @@
                 slots[i][...] = turn_ref[i]
 
 
-def front(ids, xs, base, wt, ft, mask, parts, before=None):
-    tokens, depth = xs[0].shape
+def front(ids, xs, base, offset, tokens, wt, ft, mask, parts, before=None, last=False):
+    rows, depth = xs[0].shape
     heads, _, units, dim = ft.shape
     dim //= 2
     cols = heads * dim
-    tile = min(FRONT_TILE, tokens)
-    steps = tokens // tile
+    tile = min(FRONT_TILE, rows)
+    steps = rows // tile
     chunks = len(xs)
     total = parts * tokens
-    first = base * steps
-    last = before is not None
+    more = before is not None
+
+    def block(i):
+        return (base + i // steps) * (tokens // tile) + offset // tile + i % steps
 
     def pick(c):
         return lambda i: (jnp.clip(i - c * steps, 0, steps - 1), 0)
@@ -243,9 +253,9 @@
     in_specs = [SMEM, whole(mask.shape), whole(wt.shape), whole(ft.shape)]
     in_specs += [pl.BlockSpec((tile, depth), pick(c)) for c in range(chunks)]
     out_specs = [
-        pl.BlockSpec((tile, cols), lambda i: (first + i, 0)),
-        pl.BlockSpec((cols, tile), lambda i: (0, first + i)),
-        pl.BlockSpec((heads, tile, 2 * dim), lambda i: (0, first + i, 0)),
+        pl.BlockSpec((tile, cols), lambda i: (block(i), 0)),
+        pl.BlockSpec((cols, tile), lambda i: (0, block(i))),
+        pl.BlockSpec((heads, tile, 2 * dim), lambda i: (0, block(i), 0)),
     ]
     out_shape = [
         jax.ShapeDtypeStruct((total, cols), BF16),
@@ -259,19 +269,20 @@
         pltpu.VMEM((heads, 2 * dim, tile), BF16),
     ]
     aliases = {}
-    if last:
+    if more:
         in_specs += [whole(before[3].shape)] + [ANY] * 3
         aliases = {len(args) + 1 + i: i for i in range(3)}
         args += [before[3], *before[:3]]
+    if last:
         out_specs += [whole((3 * dim, units))] * heads
         out_shape += [jax.ShapeDtypeStruct((3 * dim, units), BF16)] * heads
         scratch.append(pltpu.VMEM((heads, 3 * dim, units), BF16))
     else:
         out_specs.append(whole((heads, 3 * dim, units)))
         out_shape.append(jax.ShapeDtypeStruct((heads, 3 * dim, units), F32))
-    here = chunks * tokens
+    here = chunks * rows
     return pl.pallas_call(
-        functools.partial(front_kernel, heads, dim, chunks, steps, base, tokens, last),
+        functools.partial(front_kernel, heads, dim, chunks, steps, base, offset, tokens, more, last),
         grid=(chunks * steps,),
         in_specs=in_specs,
         out_specs=out_specs,
@@ -354,17 +365,20 @@
     eye = lax.broadcasted_iota(jnp.int32, gram.shape, 0) == lax.broadcasted_iota(jnp.int32, gram.shape, 1)
     identity = jnp.where(eye, 1.0, 0.0)
 
+    def polynomial(gram, parts):
+        squared = mm_split(parts, parts, 1, 0)
+        return newton_coeffs[0] * identity + newton_coeffs[1] * gram + newton_coeffs[2] * squared
+
     def advance(_, state):
         gram, factor = state
         parts = split(gram)
-        squared = mm_split(parts, parts, 1, 0)
-        polynomial = newton_coeffs[0] * identity + newton_coeffs[1] * gram + newton_coeffs[2] * squared
-        step = split(polynomial)
+        step = split(polynomial(gram, parts))
         factor = mm_split(step, split(factor), 1, 0)
         gram = mm_split(step, split(mm_split(parts, step, 1, 0)), 1, 0)
         return gram, factor
 
-    _, factor = lax.fori_loop(0, NS_STEPS, advance, (gram, identity))
+    gram, factor = lax.fori_loop(0, NS_STEPS - 1, advance, (gram, identity))
+    factor = mm_split(split(polynomial(gram, split(gram))), split(factor), 1, 0)
     current = mm_split(split(factor), halves, 1, 0)
     for j in range(3):
         rows = slice(j * dim, (j + 1) * dim)
@@ -394,8 +408,8 @@
     )(ids, ft, own, got)
 
 
-def apply_kernel(heads, dim, group, stage, first_k, count, ids_ref, q_ref, a_ref, *refs):
-    early_ref, refs = (refs[0], refs[1:]) if stage == "late" else (None, refs)
+def apply_kernel(heads, dim, group, stage, first_k, count, merge, tokens, spans, ids_ref, q_ref, a_ref, *refs):
+    early_ref, refs = (refs[0], refs[1:]) if merge else (None, refs)
     units_refs, o_refs, fast_ref = refs[:count], refs[count:-1], refs[-1]
     step = pl.program_id(0)
     place = ids_ref[0] >> 1
@@ -428,87 +442,96 @@
         hidden = (first * sigmoid(first) * third).astype(BF16)
         outs.append(unit(mm(hidden, fast_ref[h, 2 * dim :], 1, 1), 1))
     mixed = (jnp.concatenate(outs, axis=1) + a_ref[:, at].astype(F32)).astype(BF16)
-    if stage == "early":
-        o_refs[0][...] = mixed
-        return
-    steps = o_refs[0].shape[0] // mixed.shape[0]
-    for c, o_ref in enumerate(o_refs):
-
-        @pl.when(step // steps == c)
+    tile = mixed.shape[0]
+    steps = tokens // tile
+    for (chunk, chunks), o_ref in zip(spans, o_refs):
+
+        @pl.when((step >= chunk * steps) & (step < (chunk + chunks) * steps))
         def _():
-            rows = pl.ds(pl.multiple_of((step % steps) * mixed.shape[0], mixed.shape[0]), mixed.shape[0])
-            if stage == "late":
+            rows = pl.ds(pl.multiple_of((step - chunk * steps) * tile, tile), tile)
+            if early_ref is None:
+                o_ref[rows] = mixed
+            else:
                 o_ref[rows, at] = mixed
                 o_ref[rows, pl.ds(pl.multiple_of(mine * span, span), span)] = early_ref[...]
-            else:
-                o_ref[rows] = mixed
-
-
-def apply_fast(ids, q, attended, fast, heads, stage, tokens, start, chunks, early=None):
-    total, cols = q.shape
+
+
+def apply_fast(ids, q, attended, fast, heads, stage, tokens, base, spans, early=None):
+    cols = q.shape[1]
     dim = cols // heads
     units = fast[0].shape[1]
-    group = heads if stage == "all" else heads // 2
-    first_k = 0
+    group, first_k = heads, 0
     if stage != "all":
+        group = heads // 2
         first_k = 0 if stage == "early" else group
         fast = fast[first_k : first_k + group]
     tile = min(APPLY_TILE, tokens)
-    first = start // tile
+    first = base * tokens // tile
     rows = pl.BlockSpec((tile, cols), lambda i: (first + i, 0))
     args, in_specs = [ids, q, attended], [SMEM, rows, rows]
-    if stage == "late":
+    merge = early is not None
+    if merge:
         args.append(early)
         in_specs.append(pl.BlockSpec((tile, group * dim), lambda i: (first + i, 0)))
-    if stage == "early":
-        out_specs = pl.BlockSpec((tile, group * dim), lambda i: (first + i, 0))
-        out_shape = jax.ShapeDtypeStruct((total, group * dim), BF16)
-    else:
-        out_specs = [whole((tokens, cols))] * chunks
-        out_shape = [jax.ShapeDtypeStruct((tokens, cols), BF16)] * chunks
-    here = chunks * tokens
+    width = cols if merge or stage == "all" else group * dim
+    shapes = [(chunks * tokens, width) for _, chunks in spans]
+    here = sum(chunks for _, chunks in spans) * tokens
     return pl.pallas_call(
-        functools.partial(apply_kernel, heads, dim, group, stage, first_k, len(fast)),
+        functools.partial(
+            apply_kernel, heads, dim, group, stage, first_k, len(fast), merge, tokens, tuple(spans)
+        ),
         grid=(here // tile,),
         in_specs=in_specs + [whole(a.shape) for a in fast],
-        out_specs=out_specs,
-        out_shape=out_shape,
+        out_specs=[whole(shape) for shape in shapes],
+        out_shape=[jax.ShapeDtypeStruct(shape, BF16) for shape in shapes],
         scratch_shapes=[pltpu.VMEM((group, 3 * dim, units), BF16)],
         cost_estimate=cost(4 * 2 * here * group * dim * units * 3, 2 * 2**20),
         compiler_params=LIMIT,
     )(*args, *fast)
 
 
-def project_kernel(count, more, ids_ref, s_ref, own_ref, pair_ref, *refs):
+def project_kernel(heads, dim, places, more, ids_ref, s_ref, own_ref, pair_ref, *refs):
+    count = len(places)
     parts, outs = refs[:count], refs[count:]
-    cols = parts[0].shape[1]
+    cols = heads * dim
+    group = max(heads // 2, 1)
+    mine = lax.rem(ids_ref[0] >> 1, heads) // group
     half = own_ref.shape[1]
     low = ids_ref[1] & 1
     for which, w_ref in ((low, own_ref), (1 - low, pair_ref)):
         projected = None
-        for k in range(count):
-            place = pl.multiple_of((ids_ref[1] ^ k) * cols, cols)
-            part = mm(parts[k][...], w_ref[pl.ds(place, cols)], 1, 0)
+        for (k, late), part_ref in zip(places, parts):
+            place, wide = (ids_ref[1] ^ k) * cols, part_ref.shape[1]
+            if late is not None:
+                place += (1 - mine if late else mine) * wide
+            part = mm(part_ref[...], w_ref[pl.ds(pl.multiple_of(place, wide), wide)], 1, 0)
             projected = part if projected is None else projected + part
         here = pl.ds(pl.multiple_of(which * half, half), half)
         outs[0][:, here] = (s_ref[:, here].astype(F32) + projected).astype(BF16)
-    if more:
-        outs[1][...] = unit(outs[0][...].astype(F32), 1).astype(BF16)
-
-
-def project(ids, stream, own, pair, layer, parts, more):
+    if not more:
+        return
+    normed = unit(outs[0][...].astype(F32), 1).astype(BF16)
+    outs[1][...] = normed
+    for c in range(2):
+
+        @pl.when(pl.program_id(0) == c)
+        def _():
+            outs[2 + c][...] = normed
+
+
+def project(ids, stream, own, pair, layer, parts, places, heads, dim, more):
     tokens, depth = stream.shape
-    tile = min(256, tokens)
-    cols = parts[0].shape[1]
-    count = 2 if more else 1
+    tile = tokens // 2
     weight = pl.BlockSpec((depth, own.shape[1]), lambda i: (layer, 0))
+    rows = pl.BlockSpec((tile, depth), lambda i: (i, 0))
+    out_specs = [rows] + ([rows] + [whole((tile, depth))] * 2 if more else [])
+    sizes = [tokens] + ([tokens, tile, tile] if more else [])
     return pl.pallas_call(
-        functools.partial(project_kernel, len(parts), more),
-        grid=(tokens // tile,),
-        in_specs=[SMEM, pl.BlockSpec((tile, depth), lambda i: (i, 0)), weight, weight]
-        + [pl.BlockSpec((tile, cols), lambda i: (i, 0))] * len(parts),
-        out_specs=[pl.BlockSpec((tile, depth), lambda i: (i, 0))] * count,
-        out_shape=[jax.ShapeDtypeStruct((tokens, depth), BF16)] * count,
+        functools.partial(project_kernel, heads, dim, tuple(places), more),
+        grid=(2,),
+        in_specs=[SMEM, rows, weight, weight] + [pl.BlockSpec((tile, p.shape[1]), lambda i: (i, 0)) for p in parts],
+        out_specs=out_specs,
+        out_shape=[jax.ShapeDtypeStruct((n, depth), BF16) for n in sizes],
         cost_estimate=cost(2 * tokens * depth * depth, 6 * 2**20),
         compiler_params=LIMIT,
         name="project",
@@ -540,16 +563,23 @@
         staged = views // 2 == heads and heads % 4 == 0
         ids = jnp.stack([lax.axis_index("view"), lax.axis_index("head")]).astype(jnp.int32)
         o_rows, o_parts = output_weight.shape[1], output_weight.shape[2] // 2 // cols
-        payloads = pack(ids, attend_weight, fast_init, output_weight)
+        payloads = []
+        for b in range(blocks):
+            payloads.append(pack(b, attend_weight, fast_init, *((ids, output_weight) if b == 1 else ())))
 
         stream = features
         normed = unit(features.astype(F32), 1).astype(BF16)
         for layer in range(blocks):
-            xs = [normed]
-            for k in range(1, parts):
+            pieces = halves if layer else [normed]
+            near_xs, far_xs = [normed], [[p] for p in pieces]
+            for k in range(1, half):
                 high = 1 << (k.bit_length() - 1)
                 from_k, hop = (0, k) if high == k else (high, k ^ high)
-                xs.append(swap(xs[from_k], "head", hop))
+                near_xs.append(swap(near_xs[from_k], "head", hop))
+            for far in far_xs:
+                far[0] = swap(far[0], "head", half)
+                for k in range(1, half):
+                    far.append(swap(far[0], "head", k))
             if layer == 0:
                 slabs = gather_view(payloads[0])
                 wt, ft = prepare(ids, slabs, d_slab, f_slab, heads, dim)
@@ -562,8 +592,12 @@
                 out_pair = swap(out_own, "head", 1)
             else:
                 wt, ft = later[layer - 1][:2]
-            front_a = front(ids, xs[:half], 0, wt, ft, update_mask, parts)
-            q, k, v, *grads = front(ids, xs[half:], half, wt, ft, update_mask, parts, front_a)
+            state = front(ids, near_xs, 0, 0, tokens, wt, ft, update_mask, parts)
+            for p, far in enumerate(far_xs):
+                offset = p * far[0].shape[0]
+                final = p + 1 == len(far_xs)
+                state = front(ids, far, half, offset, tokens, wt, ft, update_mask, parts, state, final)
+            q, k, v, *grads = state
             near = grads[0].astype(F32)
             for i in range(1, views // 2):
                 part = swap(grads[i % heads], "view", 2 * i, lambda _, o: (o >> 1) < heads)
@@ -577,18 +611,33 @@
                 attended = attend(q, k, v, start, n, attended)
             fresh = newton(ids, ft, near, got)
             fast = [fresh] + [swap(fresh, "view", 2 * i, lambda i, o: (i >> 1) < heads) for i in range(1, views // 2)]
-            stage, early = "all", None
+            received, places = [], []
+            far_chunks = [(c, 1) for c in range(half)]
             if staged:
-                stage = "late"
-                early = apply_fast(ids, q, attended, fast, heads, "early", tokens, 0, parts)
-            mixed_b = apply_fast(ids, q, attended, fast, heads, stage, tokens, count, half, early)
-            mixed_a = apply_fast(ids, q, attended, fast, heads, stage, tokens, 0, half, early)
-            mixed = [*mixed_a, *mixed_b]
-            received = [mixed[0]] + [swap(mixed[i], "head", i) for i in range(1, parts)]
+                spans = [(0, half)] + [(c, 1) for c in range(half, parts)]
+                early, *sent = apply_fast(ids, q, attended, fast, heads, "early", tokens, 0, spans)
+                for i, x in enumerate(sent, half):
+                    received.append(swap(x, "head", i))
+                    places.append((i, 0))
+                sent = apply_fast(ids, q, attended, fast, heads, "late", tokens, half, far_chunks)
+                for i, x in enumerate(sent, half):
+                    received.append(swap(x, "head", i))
+                    places.append((i, 1))
+                mixed = apply_fast(ids, q, attended, fast, heads, "late", tokens, 0, far_chunks, early)
+            else:
+                sent = apply_fast(ids, q, attended, fast, heads, "all", tokens, half, far_chunks)
+                for i, x in enumerate(sent, half):
+                    received.append(swap(x, "head", i))
+                    places.append((i, None))
+                mixed = apply_fast(ids, q, attended, fast, heads, "all", tokens, 0, far_chunks)
+            near_parts = [x if i == 0 else swap(x, "head", i) for i, x in enumerate(mixed)]
+            received = near_parts + received
+            places = [(i, None) for i in range(half)] + places
             more = layer + 1 < blocks
-            result = project(ids, stream, out_own, out_pair, layer, received, more)
+            result = project(ids, stream, out_own, out_pair, layer, received, places, heads, dim, more)
             stream = result[0]
-            normed = result[-1]
+            if more:
+                normed, *halves = result[1:]
         return stream
 
 

time: 349 us -> 362 us (1.037)
  Pallas kernels: 146 us -> 158 us
    pallas_call x3 -> x4, Pallas kernels: 6 us -> 10.7 us  [the longest x2 6.34 us: project(): pl.pallas_call(functools.partial(project_kernel, heads, dim, tuple(places...]
    pallas_call x6, Pallas kernels: 28.4 us -> 32.8 us  [apply_fast(): pl.pallas_call(functools.partial(apply_kernel, heads, dim, group, stage,...]
    pallas_call x4 -> x5, Pallas kernels: 53.3 us -> 56.9 us  [front(): pl.pallas_call(functools.partial(front_kernel, heads, dim, chunks, steps,...]
    ppermute x41 -> x47, starting transfers between devices: 60.8 us -> 63.6 us  [swap(): return lax.ppermute(x, axis, pairs)]
    ppermute x41 -> x47, waiting for transfers between devices: 134 us -> 133 us  [swap(): return lax.ppermute(x, axis, pairs)]
  transfers between devices with their start and end apart: 41 -> 47, of which waited for: 17 -> 21; matrix products, arithmetic and copies ran while one was open for 1% -> 1% of each run, Pallas kernels for 34% -> 37%
where the time goes in v1:
time: 362 us; the launch traced here: 360 us
  Pallas kernels  158 us (44%)
  waiting for transfers between devices  133 us (37%)
  starting transfers between devices  63.6 us (18%)
    ppermute x47, waiting for transfers between devices, swap(): return lax.ppermute(x, axis, pairs)  133 us
    ppermute x47, starting transfers between devices, swap(): return lax.ppermute(x, axis, pairs)  63.6 us
    pallas_call x5, Pallas kernels, front(): pl.pallas_call(functools.partial(front_kernel, heads, dim, chunks, steps,...  56.9 us
    pallas_call x4, Pallas kernels, attend(): pl.pallas_call(functools.partial(attend_kernel, heads, twice // 2), grid=...  44.5 us
    pallas_call x6, Pallas kernels, apply_fast(): pl.pallas_call(functools.partial(apply_kernel, heads, dim, group, stage,...  32.8 us
    pallas_call x2, Pallas kernels, newton(): pl.pallas_call(newton_kernel, grid_spec=pltpu.PrefetchScalarGridSpec(num_...  10.6 us
  transfers between devices with their start and end apart: 47, of which 21 were waited for; matrix products, arithmetic and copies ran while one was open for 1% of the time, Pallas kernels for 37%

profile of v1, /device:TPU:0, one launch (start us, length us, event | category | flops | bytes accessed | tf_op | source)
XLA Modules:
  0.0 359.8 jit_solution(10533775246372557488)
XLA Ops:
  0.0 2.0 pack.3.refs_0_
  2.0 3.1 collective-permute-start.9
  5.1 2.6 collective-permute-start.11
  7.7 1.7 collective-permute-start.8
  9.4 1.5 fusion
  11.3 6.6 %collective-permute-done.9.refs_2_ = bf16[576,256]{1,0:T(8,128)(2,1)S(1)} collective-permute-done((bf16[576,256]{1,0:T(8,128)(2,1)}, bf16[576,256]{1,0:T(8,128)(2,1)S(1)}, u32[]{:S(2)}, u32[]{:S(2)}) %collective-permute-start.9) | collective-permute-done | bytes 294944 | tf_op jit(solution)/shard_map/ppermute | solution.py:548
  17.9 1.7 collective-permute-start.15
  19.6 9.1 %collective-permute-done.11.refs_4_ = bf16[576,256]{1,0:T(8,128)(2,1)S(1)} collective-permute-done((bf16[576,256]{1,0:T(8,128)(2,1)}, bf16[576,256]{1,0:T(8,128)(2,1)S(1)}, u32[]{:S(2)}, u32[]{:S(2)}) %collective-permute-start.11) | collective-permute-done | bytes 294944 | tf_op jit(solution)/shard_map/ppermute | solution.py:548
  28.7 1.5 collective-permute-start.10
  33.6 2.3 pack.2.refs_0_
  35.9 2.5 collective-permute-done.10.refs_3_
  38.4 1.6 collective-permute-start.1
  39.9 1.6 collective-permute-done.12.refs_5_
  41.5 3.7 %collective-permute-start.3 = (bf16[1088,256]{1,0:T(8,128)(2,1)}, bf16[1088,256]{1,0:T(8,128)(2,1)S(1)}, u32[]{:S(2)}, u32[]{:S(2)}) collective-permute-start(bf16[1088,256]{1,0:T(8,128)(2,1)} %pack.2.refs_0_), channel_id=1, source_target_pairs={{0,16},{4,20},{8,24},{12,28},{16,0},{20,4},{24,8},{28,12},{1,17},{... | collective-permute-start | bytes 1671176 | tf_op jit(solution)/shard_map/ppermute | solution.py:548
  48.2 1.7 prepare.3
  49.9 10.6 %collective-permute-done.1.refs_2_ = bf16[1088,256]{1,0:T(8,128)(2,1)S(1)} collective-permute-done((bf16[1088,256]{1,0:T(8,128)(2,1)}, bf16[1088,256]{1,0:T(8,128)(2,1)S(1)}, u32[]{:S(2)}, u32[]{:S(2)}) %collective-permute-start.1) | collective-permute-done | bytes 557088 | tf_op jit(solution)/shard_map/ppermute | solution.py:548
  62.0 20.8 %collective-permute-done.3.refs_4_ = bf16[1088,256]{1,0:T(8,128)(2,1)S(1)} collective-permute-done((bf16[1088,256]{1,0:T(8,128)(2,1)}, bf16[1088,256]{1,0:T(8,128)(2,1)S(1)}, u32[]{:S(2)}, u32[]{:S(2)}) %collective-permute-start.3) | collective-permute-done | bytes 557088 | tf_op jit(solution)/shard_map/ppermute | solution.py:548
  84.8 1.5 collective-permute-start.6
  86.4 14.2 %front.5 = (bf16[2048,256]{1,0:T(8,128)(2,1)S(1)}, bf16[256,2048]{1,0:T(8,128)(2,1)S(1)}, bf16[4,2048,128]{2,1,0:T(8,128)(2,1)S(1)}, f32[4,192,512]{2,1,0:T(8,128)S(1)}) custom-call(s32[2]{0:T(128)S(1)} %copy-done.6, s32[1,2048]{1,0:T(1,128)S(1)} %copy-done.7, bf16[1024,768]{1,0:T(8,128)(2,1)S(1)} %get-tuple-element.55.w_ref, ...), custom_call_target="tpu_custom_call" | custom-call | flops 12884901888 | bytes 6291456 | tf_op jit(solution)/shard_map/front/pallas_call | solution.py:284
  100.6 14.1 %front.6 = (bf16[2048,256]{1,0:T(8,128)(2,1)S(1)}, bf16[256,2048]{1,0:T(8,128)(2,1)S(1)}, bf16[4,2048,128]{2,1,0:T(8,128)(2,1)S(1)}, bf16[192,512]{1,0:T(8,128)(...) custom-call(s32[2]{0:T(128)S(1)} %copy-done.6, ...), custom_call_target="tpu_custom_call", output_to_operand_aliasing={{0}: (7, {}), {1}: (8, {}), {2}: (9, {})} | custom-call | flops 12884901888 | bytes 6291456 | tf_op jit(solution)/shard_map/front/pallas_call | solution.py:284
  114.7 6.3 %collective-permute-start.18 = (bf16[192,512]{1,0:T(8,128)(2,1)S(1)}, bf16[192,512]{1,0:T(8,128)(2,1)S(1)}, u32[]{:S(2)}, u32[]{:S(2)}) collective-permute-start(bf16[192,512]{1,0:T(8,128)(2,1)S(1)} %get-tuple-element.65), channel_id=1, source_target_pairs={{0,8},{4,12},{8,0},{12,4},{16,24},{20,28},{24,16},{28,20},{1,9},{5... | collective-permute-start | bytes 589832 | tf_op jit(solution)/shard_map/ppermute | solution.py:548
  121.5 1.9 collective-permute-start.20
  124.8 4.9 %collective-permute-done.18 = bf16[192,512]{1,0:T(8,128)(2,1)S(1)} collective-permute-done((bf16[192,512]{1,0:T(8,128)(2,1)S(1)}, bf16[192,512]{1,0:T(8,128)(2,1)S(1)}, u32[]{:S(2)}, u32[]{:S(2)}) %collective-permute-start.18) | collective-permute-done | bytes 196640 | tf_op jit(solution)/shard_map/ppermute | solution.py:548
  129.7 8.4 %collective-permute-done.19 = bf16[192,512]{1,0:T(8,128)(2,1)S(1)} collective-permute-done((bf16[192,512]{1,0:T(8,128)(2,1)S(1)}, bf16[192,512]{1,0:T(8,128)(2,1)S(1)}, u32[]{:S(2)}, u32[]{:S(2)}) %collective-permute-start.19) | collective-permute-done | bytes 196640 | tf_op jit(solution)/shard_map/ppermute | solution.py:548
  138.2 1.6 collective-permute-start.21
  139.8 16.7 %attend.4.refs_0_ = bf16[2048,256]{1,0:T(8,128)(2,1)S(1)} custom-call(bf16[2048,256]{1,0:T(8,128)(2,1)S(1)} %get-tuple-element.61.q_ref, bf16[256,2048]{1,0:T(8,128)(2,1)S(1)} %get-tuple-element.62.k_ref, bf16[4,2048,128]{2,1,0:T(8,128)(2,1)S(1)} %get-tuple-element.63.v_ref), custom_call_target="tpu_custom_call" | custom-call | flops 12884901888 | bytes 4194304 | tf_op jit(solution)/shard_map/attend/pallas_call | solution.py:328
  156.5 5.3 %newton.2.refs_0_ = bf16[192,512]{1,0:T(8,128)(2,1)S(1)} custom-call(s32[2]{0:T(128)S(1)} %copy-done.6, bf16[4,3,512,128]{3,2,1,0:T(8,128)(2,1)S(1)} %get-tuple-element.56.ft_ref, bf16[192,512]{1,0:T(8,128)(2,1)S(1)} %add_convert_fusion.1.own_ref, bf16[192,512]{1,0:T(8,128)(2,1)S(1)} %collective-permute-done.21.got_ref), custom_call_target="tpu_custom_call" | custom-call | flops 1073741824 | bytes 2097152 | tf_op jit(solution)/shard_map/newton/pallas_call | solution.py:392
  161.7 4.3 %collective-permute-start.23 = (bf16[192,512]{1,0:T(8,128)(2,1)S(1)}, bf16[192,512]{1,0:T(8,128)(2,1)S(1)}, u32[]{:S(2)}, u32[]{:S(2)}) collective-permute-start(bf16[192,512]{1,0:T(8,128)(2,1)S(1)} %newton.2.refs_0_), channel_id=1, source_target_pairs={{0,16},{4,20},{8,24},{12,28},{16,0},{20,4},{24,8},{28,12},{1,17},{... | collective-permute-start | bytes 589832 | tf_op jit(solution)/shard_map/ppermute | solution.py:548
  166.0 1.9 collective-permute-start.24
  168.0 5.6 %attend.5.a_ref = bf16[2048,256]{1,0:T(8,128)(2,1)S(1)} custom-call(bf16[2048,256]{1,0:T(8,128)(2,1)S(1)} %get-tuple-element.61.q_ref, bf16[256,2048]{1,0:T(8,128)(2,1)S(1)} %get-tuple-element.62.k_ref, bf16[4,2048,128]{2,1,0:T(8,128)(2,1)S(1)} %get-tuple-element.63.v_ref, bf16[2048,256]{1,0:T(8,128)(2,1)S(1)} %attend.4.refs_0_), custom_call_target="tpu_custom_call", output_to_operand_aliasing={{}: (3, {})} | custom-call | flops 4294967296 | bytes 4194304 | tf_op jit(solution)/shard_map/attend/pallas_call | solution.py:328
  173.5 6.6 %collective-permute-done.23.refs_1_.refs_0_ = bf16[192,512]{1,0:T(8,128)(2,1)S(1)} collective-permute-done((bf16[192,512]{1,0:T(8,128)(2,1)S(1)}, bf16[192,512]{1,0:T(8,128)(2,1)S(1)}, u32[]{:S(2)}, u32[]{:S(2)}) %collective-permute-start.23) | collective-permute-done | bytes 196640 | tf_op jit(solution)/shard_map/ppermute | solution.py:548
  180.2 4.2 %shard_map.57 = (bf16[512,128]{1,0:T(8,128)(2,1)S(1)}, bf16[512,128]{1,0:T(8,128)(2,1)S(1)}) custom-call(s32[2]{0:T(128)S(1)} %copy-done.6, bf16[2048,256]{1,0:T(8,128)(2,1)S(1)} %get-tuple-element.61.q_ref, bf16[2048,256]{1,0:T(8,128)(2,1)S(1)} %attend.5.a_ref, bf16[192,512]{1,0:T(8,128)(2,1)S(1)} %collective-permute-done.23.refs_1_.refs_0_, ...), custom_call_target="tpu_custom_call" | custom-call | flops 1610612736 | bytes 2097152 | tf_op jit(solution)/shard_map/pallas_call | solution.py:479
  184.4 1.6 collective-permute-start.28
  186.0 7.9 %shard_map.55 = (bf16[1024,128]{1,0:T(8,128)(2,1)S(1)}, bf16[512,128]{1,0:T(8,128)(2,1)S(1)}, bf16[512,128]{1,0:T(8,128)(2,1)S(1)}) custom-call(s32[2]{0:T(128)S(1)} %copy-done.6, bf16[2048,256]{1,0:T(8,128)(2,1)S(1)} %get-tuple-element.61.q_ref, bf16[2048,256]{1,0:T(8,128)(2,1)S(1)} %attend.5.a_ref, bf16[192,512]{1,0:T(8,128)(2,1)S(1)} %newton.2.refs_0_, ...), custom_call_target="tpu_custom_call" | custom-call | flops 3221225472 | bytes 2097152 | tf_op jit(solution)/shard_map/pallas_call | solution.py:479
  193.9 4.3 %shard_map.56 = (bf16[512,256]{1,0:T(8,128)(2,1)S(1)}, bf16[512,256]{1,0:T(8,128)(2,1)S(1)}) custom-call(s32[2]{0:T(128)S(1)} %copy-done.6, bf16[2048,256]{1,0:T(8,128)(2,1)S(1)} %get-tuple-element.61.q_ref, bf16[2048,256]{1,0:T(8,128)(2,1)S(1)} %attend.5.a_ref, bf16[1024,128]{1,0:T(8,128)(2,1)S(1)} %get-tuple-element.68.refs_0_, ...), custom_call_target="tpu_custom_call" | custom-call | flops 1610612736 | bytes 2097152 | tf_op jit(solution)/shard_map/pallas_call | solution.py:479
  198.9 1.6 collective-permute-start.26
  200.5 3.1 collective-permute-done.29.refs_5_
  203.6 4.0 %collective-permute-done.26.refs_2_ = bf16[512,128]{1,0:T(8,128)(2,1)S(1)} collective-permute-done((bf16[512,128]{1,0:T(8,128)(2,1)S(1)}, bf16[512,128]{1,0:T(8,128)(2,1)S(1)}, u32[]{:S(2)}, u32[]{:S(2)}) %collective-permute-start.26) | collective-permute-done | bytes 131104 | tf_op jit(solution)/shard_map/ppermute | solution.py:548
  207.6 1.6 collective-permute-done.27.refs_3_
  209.2 3.0 project.2
  213.1 1.6 collective-permute-start.30
  214.7 12.8 %collective-permute-done.32.refs_0_ = bf16[256,1024]{1,0:T(8,128)(2,1)S(1)} collective-permute-done((bf16[256,1024]{1,0:T(8,128)(2,1)S(1)}, bf16[256,1024]{1,0:T(8,128)(2,1)S(1)}, u32[]{:S(2)}, u32[]{:S(2)}) %collective-permute-start.32) | collective-permute-done | bytes 524320 | tf_op jit(solution)/shard_map/ppermute | solution.py:548
  227.5 10.3 %collective-permute-done.30.refs_0_ = bf16[256,1024]{1,0:T(8,128)(2,1)S(1)} collective-permute-done((bf16[256,1024]{1,0:T(8,128)(2,1)S(1)}, bf16[256,1024]{1,0:T(8,128)(2,1)S(1)}, u32[]{:S(2)}, u32[]{:S(2)}) %collective-permute-start.30) | collective-permute-done | bytes 524320 | tf_op jit(solution)/shard_map/ppermute | solution.py:548
  237.8 13.2 %front.7 = (bf16[2048,256]{1,0:T(8,128)(2,1)S(1)}, bf16[256,2048]{1,0:T(8,128)(2,1)S(1)}, bf16[4,2048,128]{2,1,0:T(8,128)(2,1)S(1)}, f32[4,192,512]{2,1,0:T(8,128)S(1)}) custom-call(s32[2]{0:T(128)S(1)} %copy-done.6, s32[1,2048]{1,0:T(1,128)S(1)} %copy-done.7, bf16[1024,768]{1,0:T(8,128)(2,1)S(1)} %get-tuple-element.76.w_ref, ...), custom_call_target="tpu_custom_call" | custom-call | flops 12884901888 | bytes 6291456 | tf_op jit(solution)/shard_map/front/pallas_call | solution.py:284
  251.1 7.5 %front.8 = (bf16[2048,256]{1,0:T(8,128)(2,1)S(1)}, bf16[256,2048]{1,0:T(8,128)(2,1)S(1)}, bf16[4,2048,128]{2,1,0:T(8,128)(2,1)S(1)}, f32[4,192,512]{2,1,0:T(8,128)S(1)}) custom-call(s32[2]{0:T(128)S(1)} %copy-done.6, s32[1,2048]{1,0:T(1,128)S(1)} %copy-done.7, ...), custom_call_target="tpu_custom_call", output_to_operand_aliasing={{0}: (7, {}), {1}: (8, {}), {2}: (9, {})} | custom-call | flops 6442450944 | bytes 6291456 | tf_op jit(solution)/shard_map/front/pallas_call | solution.py:284
  258.6 7.9 %front.9 = (bf16[2048,256]{1,0:T(8,128)(2,1)S(1)}, bf16[256,2048]{1,0:T(8,128)(2,1)S(1)}, bf16[4,2048,128]{2,1,0:T(8,128)(2,1)S(1)}, bf16[192,512]{1,0:T(8,128)(...) custom-call(s32[2]{0:T(128)S(1)} %copy-done.6, ...), custom_call_target="tpu_custom_call", output_to_operand_aliasing={{0}: (7, {}), {1}: (8, {}), {2}: (9, {})} | custom-call | flops 6442450944 | bytes 6291456 | tf_op jit(solution)/shard_map/front/pallas_call | solution.py:284
  266.5 3.1 collective-permute-start.35
  270.1 1.9 collective-permute-start.37
  272.1 6.6 %collective-permute-done.35 = bf16[192,512]{1,0:T(8,128)(2,1)S(1)} collective-permute-done((bf16[192,512]{1,0:T(8,128)(2,1)S(1)}, bf16[192,512]{1,0:T(8,128)(2,1)S(1)}, u32[]{:S(2)}, u32[]{:S(2)}) %collective-permute-start.35) | collective-permute-done | bytes 196640 | tf_op jit(solution)/shard_map/ppermute | solution.py:548
  278.7 8.1 %collective-permute-done.36 = bf16[192,512]{1,0:T(8,128)(2,1)S(1)} collective-permute-done((bf16[192,512]{1,0:T(8,128)(2,1)S(1)}, bf16[192,512]{1,0:T(8,128)(2,1)S(1)}, u32[]{:S(2)}, u32[]{:S(2)}) %collective-permute-start.36) | collective-permute-done | bytes 196640 | tf_op jit(solution)/shard_map/ppermute | solution.py:548
  287.5 16.7 %attend.6.refs_0_ = bf16[2048,256]{1,0:T(8,128)(2,1)S(1)} custom-call(bf16[2048,256]{1,0:T(8,128)(2,1)S(1)} %get-tuple-element.89.q_ref, bf16[256,2048]{1,0:T(8,128)(2,1)S(1)} %get-tuple-element.90.k_ref, bf16[4,2048,128]{2,1,0:T(8,128)(2,1)S(1)} %get-tuple-element.91.v_ref), custom_call_target="tpu_custom_call" | custom-call | flops 12884901888 | bytes 4194304 | tf_op jit(solution)/shard_map/attend/pallas_call | solution.py:328
  304.2 5.3 %newton.3.refs_0_ = bf16[192,512]{1,0:T(8,128)(2,1)S(1)} custom-call(s32[2]{0:T(128)S(1)} %copy-done.6, bf16[4,3,512,128]{3,2,1,0:T(8,128)(2,1)S(1)} %get-tuple-element.77.ft_ref, bf16[192,512]{1,0:T(8,128)(2,1)S(1)} %add_convert_fusion.own_ref, bf16[192,512]{1,0:T(8,128)(2,1)S(1)} %collective-permute-done.38.got_ref), custom_call_target="tpu_custom_call" | custom-call | flops 1073741824 | bytes 2097152 | tf_op jit(solution)/shard_map/newton/pallas_call | solution.py:392
  309.5 4.1 %collective-permute-start.39 = (bf16[192,512]{1,0:T(8,128)(2,1)S(1)}, bf16[192,512]{1,0:T(8,128)(2,1)S(1)}, u32[]{:S(2)}, u32[]{:S(2)}) collective-permute-start(bf16[192,512]{1,0:T(8,128)(2,1)S(1)} %newton.3.refs_0_), channel_id=1, source_target_pairs={{0,8},{4,12},{8,0},{12,4},{16,24},{20,28},{24,16},{28,20},{1,9},{5... | collective-permute-start | bytes 589832 | tf_op jit(solution)/shard_map/ppermute | solution.py:548
  313.6 5.6 %attend.7.a_ref = bf16[2048,256]{1,0:T(8,128)(2,1)S(1)} custom-call(bf16[2048,256]{1,0:T(8,128)(2,1)S(1)} %get-tuple-element.89.q_ref, bf16[256,2048]{1,0:T(8,128)(2,1)S(1)} %get-tuple-element.90.k_ref, bf16[4,2048,128]{2,1,0:T(8,128)(2,1)S(1)} %get-tuple-element.91.v_ref, bf16[2048,256]{1,0:T(8,128)(2,1)S(1)} %attend.6.refs_0_), custom_call_target="tpu_custom_call", output_to_operand_aliasing={{}: (3, {})} | custom-call | flops 4294967296 | bytes 4194304 | tf_op jit(solution)/shard_map/attend/pallas_call | solution.py:328
  319.7 1.9 collective-permute-start.41
  321.6 7.9 %shard_map.58 = (bf16[1024,128]{1,0:T(8,128)(2,1)S(1)}, bf16[512,128]{1,0:T(8,128)(2,1)S(1)}, bf16[512,128]{1,0:T(8,128)(2,1)S(1)}) custom-call(s32[2]{0:T(128)S(1)} %copy-done.6, bf16[2048,256]{1,0:T(8,128)(2,1)S(1)} %get-tuple-element.89.q_ref, bf16[2048,256]{1,0:T(8,128)(2,1)S(1)} %attend.7.a_ref, bf16[192,512]{1,0:T(8,128)(2,1)S(1)} %newton.3.refs_0_, ...), custom_call_target="tpu_custom_call" | custom-call | flops 3221225472 | bytes 2097152 | tf_op jit(solution)/shard_map/pallas_call | solution.py:479
  329.5 4.5 %collective-permute-done.40.refs_1_.refs_0_ = bf16[192,512]{1,0:T(8,128)(2,1)S(1)} collective-permute-done((bf16[192,512]{1,0:T(8,128)(2,1)S(1)}, bf16[192,512]{1,0:T(8,128)(2,1)S(1)}, u32[]{:S(2)}, u32[]{:S(2)}) %collective-permute-start.40) | collective-permute-done | bytes 196640 | tf_op jit(solution)/shard_map/ppermute | solution.py:548
  334.0 4.3 %shard_map.59 = (bf16[512,256]{1,0:T(8,128)(2,1)S(1)}, bf16[512,256]{1,0:T(8,128)(2,1)S(1)}) custom-call(s32[2]{0:T(128)S(1)} %copy-done.6, bf16[2048,256]{1,0:T(8,128)(2,1)S(1)} %get-tuple-element.89.q_ref, bf16[2048,256]{1,0:T(8,128)(2,1)S(1)} %attend.7.a_ref, bf16[1024,128]{1,0:T(8,128)(2,1)S(1)} %get-tuple-element.96.refs_0_, ...), custom_call_target="tpu_custom_call" | custom-call | flops 1610612736 | bytes 2097152 | tf_op jit(solution)/shard_map/pallas_call | solution.py:479
  338.3 4.2 %shard_map.60 = (bf16[512,128]{1,0:T(8,128)(2,1)S(1)}, bf16[512,128]{1,0:T(8,128)(2,1)S(1)}) custom-call(s32[2]{0:T(128)S(1)} %copy-done.6, bf16[2048,256]{1,0:T(8,128)(2,1)S(1)} %get-tuple-element.89.q_ref, bf16[2048,256]{1,0:T(8,128)(2,1)S(1)} %attend.7.a_ref, bf16[192,512]{1,0:T(8,128)(2,1)S(1)} %collective-permute-done.40.refs_1_.refs_0_, ...), custom_call_target="tpu_custom_call" | custom-call | flops 1610612736 | bytes 2097152 | tf_op jit(solution)/shard_map/pallas_call | solution.py:479
  346.1 2.9 collective-permute-done.45.refs_4_
  349.0 1.8 collective-permute-done.46.refs_5_
  350.8 3.8 %collective-permute-done.43.refs_2_ = bf16[512,128]{1,0:T(8,128)(2,1)S(1)} collective-permute-done((bf16[512,128]{1,0:T(8,128)(2,1)S(1)}, bf16[512,128]{1,0:T(8,128)(2,1)S(1)}, u32[]{:S(2)}, u32[]{:S(2)}) %collective-permute-start.43) | collective-permute-done | bytes 131104 | tf_op jit(solution)/shard_map/ppermute | solution.py:548
  354.6 1.8 collective-permute-done.44.refs_3_
  356.5 3.3 project.3
  (75 shorter events, 19.3 us)
Async XLA Ops:
  0.0 10.9 %copy-start = (bf16[512,1024]{1,0:T(8,128)(2,1)S(1)}, bf16[512,1024]{1,0:T(8,128)(2,1)}, u32[]{:S(2)}) copy-start(bf16[512,1024]{1,0:T(8,128)(2,1)} %s_ref.1) | copy-start | bytes 3145732
  2.0 15.8 %collective-permute-start.9 = (bf16[576,256]{1,0:T(8,128)(2,1)}, bf16[576,256]{1,0:T(8,128)(2,1)S(1)}, u32[]{:S(2)}, u32[]{:S(2)}) collective-permute-start(bf16[576,256]{1,0:T(8,128)(2,1)} %pack.3.refs_0_), channel_id=1, source_target_pairs={{0,8},{4,12},{8,0},{12,4},{16,24},{20,28},{24,16},{28,20},{1,9},{5... | collective-permute-start | bytes 884744 | tf_op jit(solution)/shard_map/ppermute | solution.py:548
  5.1 23.6 %collective-permute-start.11 = (bf16[576,256]{1,0:T(8,128)(2,1)}, bf16[576,256]{1,0:T(8,128)(2,1)S(1)}, u32[]{:S(2)}, u32[]{:S(2)}) collective-permute-start(bf16[576,256]{1,0:T(8,128)(2,1)} %pack.3.refs_0_), channel_id=1, source_target_pairs={{0,16},{4,20},{8,24},{12,28},{16,0},{20,4},{24,8},{28,12},{1,17},{... | collective-permute-start | bytes 884744 | tf_op jit(solution)/shard_map/ppermute | solution.py:548
  7.7 22.5 %collective-permute-start.13 = (bf16[576,256]{1,0:T(8,128)(2,1)}, bf16[576,256]{1,0:T(8,128)(2,1)S(1)}, u32[]{:S(2)}, u32[]{:S(2)}) collective-permute-start(bf16[576,256]{1,0:T(8,128)(2,1)} %pack.3.refs_0_), channel_id=1, source_target_pairs={{0,24},{4,28},{8,16},{12,20},{16,8},{20,12},{24,0},{28,4},{1,25},{... | collective-permute-start | bytes 884744 | tf_op jit(solution)/shard_map/ppermute | solution.py:548
  7.7 23.1 %collective-permute-start.8 = (bf16[576,256]{1,0:T(8,128)(2,1)}, bf16[576,256]{1,0:T(8,128)(2,1)S(1)}, u32[]{:S(2)}, u32[]{:S(2)}) collective-permute-start(bf16[576,256]{1,0:T(8,128)(2,1)} %pack.3.refs_0_), channel_id=1, source_target_pairs={{0,4},{4,0},{8,12},{12,8},{16,20},{20,16},{24,28},{28,24},{1,5},{5... | collective-permute-start | bytes 884744 | tf_op jit(solution)/shard_map/ppermute | solution.py:548
  10.9 35.7 %copy-start.2 = (bf16[576,256]{1,0:T(8,128)(2,1)S(1)}, bf16[576,256]{1,0:T(8,128)(2,1)}, u32[]{:S(2)}) copy-start(bf16[576,256]{1,0:T(8,128)(2,1)} %pack.3.refs_0_) | copy-start | bytes 884740
  11.2 73.7 %collective-permute-start.17 = (bf16[512,1024]{1,0:T(8,128)(2,1)S(1)}, bf16[512,1024]{1,0:T(8,128)(2,1)}, u32[]{:S(2)}, u32[]{:S(2)}) collective-permute-start(bf16[512,1024]{1,0:T(8,128)(2,1)S(1)} %fusion.1.refs_0_), channel_id=1, source_target_pairs={{0,1},{1,0},{2,3},{3,2},{4,5},{5,4},{6,7},{7,6},{8,9},{9,8},{10,11... | collective-permute-start | bytes 3145736 | tf_op jit(solution)/shard_map/ppermute | solution.py:548
  17.9 68.4 %collective-permute-start.15 = (bf16[512,1024]{1,0:T(8,128)(2,1)S(1)}, bf16[512,1024]{1,0:T(8,128)(2,1)}, u32[]{:S(2)}, u32[]{:S(2)}) collective-permute-start(bf16[512,1024]{1,0:T(8,128)(2,1)S(1)} %fusion.1.refs_0_), channel_id=1, source_target_pairs={{0,2},{1,3},{2,0},{3,1},{4,6},{5,7},{6,4},{7,5},{8,10},{9,11},{10,... | collective-permute-start | bytes 3145736 | tf_op jit(solution)/shard_map/ppermute | solution.py:548
  28.7 9.6 %collective-permute-start.10 = (bf16[576,256]{1,0:T(8,128)(2,1)S(1)}, bf16[576,256]{1,0:T(8,128)(2,1)}, u32[]{:S(2)}, u32[]{:S(2)}) collective-permute-start(bf16[576,256]{1,0:T(8,128)(2,1)S(1)} %collective-permute-done.9.refs_2_), channel_id=1, source_target_pairs={{0,4},{4,0},{8,12},{12,8},{16,20},{20,16},{24,28},{28,24},{1,5},{5... | collective-permute-start | bytes 884744 | tf_op jit(solution)/shard_map/ppermute | solution.py:548
  30.2 11.3 %collective-permute-start.12 = (bf16[576,256]{1,0:T(8,128)(2,1)S(1)}, bf16[576,256]{1,0:T(8,128)(2,1)}, u32[]{:S(2)}, u32[]{:S(2)}) collective-permute-start(bf16[576,256]{1,0:T(8,128)(2,1)S(1)} %collective-permute-done.11.refs_4_), channel_id=1, source_target_pairs={{0,4},{4,0},{8,12},{12,8},{16,20},{20,16},{24,28},{28,24},{1,5},{5... | collective-permute-start | bytes 884744 | tf_op jit(solution)/shard_map/ppermute | solution.py:548
  30.8 0.7 copy-start.3
  31.5 13.8 %collective-permute-start.14 = (bf16[576,256]{1,0:T(8,128)(2,1)S(1)}, bf16[576,256]{1,0:T(8,128)(2,1)}, u32[]{:S(2)}, u32[]{:S(2)}) collective-permute-start(bf16[576,256]{1,0:T(8,128)(2,1)S(1)} %collective-permute-done.13.refs_6_), channel_id=1, source_target_pairs={{0,4},{4,0},{8,12},{12,8},{16,20},{20,16},{24,28},{28,24},{1,5},{5... | collective-permute-start | bytes 884744 | tf_op jit(solution)/shard_map/ppermute | solution.py:548
  33.6 52.8 %copy-start.6 = (s32[2]{0:T(128)S(1)}, s32[2]{0:T(128)}, u32[]{:S(2)}) copy-start(s32[2]{0:T(128)} %pad_add_fusion.refs_0_.ids_ref) | copy-start | bytes 28
  33.6 52.8 %copy-start.7 = (s32[1,2048]{1,0:T(1,128)S(1)}, s32[1,2048]{1,0:T(1,128)}, u32[]{:S(2)}) copy-start(s32[1,2048]{1,0:T(1,128)} %mask_ref.9) | copy-start | bytes 24580
  35.9 24.6 %copy-start.1 = (bf16[1088,256]{1,0:T(8,128)(2,1)S(1)}, bf16[1088,256]{1,0:T(8,128)(2,1)}, u32[]{:S(2)}) copy-start(bf16[1088,256]{1,0:T(8,128)(2,1)} %pack.2.refs_0_) | copy-start | bytes 1671172
  38.4 22.1 %collective-permute-start.1 = (bf16[1088,256]{1,0:T(8,128)(2,1)}, bf16[1088,256]{1,0:T(8,128)(2,1)S(1)}, u32[]{:S(2)}, u32[]{:S(2)}) collective-permute-start(bf16[1088,256]{1,0:T(8,128)(2,1)} %pack.2.refs_0_), channel_id=1, source_target_pairs={{0,8},{4,12},{8,0},{12,4},{16,24},{20,28},{24,16},{28,20},{1,9},{5... | collective-permute-start | bytes 1671176 | tf_op jit(solution)/shard_map/ppermute | solution.py:548
  41.5 41.3 %collective-permute-start.3 = (bf16[1088,256]{1,0:T(8,128)(2,1)}, bf16[1088,256]{1,0:T(8,128)(2,1)S(1)}, u32[]{:S(2)}, u32[]{:S(2)}) collective-permute-start(bf16[1088,256]{1,0:T(8,128)(2,1)} %pack.2.refs_0_), channel_id=1, source_target_pairs={{0,16},{4,20},{8,24},{12,28},{16,0},{20,4},{24,8},{28,12},{1,17},{... | collective-permute-start | bytes 1671176 | tf_op jit(solution)/shard_map/ppermute | solution.py:548
  45.2 39.1 %collective-permute-start.5 = (bf16[1088,256]{1,0:T(8,128)(2,1)}, bf16[1088,256]{1,0:T(8,128)(2,1)S(1)}, u32[]{:S(2)}, u32[]{:S(2)}) collective-permute-start(bf16[1088,256]{1,0:T(8,128)(2,1)} %pack.2.refs_0_), channel_id=1, source_target_pairs={{0,24},{4,28},{8,16},{12,20},{16,8},{20,12},{24,0},{28,4},{1,25},{... | collective-permute-start | bytes 1671176 | tf_op jit(solution)/shard_map/ppermute | solution.py:548
  46.6 1.0 copy-start.4
  47.6 0.6 copy-start.5
  60.5 60.4 %collective-permute-start = (bf16[1088,256]{1,0:T(8,128)(2,1)S(1)}, bf16[1088,256]{1,0:T(8,128)(2,1)S(1)}, u32[]{:S(2)}, u32[]{:S(2)}) collective-permute-start(bf16[1088,256]{1,0:T(8,128)(2,1)S(1)} %copy-done.1), channel_id=1, source_target_pairs={{0,4},{4,0},{8,12},{12,8},{16,20},{20,16},{24,28},{28,24},{1,5},{5... | collective-permute-start | bytes 1671176 | tf_op jit(solution)/shard_map/ppermute | solution.py:548
  82.8 38.7 %collective-permute-start.2 = (bf16[1088,256]{1,0:T(8,128)(2,1)S(1)}, bf16[1088,256]{1,0:T(8,128)(2,1)S(1)}, u32[]{:S(2)}, u32[]{:S(2)}) collective-permute-start(bf16[1088,256]{1,0:T(8,128)(2,1)S(1)} %collective-permute-done.1.refs_2_), channel_id=1, source_target_pairs={{0,4},{4,0},{8,12},{12,8},{16,20},{20,16},{24,28},{28,24},{1,5},{5... | collective-permute-start | bytes 1671176 | tf_op jit(solution)/shard_map/ppermute | solution.py:548
  84.3 39.1 %collective-permute-start.4 = (bf16[1088,256]{1,0:T(8,128)(2,1)S(1)}, bf16[1088,256]{1,0:T(8,128)(2,1)S(1)}, u32[]{:S(2)}, u32[]{:S(2)}) collective-permute-start(bf16[1088,256]{1,0:T(8,128)(2,1)S(1)} %collective-permute-done.3.refs_4_), channel_id=1, source_target_pairs={{0,4},{4,0},{8,12},{12,8},{16,20},{20,16},{24,28},{28,24},{1,5},{5... | collective-permute-start | bytes 1671176 | tf_op jit(solution)/shard_map/ppermute | solution.py:548
  84.8 38.6 %collective-permute-start.6 = (bf16[1088,256]{1,0:T(8,128)(2,1)S(1)}, bf16[1088,256]{1,0:T(8,128)(2,1)S(1)}, u32[]{:S(2)}, u32[]{:S(2)}) collective-permute-start(bf16[1088,256]{1,0:T(8,128)(2,1)S(1)} %collective-permute-done.5.refs_6_), channel_id=1, source_target_pairs={{0,4},{4,0},{8,12},{12,8},{16,20},{20,16},{24,28},{28,24},{1,5},{5... | collective-permute-start | bytes 1671176 | tf_op jit(solution)/shard_map/ppermute | solution.py:548
  86.3 14.2 %collective-permute-start.16 = (bf16[512,1024]{1,0:T(8,128)(2,1)}, bf16[512,1024]{1,0:T(8,128)(2,1)S(1)}, u32[]{:S(2)}, u32[]{:S(2)}) collective-permute-start(bf16[512,1024]{1,0:T(8,128)(2,1)} %collective-permute-done.15.refs_0_), channel_id=1, source_target_pairs={{0,1},{1,0},{2,3},{3,2},{4,5},{5,4},{6,7},{7,6},{8,9},{9,8},{10,11... | collective-permute-start | bytes 3145736 | tf_op jit(solution)/shard_map/ppermute | solution.py:548
  114.7 15.0 %collective-permute-start.18 = (bf16[192,512]{1,0:T(8,128)(2,1)S(1)}, bf16[192,512]{1,0:T(8,128)(2,1)S(1)}, u32[]{:S(2)}, u32[]{:S(2)}) collective-permute-start(bf16[192,512]{1,0:T(8,128)(2,1)S(1)} %get-tuple-element.65), channel_id=1, source_target_pairs={{0,8},{4,12},{8,0},{12,4},{16,24},{20,28},{24,16},{28,20},{1,9},{5... | collective-permute-start | bytes 589832 | tf_op jit(solution)/shard_map/ppermute | solution.py:548
  120.9 17.1 %collective-permute-start.19 = (bf16[192,512]{1,0:T(8,128)(2,1)S(1)}, bf16[192,512]{1,0:T(8,128)(2,1)S(1)}, u32[]{:S(2)}, u32[]{:S(2)}) collective-permute-start(bf16[192,512]{1,0:T(8,128)(2,1)S(1)} %get-tuple-element.66), channel_id=1, source_target_pairs={{0,16},{4,20},{8,24},{12,28},{16,0},{20,4},{24,8},{28,12},{1,17},{... | collective-permute-start | bytes 589832 | tf_op jit(solution)/shard_map/ppermute | solution.py:548
  121.5 16.6 %collective-permute-start.20 = (bf16[192,512]{1,0:T(8,128)(2,1)S(1)}, bf16[192,512]{1,0:T(8,128)(2,1)S(1)}, u32[]{:S(2)}, u32[]{:S(2)}) collective-permute-start(bf16[192,512]{1,0:T(8,128)(2,1)S(1)} %get-tuple-element.67), channel_id=1, source_target_pairs={{0,24},{4,28},{8,16},{12,20},{16,8},{20,12},{24,0},{28,4},{1,25},{... | collective-permute-start | bytes 589832 | tf_op jit(solution)/shard_map/ppermute | solution.py:548
  124.7 84.5 %collective-permute-start.7 = (bf16[2048,512]{1,0:T(8,128)(2,1)S(1)}, bf16[2048,512]{1,0:T(8,128)(2,1)S(1)}, u32[]{:S(2)}, u32[]{:S(2)}) collective-permute-start(bf16[2048,512]{1,0:T(8,128)(2,1)S(1)} %get-tuple-element.54.own_ref), channel_id=1, source_target_pairs={{0,1},{1,0},{2,3},{3,2},{4,5},{5,4},{6,7},{7,6},{8,9},{9,8},{10,11... | collective-permute-start | bytes 6291464 | tf_op jit(solution)/shard_map/ppermute | solution.py:548
  138.2 18.3 %collective-permute-start.21 = (bf16[192,512]{1,0:T(8,128)(2,1)S(1)}, bf16[192,512]{1,0:T(8,128)(2,1)S(1)}, u32[]{:S(2)}, u32[]{:S(2)}) collective-permute-start(bf16[192,512]{1,0:T(8,128)(2,1)S(1)} %add_convert_fusion.1.own_ref), channel_id=1, source_target_pairs={{0,4},{4,0},{8,12},{12,8},{16,20},{20,16},{24,28},{28,24},{1,5},{5... | collective-permute-start | bytes 589832 | tf_op jit(solution)/shard_map/ppermute | solution.py:548
  161.7 18.4 %collective-permute-start.23 = (bf16[192,512]{1,0:T(8,128)(2,1)S(1)}, bf16[192,512]{1,0:T(8,128)(2,1)S(1)}, u32[]{:S(2)}, u32[]{:S(2)}) collective-permute-start(bf16[192,512]{1,0:T(8,128)(2,1)S(1)} %newton.2.refs_0_), channel_id=1, source_target_pairs={{0,16},{4,20},{8,24},{12,28},{16,0},{20,4},{24,8},{28,12},{1,17},{... | collective-permute-start | bytes 589832 | tf_op jit(solution)/shard_map/ppermute | solution.py:548
  166.0 14.1 %collective-permute-start.24 = (bf16[192,512]{1,0:T(8,128)(2,1)S(1)}, bf16[192,512]{1,0:T(8,128)(2,1)S(1)}, u32[]{:S(2)}, u32[]{:S(2)}) collective-permute-start(bf16[192,512]{1,0:T(8,128)(2,1)S(1)} %newton.2.refs_0_), channel_id=1, source_target_pairs={{0,24},{4,28},{8,16},{12,20},{16,8},{20,12},{24,0},{28,4},{1,25},{... | collective-permute-start | bytes 589832 | tf_op jit(solution)/shard_map/ppermute | solution.py:548
  168.0 18.1 %collective-permute-start.22 = (bf16[192,512]{1,0:T(8,128)(2,1)S(1)}, bf16[192,512]{1,0:T(8,128)(2,1)S(1)}, u32[]{:S(2)}, u32[]{:S(2)}) collective-permute-start(bf16[192,512]{1,0:T(8,128)(2,1)S(1)} %newton.2.refs_0_), channel_id=1, source_target_pairs={{0,8},{4,12},{8,0},{12,4},{16,24},{20,28},{24,16},{28,20},{1,9},{5... | collective-permute-start | bytes 589832 | tf_op jit(solution)/shard_map/ppermute | solution.py:548
  184.4 16.1 %collective-permute-start.28 = (bf16[512,128]{1,0:T(8,128)(2,1)S(1)}, bf16[512,128]{1,0:T(8,128)(2,1)S(1)}, u32[]{:S(2)}, u32[]{:S(2)}) collective-permute-start(bf16[512,128]{1,0:T(8,128)(2,1)S(1)} %get-tuple-element.73), channel_id=1, source_target_pairs={{0,2},{1,3},{2,0},{3,1},{4,6},{5,7},{6,4},{7,5},{8,10},{9,11},{10,... | collective-permute-start | bytes 393224 | tf_op jit(solution)/shard_map/ppermute | solution.py:548
  198.2 10.9 %collective-permute-start.25 = (bf16[512,256]{1,0:T(8,128)(2,1)S(1)}, bf16[512,256]{1,0:T(8,128)(2,1)S(1)}, u32[]{:S(2)}, u32[]{:S(2)}) collective-permute-start(bf16[512,256]{1,0:T(8,128)(2,1)S(1)} %get-tuple-element.70), channel_id=1, source_target_pairs={{0,1},{1,0},{2,3},{3,2},{4,5},{5,4},{6,7},{7,6},{8,9},{9,8},{10,11... | collective-permute-start | bytes 786440 | tf_op jit(solution)/shard_map/ppermute | solution.py:548
  198.3 5.2 %collective-permute-start.29 = (bf16[512,128]{1,0:T(8,128)(2,1)S(1)}, bf16[512,128]{1,0:T(8,128)(2,1)S(1)}, u32[]{:S(2)}, u32[]{:S(2)}) collective-permute-start(bf16[512,128]{1,0:T(8,128)(2,1)S(1)} %get-tuple-element.74), channel_id=1, source_target_pairs={{0,3},{1,2},{2,1},{3,0},{4,7},{5,6},{6,5},{7,4},{8,11},{9,10},{10,... | collective-permute-start | bytes 393224 | tf_op jit(solution)/shard_map/ppermute | solution.py:548
  198.9 8.7 %collective-permute-start.26 = (bf16[512,128]{1,0:T(8,128)(2,1)S(1)}, bf16[512,128]{1,0:T(8,128)(2,1)S(1)}, u32[]{:S(2)}, u32[]{:S(2)}) collective-permute-start(bf16[512,128]{1,0:T(8,128)(2,1)S(1)} %get-tuple-element.71), channel_id=1, source_target_pairs={{0,2},{1,3},{2,0},{3,1},{4,6},{5,7},{6,4},{7,5},{8,10},{9,11},{10,... | collective-permute-start | bytes 393224 | tf_op jit(solution)/shard_map/ppermute | solution.py:548
  200.4 8.7 %collective-permute-start.27 = (bf16[512,128]{1,0:T(8,128)(2,1)S(1)}, bf16[512,128]{1,0:T(8,128)(2,1)S(1)}, u32[]{:S(2)}, u32[]{:S(2)}) collective-permute-start(bf16[512,128]{1,0:T(8,128)(2,1)S(1)} %get-tuple-element.72), channel_id=1, source_target_pairs={{0,3},{1,2},{2,1},{3,0},{4,7},{5,6},{6,5},{7,4},{8,11},{9,10},{10,... | collective-permute-start | bytes 393224 | tf_op jit(solution)/shard_map/ppermute | solution.py:548
  212.2 25.6 %collective-permute-start.34 = (bf16[512,1024]{1,0:T(8,128)(2,1)S(1)}, bf16[512,1024]{1,0:T(8,128)(2,1)S(1)}, u32[]{:S(2)}, u32[]{:S(2)}) collective-permute-start(bf16[512,1024]{1,0:T(8,128)(2,1)S(1)} %get-tuple-element.80.refs_0_), channel_id=1, source_target_pairs={{0,1},{1,0},{2,3},{3,2},{4,5},{5,4},{6,7},{7,6},{8,9},{9,8},{10,11... | collective-permute-start | bytes 3145736 | tf_op jit(solution)/shard_map/ppermute | solution.py:548
  212.7 14.8 %collective-permute-start.32 = (bf16[256,1024]{1,0:T(8,128)(2,1)S(1)}, bf16[256,1024]{1,0:T(8,128)(2,1)S(1)}, u32[]{:S(2)}, u32[]{:S(2)}) collective-permute-start(bf16[256,1024]{1,0:T(8,128)(2,1)S(1)} %get-tuple-element.79), channel_id=1, source_target_pairs={{0,2},{1,3},{2,0},{3,1},{4,6},{5,7},{6,4},{7,5},{8,10},{9,11},{10,... | collective-permute-start | bytes 1572872 | tf_op jit(solution)/shard_map/ppermute | solution.py:548
  213.1 24.7 %collective-permute-start.30 = (bf16[256,1024]{1,0:T(8,128)(2,1)S(1)}, bf16[256,1024]{1,0:T(8,128)(2,1)S(1)}, u32[]{:S(2)}, u32[]{:S(2)}) collective-permute-start(bf16[256,1024]{1,0:T(8,128)(2,1)S(1)} %get-tuple-element.78), channel_id=1, source_target_pairs={{0,2},{1,3},{2,0},{3,1},{4,6},{5,7},{6,4},{7,5},{8,10},{9,11},{10,... | collective-permute-start | bytes 1572872 | tf_op jit(solution)/shard_map/ppermute | solution.py:548
  227.5 23.6 %collective-permute-start.33 = (bf16[256,1024]{1,0:T(8,128)(2,1)S(1)}, bf16[256,1024]{1,0:T(8,128)(2,1)S(1)}, u32[]{:S(2)}, u32[]{:S(2)}) collective-permute-start(bf16[256,1024]{1,0:T(8,128)(2,1)S(1)} %collective-permute-done.32.refs_0_), channel_id=1, source_target_pairs={{0,1},{1,0},{2,3},{3,2},{4,5},{5,4},{6,7},{7,6},{8,9},{9,8},{10,11... | collective-permute-start | bytes 1572872 | tf_op jit(solution)/shard_map/ppermute | solution.py:548
  237.8 20.8 %collective-permute-start.31 = (bf16[256,1024]{1,0:T(8,128)(2,1)S(1)}, bf16[256,1024]{1,0:T(8,128)(2,1)S(1)}, u32[]{:S(2)}, u32[]{:S(2)}) collective-permute-start(bf16[256,1024]{1,0:T(8,128)(2,1)S(1)} %collective-permute-done.30.refs_0_), channel_id=1, source_target_pairs={{0,1},{1,0},{2,3},{3,2},{4,5},{5,4},{6,7},{7,6},{8,9},{9,8},{10,11... | collective-permute-start | bytes 1572872 | tf_op jit(solution)/shard_map/ppermute | solution.py:548
  266.5 12.2 %collective-permute-start.35 = (bf16[192,512]{1,0:T(8,128)(2,1)S(1)}, bf16[192,512]{1,0:T(8,128)(2,1)S(1)}, u32[]{:S(2)}, u32[]{:S(2)}) collective-permute-start(bf16[192,512]{1,0:T(8,128)(2,1)S(1)} %get-tuple-element.93), channel_id=1, source_target_pairs={{0,8},{4,12},{8,0},{12,4},{16,24},{20,28},{24,16},{28,20},{1,9},{5... | collective-permute-start | bytes 589832 | tf_op jit(solution)/shard_map/ppermute | solution.py:548
  269.6 17.1 %collective-permute-start.36 = (bf16[192,512]{1,0:T(8,128)(2,1)S(1)}, bf16[192,512]{1,0:T(8,128)(2,1)S(1)}, u32[]{:S(2)}, u32[]{:S(2)}) collective-permute-start(bf16[192,512]{1,0:T(8,128)(2,1)S(1)} %get-tuple-element.94), channel_id=1, source_target_pairs={{0,16},{4,20},{8,24},{12,28},{16,0},{20,4},{24,8},{28,12},{1,17},{... | collective-permute-start | bytes 589832 | tf_op jit(solution)/shard_map/ppermute | solution.py:548
  270.1 16.6 %collective-permute-start.37 = (bf16[192,512]{1,0:T(8,128)(2,1)S(1)}, bf16[192,512]{1,0:T(8,128)(2,1)S(1)}, u32[]{:S(2)}, u32[]{:S(2)}) collective-permute-start(bf16[192,512]{1,0:T(8,128)(2,1)S(1)} %get-tuple-element.95), channel_id=1, source_target_pairs={{0,24},{4,28},{8,16},{12,20},{16,8},{20,12},{24,0},{28,4},{1,25},{... | collective-permute-start | bytes 589832 | tf_op jit(solution)/shard_map/ppermute | solution.py:548
  286.9 17.3 %collective-permute-start.38 = (bf16[192,512]{1,0:T(8,128)(2,1)S(1)}, bf16[192,512]{1,0:T(8,128)(2,1)S(1)}, u32[]{:S(2)}, u32[]{:S(2)}) collective-permute-start(bf16[192,512]{1,0:T(8,128)(2,1)S(1)} %add_convert_fusion.own_ref), channel_id=1, source_target_pairs={{0,4},{4,0},{8,12},{12,8},{16,20},{20,16},{24,28},{28,24},{1,5},{5... | collective-permute-start | bytes 589832 | tf_op jit(solution)/shard_map/ppermute | solution.py:548
  309.5 12.1 %collective-permute-start.39 = (bf16[192,512]{1,0:T(8,128)(2,1)S(1)}, bf16[192,512]{1,0:T(8,128)(2,1)S(1)}, u32[]{:S(2)}, u32[]{:S(2)}) collective-permute-start(bf16[192,512]{1,0:T(8,128)(2,1)S(1)} %newton.3.refs_0_), channel_id=1, source_target_pairs={{0,8},{4,12},{8,0},{12,4},{16,24},{20,28},{24,16},{28,20},{1,9},{5... | collective-permute-start | bytes 589832 | tf_op jit(solution)/shard_map/ppermute | solution.py:548
  319.1 14.9 %collective-permute-start.40 = (bf16[192,512]{1,0:T(8,128)(2,1)S(1)}, bf16[192,512]{1,0:T(8,128)(2,1)S(1)}, u32[]{:S(2)}, u32[]{:S(2)}) collective-permute-start(bf16[192,512]{1,0:T(8,128)(2,1)S(1)} %newton.3.refs_0_), channel_id=1, source_target_pairs={{0,16},{4,20},{8,24},{12,28},{16,0},{20,4},{24,8},{28,12},{1,17},{... | collective-permute-start | bytes 589832 | tf_op jit(solution)/shard_map/ppermute | solution.py:548
  319.7 14.3 %collective-permute-start.41 = (bf16[192,512]{1,0:T(8,128)(2,1)S(1)}, bf16[192,512]{1,0:T(8,128)(2,1)S(1)}, u32[]{:S(2)}, u32[]{:S(2)}) collective-permute-start(bf16[192,512]{1,0:T(8,128)(2,1)S(1)} %newton.3.refs_0_), channel_id=1, source_target_pairs={{0,24},{4,28},{8,16},{12,20},{16,8},{20,12},{24,0},{28,4},{1,25},{... | collective-permute-start | bytes 589832 | tf_op jit(solution)/shard_map/ppermute | solution.py:548
  338.3 18.2 %collective-permute-start.42 = (bf16[512,256]{1,0:T(8,128)(2,1)S(1)}, bf16[512,256]{1,0:T(8,128)(2,1)S(1)}, u32[]{:S(2)}, u32[]{:S(2)}) collective-permute-start(bf16[512,256]{1,0:T(8,128)(2,1)S(1)} %get-tuple-element.98), channel_id=1, source_target_pairs={{0,1},{1,0},{2,3},{3,2},{4,5},{5,4},{6,7},{7,6},{8,9},{9,8},{10,11... | collective-permute-start | bytes 786440 | tf_op jit(solution)/shard_map/ppermute | solution.py:548
  342.6 6.4 %collective-permute-start.45 = (bf16[512,128]{1,0:T(8,128)(2,1)S(1)}, bf16[512,128]{1,0:T(8,128)(2,1)S(1)}, u32[]{:S(2)}, u32[]{:S(2)}) collective-permute-start(bf16[512,128]{1,0:T(8,128)(2,1)S(1)} %get-tuple-element.101), channel_id=1, source_target_pairs={{0,2},{1,3},{2,0},{3,1},{4,6},{5,7},{6,4},{7,5},{8,10},{9,11},{10,... | collective-permute-start | bytes 393224 | tf_op jit(solution)/shard_map/ppermute | solution.py:548
  343.1 7.7 %collective-permute-start.46 = (bf16[512,128]{1,0:T(8,128)(2,1)S(1)}, bf16[512,128]{1,0:T(8,128)(2,1)S(1)}, u32[]{:S(2)}, u32[]{:S(2)}) collective-permute-start(bf16[512,128]{1,0:T(8,128)(2,1)S(1)} %get-tuple-element.102), channel_id=1, source_target_pairs={{0,3},{1,2},{2,1},{3,0},{4,7},{5,6},{6,5},{7,4},{8,11},{9,10},{10,... | collective-permute-start | bytes 393224 | tf_op jit(solution)/shard_map/ppermute | solution.py:548
  344.5 10.2 %collective-permute-start.43 = (bf16[512,128]{1,0:T(8,128)(2,1)S(1)}, bf16[512,128]{1,0:T(8,128)(2,1)S(1)}, u32[]{:S(2)}, u32[]{:S(2)}) collective-permute-start(bf16[512,128]{1,0:T(8,128)(2,1)S(1)} %get-tuple-element.99), channel_id=1, source_target_pairs={{0,2},{1,3},{2,0},{3,1},{4,6},{5,7},{6,4},{7,5},{8,10},{9,11},{10,... | collective-permute-start | bytes 393224 | tf_op jit(solution)/shard_map/ppermute | solution.py:548
  345.0 11.5 %collective-permute-start.44 = (bf16[512,128]{1,0:T(8,128)(2,1)S(1)}, bf16[512,128]{1,0:T(8,128)(2,1)S(1)}, u32[]{:S(2)}, u32[]{:S(2)}) collective-permute-start(bf16[512,128]{1,0:T(8,128)(2,1)S(1)} %get-tuple-element.100), channel_id=1, source_target_pairs={{0,3},{1,2},{2,1},{3,0},{4,7},{5,6},{6,5},{7,4},{8,11},{9,10},{10,... | collective-permute-start | bytes 393224 | tf_op jit(solution)/shard_map/ppermute | solution.py:548

commit v2 on v1

--- a/solution.py
+++ b/solution.py
@@ -17,6 +17,10 @@
 log2_e = math.log2(math.e)
 
 F32, BF16 = jnp.float32, jnp.bfloat16
+VIEW, HEAD = "view", "head"
+EARLY, LATE, ALL = "early", "late", "all"
+
+
 SMEM = pl.BlockSpec(memory_space=pltpu.SMEM)
 
 FRONT_TILE, FRONT_WIDTH, FRONT_UNROLL, FRONT_TYPE = 256, 512, 4, F32
@@ -414,9 +418,9 @@
     step = pl.program_id(0)
     place = ids_ref[0] >> 1
     mine = lax.rem(place, heads) // group
-    side = 1 - mine if stage == "late" else mine
+    side = 1 - mine if stage == LATE else mine
     span = group * dim
-    if stage == "all":
+    if stage == ALL:
         at = slice(None)
     else:
         at = pl.ds(pl.multiple_of(side * span, span), span)
@@ -425,7 +429,7 @@
     def _():
         for k in range(count):
             head = place ^ (first_k + k)
-            if stage != "all":
+            if stage != ALL:
                 fast_ref[lax.rem(head, group)] = units_refs[k][...]
                 continue
 
@@ -461,9 +465,9 @@
     dim = cols // heads
     units = fast[0].shape[1]
     group, first_k = heads, 0
-    if stage != "all":
+    if stage != ALL:
         group = heads // 2
-        first_k = 0 if stage == "early" else group
+        first_k = 0 if stage == EARLY else group
         fast = fast[first_k : first_k + group]
     tile = min(APPLY_TILE, tokens)
     first = base * tokens // tile
@@ -473,7 +477,7 @@
     if merge:
         args.append(early)
         in_specs.append(pl.BlockSpec((tile, group * dim), lambda i: (first + i, 0)))
-    width = cols if merge or stage == "all" else group * dim
+    width = cols if merge or stage == ALL else group * dim
     shapes = [(chunks * tokens, width) for _, chunks in spans]
     here = sum(chunks for _, chunks in spans) * tokens
     return pl.pallas_call(
@@ -539,7 +543,7 @@
 
 
 def solution(mesh):
-    views, parts = mesh.shape["view"], mesh.shape["head"]
+    views, parts = mesh.shape[VIEW], mesh.shape[HEAD]
 
     def swap(x, axis, k, keep=None):
         pairs = [(i, i ^ k) for i in range(mesh.shape[axis])]
@@ -550,9 +554,9 @@
     def gather_view(block):
         slabs = {0: block}
         for k in range(2, views, 2):
-            slabs[k] = swap(block, "view", k)
+            slabs[k] = swap(block, VIEW, k)
         for k in range(0, views, 2):
-            slabs[k + 1] = swap(slabs[k], "view", 1)
+            slabs[k + 1] = swap(slabs[k], VIEW, 1)
         return [slabs[k] for k in range(views)]
 
     def shards(features, attend_weight, output_weight, fast_init, update_mask):
@@ -561,7 +565,7 @@
         tokens = features.shape[0]
         half = parts // 2
         staged = views // 2 == heads and heads % 4 == 0
-        ids = jnp.stack([lax.axis_index("view"), lax.axis_index("head")]).astype(jnp.int32)
+        ids = jnp.stack([lax.axis_index(VIEW), lax.axis_index(HEAD)]).astype(jnp.int32)
         o_rows, o_parts = output_weight.shape[1], output_weight.shape[2] // 2 // cols
         payloads = []
         for b in range(blocks):
@@ -575,11 +579,11 @@
             for k in range(1, half):
                 high = 1 << (k.bit_length() - 1)
                 from_k, hop = (0, k) if high == k else (high, k ^ high)
-                near_xs.append(swap(near_xs[from_k], "head", hop))
+                near_xs.append(swap(near_xs[from_k], HEAD, hop))
             for far in far_xs:
-                far[0] = swap(far[0], "head", half)
+                far[0] = swap(far[0], HEAD, half)
                 for k in range(1, half):
-                    far.append(swap(far[0], "head", k))
+                    far.append(swap(far[0], HEAD, k))
             if layer == 0:
                 slabs = gather_view(payloads[0])
                 wt, ft = prepare(ids, slabs, d_slab, f_slab, heads, dim)
@@ -589,7 +593,7 @@
                     shape = (blocks, o_rows, o_parts) if b == 1 else ()
                     later.append(prepare(ids, slabs, d_slab, f_slab, heads, dim, *shape))
                 out_own = later[0][2]
-                out_pair = swap(out_own, "head", 1)
+                out_pair = swap(out_own, HEAD, 1)
             else:
                 wt, ft = later[layer - 1][:2]
             state = front(ids, near_xs, 0, 0, tokens, wt, ft, update_mask, parts)
@@ -600,37 +604,37 @@
             q, k, v, *grads = state
             near = grads[0].astype(F32)
             for i in range(1, views // 2):
-                part = swap(grads[i % heads], "view", 2 * i, lambda _, o: (o >> 1) < heads)
+                part = swap(grads[i % heads], VIEW, 2 * i, lambda _, o: (o >> 1) < heads)
                 near = near + part.astype(F32)
             near = near.astype(BF16)
-            got = swap(near, "view", 1)
+            got = swap(near, VIEW, 1)
             count = half * tokens
             attended = None
             least = count // 2
             for start, n in ((least, 2 * count - least), (0, least)):
                 attended = attend(q, k, v, start, n, attended)
             fresh = newton(ids, ft, near, got)
-            fast = [fresh] + [swap(fresh, "view", 2 * i, lambda i, o: (i >> 1) < heads) for i in range(1, views // 2)]
+            fast = [fresh] + [swap(fresh, VIEW, 2 * i, lambda i, o: (i >> 1) < heads) for i in range(1, views // 2)]
             received, places = [], []
             far_chunks = [(c, 1) for c in range(half)]
             if staged:
                 spans = [(0, half)] + [(c, 1) for c in range(half, parts)]
-                early, *sent = apply_fast(ids, q, attended, fast, heads, "early", tokens, 0, spans)
+                early, *sent = apply_fast(ids, q, attended, fast, heads, EARLY, tokens, 0, spans)
                 for i, x in enumerate(sent, half):
-                    received.append(swap(x, "head", i))
+                    received.append(swap(x, HEAD, i))
                     places.append((i, 0))
-                sent = apply_fast(ids, q, attended, fast, heads, "late", tokens, half, far_chunks)
+                sent = apply_fast(ids, q, attended, fast, heads, LATE, tokens, half, far_chunks)
                 for i, x in enumerate(sent, half):
-                    received.append(swap(x, "head", i))
+                    received.append(swap(x, HEAD, i))
                     places.append((i, 1))
-                mixed = apply_fast(ids, q, attended, fast, heads, "late", tokens, 0, far_chunks, early)
+                mixed = apply_fast(ids, q, attended, fast, heads, LATE, tokens, 0, far_chunks, early)
             else:
-                sent = apply_fast(ids, q, attended, fast, heads, "all", tokens, half, far_chunks)
+                sent = apply_fast(ids, q, attended, fast, heads, ALL, tokens, half, far_chunks)
                 for i, x in enumerate(sent, half):
-                    received.append(swap(x, "head", i))
+                    received.append(swap(x, HEAD, i))
                     places.append((i, None))
-                mixed = apply_fast(ids, q, attended, fast, heads, "all", tokens, 0, far_chunks)
-            near_parts = [x if i == 0 else swap(x, "head", i) for i, x in enumerate(mixed)]
+                mixed = apply_fast(ids, q, attended, fast, heads, ALL, tokens, 0, far_chunks)
+            near_parts = [x if i == 0 else swap(x, HEAD, i) for i, x in enumerate(mixed)]
             received = near_parts + received
             places = [(i, None) for i in range(half)] + places
             more = layer + 1 < blocks
@@ -645,12 +649,12 @@
         shards,
         mesh=mesh,
         in_specs=(
-            P(("view", "head"), None),
-            P(None, None, "view", "head"),
-            P(None, "view", None),
-            P(None, "head", None, None, "view"),
-            P("view", None),
+            P((VIEW, HEAD), None),
+            P(None, None, VIEW, HEAD),
+            P(None, VIEW, None),
+            P(None, HEAD, None, None, VIEW),
+            P(VIEW, None),
         ),
-        out_specs=P(("view", "head"), None),
+        out_specs=P((VIEW, HEAD), None),
         check_vma=False,
     )

time: 362 us -> 362 us (level)
  no operation moved by 1% of the time
where the time goes in v2:
time: 362 us; the launch traced here: 360 us
  Pallas kernels  158 us (44%)
  waiting for transfers between devices  133 us (37%)
  starting transfers between devices  63.6 us (18%)
    ppermute x47, waiting for transfers between devices, swap(): return lax.ppermute(x, axis, pairs)  133 us
    ppermute x47, starting transfers between devices, swap(): return lax.ppermute(x, axis, pairs)  63.6 us
    pallas_call x5, Pallas kernels, front(): pl.pallas_call(functools.partial(front_kernel, heads, dim, chunks, steps,...  56.9 us
    pallas_call x4, Pallas kernels, attend(): pl.pallas_call(functools.partial(attend_kernel, heads, twice // 2), grid=...  44.5 us
    pallas_call x6, Pallas kernels, apply_fast(): pl.pallas_call(functools.partial(apply_kernel, heads, dim, group, stage,...  32.8 us
    pallas_call x2, Pallas kernels, newton(): pl.pallas_call(newton_kernel, grid_spec=pltpu.PrefetchScalarGridSpec(num_...  10.6 us
  transfers between devices with their start and end apart: 47, of which 21 were waited for; matrix products, arithmetic and copies ran while one was open for 1% of the time, Pallas kernels for 37%

profile of v2, /device:TPU:0, one launch (start us, length us, event | category | flops | bytes accessed | tf_op | source)
XLA Modules:
  0.0 359.8 jit_solution(10533775246372557488)
XLA Ops:
  0.0 2.0 pack.3.refs_0_
  2.0 3.1 collective-permute-start.9
  5.1 2.6 collective-permute-start.11
  7.7 1.7 collective-permute-start.8
  9.4 1.5 fusion
  11.3 6.6 %collective-permute-done.9.refs_2_ = bf16[576,256]{1,0:T(8,128)(2,1)S(1)} collective-permute-done((bf16[576,256]{1,0:T(8,128)(2,1)}, bf16[576,256]{1,0:T(8,128)(2,1)S(1)}, u32[]{:S(2)}, u32[]{:S(2)}) %collective-permute-start.9) | collective-permute-done | bytes 294944 | tf_op jit(solution)/shard_map/ppermute | solution.py:552
  17.9 1.7 collective-permute-start.15
  19.6 9.1 %collective-permute-done.11.refs_4_ = bf16[576,256]{1,0:T(8,128)(2,1)S(1)} collective-permute-done((bf16[576,256]{1,0:T(8,128)(2,1)}, bf16[576,256]{1,0:T(8,128)(2,1)S(1)}, u32[]{:S(2)}, u32[]{:S(2)}) %collective-permute-start.11) | collective-permute-done | bytes 294944 | tf_op jit(solution)/shard_map/ppermute | solution.py:552
  28.7 1.5 collective-permute-start.10
  33.6 2.3 pack.2.refs_0_
  35.9 2.5 collective-permute-done.10.refs_3_
  38.4 1.6 collective-permute-start.1
  39.9 1.6 collective-permute-done.12.refs_5_
  41.5 3.7 %collective-permute-start.3 = (bf16[1088,256]{1,0:T(8,128)(2,1)}, bf16[1088,256]{1,0:T(8,128)(2,1)S(1)}, u32[]{:S(2)}, u32[]{:S(2)}) collective-permute-start(bf16[1088,256]{1,0:T(8,128)(2,1)} %pack.2.refs_0_), channel_id=1, source_target_pairs={{0,16},{4,20},{8,24},{12,28},{16,0},{20,4},{24,8},{28,12},{1,17},{... | collective-permute-start | bytes 1671176 | tf_op jit(solution)/shard_map/ppermute | solution.py:552
  48.2 1.7 prepare.3
  49.9 10.6 %collective-permute-done.1.refs_2_ = bf16[1088,256]{1,0:T(8,128)(2,1)S(1)} collective-permute-done((bf16[1088,256]{1,0:T(8,128)(2,1)}, bf16[1088,256]{1,0:T(8,128)(2,1)S(1)}, u32[]{:S(2)}, u32[]{:S(2)}) %collective-permute-start.1) | collective-permute-done | bytes 557088 | tf_op jit(solution)/shard_map/ppermute | solution.py:552
  62.0 20.8 %collective-permute-done.3.refs_4_ = bf16[1088,256]{1,0:T(8,128)(2,1)S(1)} collective-permute-done((bf16[1088,256]{1,0:T(8,128)(2,1)}, bf16[1088,256]{1,0:T(8,128)(2,1)S(1)}, u32[]{:S(2)}, u32[]{:S(2)}) %collective-permute-start.3) | collective-permute-done | bytes 557088 | tf_op jit(solution)/shard_map/ppermute | solution.py:552
  84.8 1.5 collective-permute-start.6
  86.4 14.2 %front.5 = (bf16[2048,256]{1,0:T(8,128)(2,1)S(1)}, bf16[256,2048]{1,0:T(8,128)(2,1)S(1)}, bf16[4,2048,128]{2,1,0:T(8,128)(2,1)S(1)}, f32[4,192,512]{2,1,0:T(8,128)S(1)}) custom-call(s32[2]{0:T(128)S(1)} %copy-done.6, s32[1,2048]{1,0:T(1,128)S(1)} %copy-done.7, bf16[1024,768]{1,0:T(8,128)(2,1)S(1)} %get-tuple-element.55.w_ref, ...), custom_call_target="tpu_custom_call" | custom-call | flops 12884901888 | bytes 6291456 | tf_op jit(solution)/shard_map/front/pallas_call | solution.py:288
  100.6 14.1 %front.6 = (bf16[2048,256]{1,0:T(8,128)(2,1)S(1)}, bf16[256,2048]{1,0:T(8,128)(2,1)S(1)}, bf16[4,2048,128]{2,1,0:T(8,128)(2,1)S(1)}, bf16[192,512]{1,0:T(8,128)(...) custom-call(s32[2]{0:T(128)S(1)} %copy-done.6, ...), custom_call_target="tpu_custom_call", output_to_operand_aliasing={{0}: (7, {}), {1}: (8, {}), {2}: (9, {})} | custom-call | flops 12884901888 | bytes 6291456 | tf_op jit(solution)/shard_map/front/pallas_call | solution.py:288
  114.7 6.3 %collective-permute-start.18 = (bf16[192,512]{1,0:T(8,128)(2,1)S(1)}, bf16[192,512]{1,0:T(8,128)(2,1)S(1)}, u32[]{:S(2)}, u32[]{:S(2)}) collective-permute-start(bf16[192,512]{1,0:T(8,128)(2,1)S(1)} %get-tuple-element.65), channel_id=1, source_target_pairs={{0,8},{4,12},{8,0},{12,4},{16,24},{20,28},{24,16},{28,20},{1,9},{5... | collective-permute-start | bytes 589832 | tf_op jit(solution)/shard_map/ppermute | solution.py:552
  121.5 1.9 collective-permute-start.20
  124.8 4.9 %collective-permute-done.18 = bf16[192,512]{1,0:T(8,128)(2,1)S(1)} collective-permute-done((bf16[192,512]{1,0:T(8,128)(2,1)S(1)}, bf16[192,512]{1,0:T(8,128)(2,1)S(1)}, u32[]{:S(2)}, u32[]{:S(2)}) %collective-permute-start.18) | collective-permute-done | bytes 196640 | tf_op jit(solution)/shard_map/ppermute | solution.py:552
  129.7 8.4 %collective-permute-done.19 = bf16[192,512]{1,0:T(8,128)(2,1)S(1)} collective-permute-done((bf16[192,512]{1,0:T(8,128)(2,1)S(1)}, bf16[192,512]{1,0:T(8,128)(2,1)S(1)}, u32[]{:S(2)}, u32[]{:S(2)}) %collective-permute-start.19) | collective-permute-done | bytes 196640 | tf_op jit(solution)/shard_map/ppermute | solution.py:552
  138.2 1.6 collective-permute-start.21
  139.8 16.7 %attend.4.refs_0_ = bf16[2048,256]{1,0:T(8,128)(2,1)S(1)} custom-call(bf16[2048,256]{1,0:T(8,128)(2,1)S(1)} %get-tuple-element.61.q_ref, bf16[256,2048]{1,0:T(8,128)(2,1)S(1)} %get-tuple-element.62.k_ref, bf16[4,2048,128]{2,1,0:T(8,128)(2,1)S(1)} %get-tuple-element.63.v_ref), custom_call_target="tpu_custom_call" | custom-call | flops 12884901888 | bytes 4194304 | tf_op jit(solution)/shard_map/attend/pallas_call | solution.py:332
  156.5 5.3 %newton.2.refs_0_ = bf16[192,512]{1,0:T(8,128)(2,1)S(1)} custom-call(s32[2]{0:T(128)S(1)} %copy-done.6, bf16[4,3,512,128]{3,2,1,0:T(8,128)(2,1)S(1)} %get-tuple-element.56.ft_ref, bf16[192,512]{1,0:T(8,128)(2,1)S(1)} %add_convert_fusion.1.own_ref, bf16[192,512]{1,0:T(8,128)(2,1)S(1)} %collective-permute-done.21.got_ref), custom_call_target="tpu_custom_call" | custom-call | flops 1073741824 | bytes 2097152 | tf_op jit(solution)/shard_map/newton/pallas_call | solution.py:396
  161.7 4.3 %collective-permute-start.23 = (bf16[192,512]{1,0:T(8,128)(2,1)S(1)}, bf16[192,512]{1,0:T(8,128)(2,1)S(1)}, u32[]{:S(2)}, u32[]{:S(2)}) collective-permute-start(bf16[192,512]{1,0:T(8,128)(2,1)S(1)} %newton.2.refs_0_), channel_id=1, source_target_pairs={{0,16},{4,20},{8,24},{12,28},{16,0},{20,4},{24,8},{28,12},{1,17},{... | collective-permute-start | bytes 589832 | tf_op jit(solution)/shard_map/ppermute | solution.py:552
  166.0 1.9 collective-permute-start.24
  168.0 5.6 %attend.5.a_ref = bf16[2048,256]{1,0:T(8,128)(2,1)S(1)} custom-call(bf16[2048,256]{1,0:T(8,128)(2,1)S(1)} %get-tuple-element.61.q_ref, bf16[256,2048]{1,0:T(8,128)(2,1)S(1)} %get-tuple-element.62.k_ref, bf16[4,2048,128]{2,1,0:T(8,128)(2,1)S(1)} %get-tuple-element.63.v_ref, bf16[2048,256]{1,0:T(8,128)(2,1)S(1)} %attend.4.refs_0_), custom_call_target="tpu_custom_call", output_to_operand_aliasing={{}: (3, {})} | custom-call | flops 4294967296 | bytes 4194304 | tf_op jit(solution)/shard_map/attend/pallas_call | solution.py:332
  173.5 6.6 %collective-permute-done.23.refs_1_.refs_0_ = bf16[192,512]{1,0:T(8,128)(2,1)S(1)} collective-permute-done((bf16[192,512]{1,0:T(8,128)(2,1)S(1)}, bf16[192,512]{1,0:T(8,128)(2,1)S(1)}, u32[]{:S(2)}, u32[]{:S(2)}) %collective-permute-start.23) | collective-permute-done | bytes 196640 | tf_op jit(solution)/shard_map/ppermute | solution.py:552
  180.2 4.2 %shard_map.57 = (bf16[512,128]{1,0:T(8,128)(2,1)S(1)}, bf16[512,128]{1,0:T(8,128)(2,1)S(1)}) custom-call(s32[2]{0:T(128)S(1)} %copy-done.6, bf16[2048,256]{1,0:T(8,128)(2,1)S(1)} %get-tuple-element.61.q_ref, bf16[2048,256]{1,0:T(8,128)(2,1)S(1)} %attend.5.a_ref, bf16[192,512]{1,0:T(8,128)(2,1)S(1)} %collective-permute-done.23.refs_1_.refs_0_, ...), custom_call_target="tpu_custom_call" | custom-call | flops 1610612736 | bytes 2097152 | tf_op jit(solution)/shard_map/pallas_call | solution.py:483
  184.4 1.6 collective-permute-start.28
  186.0 7.9 %shard_map.55 = (bf16[1024,128]{1,0:T(8,128)(2,1)S(1)}, bf16[512,128]{1,0:T(8,128)(2,1)S(1)}, bf16[512,128]{1,0:T(8,128)(2,1)S(1)}) custom-call(s32[2]{0:T(128)S(1)} %copy-done.6, bf16[2048,256]{1,0:T(8,128)(2,1)S(1)} %get-tuple-element.61.q_ref, bf16[2048,256]{1,0:T(8,128)(2,1)S(1)} %attend.5.a_ref, bf16[192,512]{1,0:T(8,128)(2,1)S(1)} %newton.2.refs_0_, ...), custom_call_target="tpu_custom_call" | custom-call | flops 3221225472 | bytes 2097152 | tf_op jit(solution)/shard_map/pallas_call | solution.py:483
  193.9 4.3 %shard_map.56 = (bf16[512,256]{1,0:T(8,128)(2,1)S(1)}, bf16[512,256]{1,0:T(8,128)(2,1)S(1)}) custom-call(s32[2]{0:T(128)S(1)} %copy-done.6, bf16[2048,256]{1,0:T(8,128)(2,1)S(1)} %get-tuple-element.61.q_ref, bf16[2048,256]{1,0:T(8,128)(2,1)S(1)} %attend.5.a_ref, bf16[1024,128]{1,0:T(8,128)(2,1)S(1)} %get-tuple-element.68.refs_0_, ...), custom_call_target="tpu_custom_call" | custom-call | flops 1610612736 | bytes 2097152 | tf_op jit(solution)/shard_map/pallas_call | solution.py:483
  198.9 1.6 collective-permute-start.26
  200.5 3.1 collective-permute-done.29.refs_5_
  203.6 4.0 %collective-permute-done.26.refs_2_ = bf16[512,128]{1,0:T(8,128)(2,1)S(1)} collective-permute-done((bf16[512,128]{1,0:T(8,128)(2,1)S(1)}, bf16[512,128]{1,0:T(8,128)(2,1)S(1)}, u32[]{:S(2)}, u32[]{:S(2)}) %collective-permute-start.26) | collective-permute-done | bytes 131104 | tf_op jit(solution)/shard_map/ppermute | solution.py:552
  207.6 1.6 collective-permute-done.27.refs_3_
  209.2 3.0 project.2
  213.1 1.6 collective-permute-start.30
  214.7 12.8 %collective-permute-done.32.refs_0_ = bf16[256,1024]{1,0:T(8,128)(2,1)S(1)} collective-permute-done((bf16[256,1024]{1,0:T(8,128)(2,1)S(1)}, bf16[256,1024]{1,0:T(8,128)(2,1)S(1)}, u32[]{:S(2)}, u32[]{:S(2)}) %collective-permute-start.32) | collective-permute-done | bytes 524320 | tf_op jit(solution)/shard_map/ppermute | solution.py:552
  227.5 10.3 %collective-permute-done.30.refs_0_ = bf16[256,1024]{1,0:T(8,128)(2,1)S(1)} collective-permute-done((bf16[256,1024]{1,0:T(8,128)(2,1)S(1)}, bf16[256,1024]{1,0:T(8,128)(2,1)S(1)}, u32[]{:S(2)}, u32[]{:S(2)}) %collective-permute-start.30) | collective-permute-done | bytes 524320 | tf_op jit(solution)/shard_map/ppermute | solution.py:552
  237.8 13.2 %front.7 = (bf16[2048,256]{1,0:T(8,128)(2,1)S(1)}, bf16[256,2048]{1,0:T(8,128)(2,1)S(1)}, bf16[4,2048,128]{2,1,0:T(8,128)(2,1)S(1)}, f32[4,192,512]{2,1,0:T(8,128)S(1)}) custom-call(s32[2]{0:T(128)S(1)} %copy-done.6, s32[1,2048]{1,0:T(1,128)S(1)} %copy-done.7, bf16[1024,768]{1,0:T(8,128)(2,1)S(1)} %get-tuple-element.76.w_ref, ...), custom_call_target="tpu_custom_call" | custom-call | flops 12884901888 | bytes 6291456 | tf_op jit(solution)/shard_map/front/pallas_call | solution.py:288
  251.1 7.5 %front.8 = (bf16[2048,256]{1,0:T(8,128)(2,1)S(1)}, bf16[256,2048]{1,0:T(8,128)(2,1)S(1)}, bf16[4,2048,128]{2,1,0:T(8,128)(2,1)S(1)}, f32[4,192,512]{2,1,0:T(8,128)S(1)}) custom-call(s32[2]{0:T(128)S(1)} %copy-done.6, s32[1,2048]{1,0:T(1,128)S(1)} %copy-done.7, ...), custom_call_target="tpu_custom_call", output_to_operand_aliasing={{0}: (7, {}), {1}: (8, {}), {2}: (9, {})} | custom-call | flops 6442450944 | bytes 6291456 | tf_op jit(solution)/shard_map/front/pallas_call | solution.py:288
  258.6 7.9 %front.9 = (bf16[2048,256]{1,0:T(8,128)(2,1)S(1)}, bf16[256,2048]{1,0:T(8,128)(2,1)S(1)}, bf16[4,2048,128]{2,1,0:T(8,128)(2,1)S(1)}, bf16[192,512]{1,0:T(8,128)(...) custom-call(s32[2]{0:T(128)S(1)} %copy-done.6, ...), custom_call_target="tpu_custom_call", output_to_operand_aliasing={{0}: (7, {}), {1}: (8, {}), {2}: (9, {})} | custom-call | flops 6442450944 | bytes 6291456 | tf_op jit(solution)/shard_map/front/pallas_call | solution.py:288
  266.5 3.1 collective-permute-start.35
  270.1 1.9 collective-permute-start.37
  272.1 6.6 %collective-permute-done.35 = bf16[192,512]{1,0:T(8,128)(2,1)S(1)} collective-permute-done((bf16[192,512]{1,0:T(8,128)(2,1)S(1)}, bf16[192,512]{1,0:T(8,128)(2,1)S(1)}, u32[]{:S(2)}, u32[]{:S(2)}) %collective-permute-start.35) | collective-permute-done | bytes 196640 | tf_op jit(solution)/shard_map/ppermute | solution.py:552
  278.7 8.1 %collective-permute-done.36 = bf16[192,512]{1,0:T(8,128)(2,1)S(1)} collective-permute-done((bf16[192,512]{1,0:T(8,128)(2,1)S(1)}, bf16[192,512]{1,0:T(8,128)(2,1)S(1)}, u32[]{:S(2)}, u32[]{:S(2)}) %collective-permute-start.36) | collective-permute-done | bytes 196640 | tf_op jit(solution)/shard_map/ppermute | solution.py:552
  287.5 16.7 %attend.6.refs_0_ = bf16[2048,256]{1,0:T(8,128)(2,1)S(1)} custom-call(bf16[2048,256]{1,0:T(8,128)(2,1)S(1)} %get-tuple-element.89.q_ref, bf16[256,2048]{1,0:T(8,128)(2,1)S(1)} %get-tuple-element.90.k_ref, bf16[4,2048,128]{2,1,0:T(8,128)(2,1)S(1)} %get-tuple-element.91.v_ref), custom_call_target="tpu_custom_call" | custom-call | flops 12884901888 | bytes 4194304 | tf_op jit(solution)/shard_map/attend/pallas_call | solution.py:332
  304.2 5.3 %newton.3.refs_0_ = bf16[192,512]{1,0:T(8,128)(2,1)S(1)} custom-call(s32[2]{0:T(128)S(1)} %copy-done.6, bf16[4,3,512,128]{3,2,1,0:T(8,128)(2,1)S(1)} %get-tuple-element.77.ft_ref, bf16[192,512]{1,0:T(8,128)(2,1)S(1)} %add_convert_fusion.own_ref, bf16[192,512]{1,0:T(8,128)(2,1)S(1)} %collective-permute-done.38.got_ref), custom_call_target="tpu_custom_call" | custom-call | flops 1073741824 | bytes 2097152 | tf_op jit(solution)/shard_map/newton/pallas_call | solution.py:396
  309.5 4.1 %collective-permute-start.39 = (bf16[192,512]{1,0:T(8,128)(2,1)S(1)}, bf16[192,512]{1,0:T(8,128)(2,1)S(1)}, u32[]{:S(2)}, u32[]{:S(2)}) collective-permute-start(bf16[192,512]{1,0:T(8,128)(2,1)S(1)} %newton.3.refs_0_), channel_id=1, source_target_pairs={{0,8},{4,12},{8,0},{12,4},{16,24},{20,28},{24,16},{28,20},{1,9},{5... | collective-permute-start | bytes 589832 | tf_op jit(solution)/shard_map/ppermute | solution.py:552
  313.6 5.6 %attend.7.a_ref = bf16[2048,256]{1,0:T(8,128)(2,1)S(1)} custom-call(bf16[2048,256]{1,0:T(8,128)(2,1)S(1)} %get-tuple-element.89.q_ref, bf16[256,2048]{1,0:T(8,128)(2,1)S(1)} %get-tuple-element.90.k_ref, bf16[4,2048,128]{2,1,0:T(8,128)(2,1)S(1)} %get-tuple-element.91.v_ref, bf16[2048,256]{1,0:T(8,128)(2,1)S(1)} %attend.6.refs_0_), custom_call_target="tpu_custom_call", output_to_operand_aliasing={{}: (3, {})} | custom-call | flops 4294967296 | bytes 4194304 | tf_op jit(solution)/shard_map/attend/pallas_call | solution.py:332
  319.7 1.9 collective-permute-start.41
  321.6 7.9 %shard_map.58 = (bf16[1024,128]{1,0:T(8,128)(2,1)S(1)}, bf16[512,128]{1,0:T(8,128)(2,1)S(1)}, bf16[512,128]{1,0:T(8,128)(2,1)S(1)}) custom-call(s32[2]{0:T(128)S(1)} %copy-done.6, bf16[2048,256]{1,0:T(8,128)(2,1)S(1)} %get-tuple-element.89.q_ref, bf16[2048,256]{1,0:T(8,128)(2,1)S(1)} %attend.7.a_ref, bf16[192,512]{1,0:T(8,128)(2,1)S(1)} %newton.3.refs_0_, ...), custom_call_target="tpu_custom_call" | custom-call | flops 3221225472 | bytes 2097152 | tf_op jit(solution)/shard_map/pallas_call | solution.py:483
  329.5 4.5 %collective-permute-done.40.refs_1_.refs_0_ = bf16[192,512]{1,0:T(8,128)(2,1)S(1)} collective-permute-done((bf16[192,512]{1,0:T(8,128)(2,1)S(1)}, bf16[192,512]{1,0:T(8,128)(2,1)S(1)}, u32[]{:S(2)}, u32[]{:S(2)}) %collective-permute-start.40) | collective-permute-done | bytes 196640 | tf_op jit(solution)/shard_map/ppermute | solution.py:552
  334.0 4.3 %shard_map.59 = (bf16[512,256]{1,0:T(8,128)(2,1)S(1)}, bf16[512,256]{1,0:T(8,128)(2,1)S(1)}) custom-call(s32[2]{0:T(128)S(1)} %copy-done.6, bf16[2048,256]{1,0:T(8,128)(2,1)S(1)} %get-tuple-element.89.q_ref, bf16[2048,256]{1,0:T(8,128)(2,1)S(1)} %attend.7.a_ref, bf16[1024,128]{1,0:T(8,128)(2,1)S(1)} %get-tuple-element.96.refs_0_, ...), custom_call_target="tpu_custom_call" | custom-call | flops 1610612736 | bytes 2097152 | tf_op jit(solution)/shard_map/pallas_call | solution.py:483
  338.3 4.2 %shard_map.60 = (bf16[512,128]{1,0:T(8,128)(2,1)S(1)}, bf16[512,128]{1,0:T(8,128)(2,1)S(1)}) custom-call(s32[2]{0:T(128)S(1)} %copy-done.6, bf16[2048,256]{1,0:T(8,128)(2,1)S(1)} %get-tuple-element.89.q_ref, bf16[2048,256]{1,0:T(8,128)(2,1)S(1)} %attend.7.a_ref, bf16[192,512]{1,0:T(8,128)(2,1)S(1)} %collective-permute-done.40.refs_1_.refs_0_, ...), custom_call_target="tpu_custom_call" | custom-call | flops 1610612736 | bytes 2097152 | tf_op jit(solution)/shard_map/pallas_call | solution.py:483
  346.1 2.9 collective-permute-done.45.refs_4_
  349.0 1.8 collective-permute-done.46.refs_5_
  350.8 3.8 %collective-permute-done.43.refs_2_ = bf16[512,128]{1,0:T(8,128)(2,1)S(1)} collective-permute-done((bf16[512,128]{1,0:T(8,128)(2,1)S(1)}, bf16[512,128]{1,0:T(8,128)(2,1)S(1)}, u32[]{:S(2)}, u32[]{:S(2)}) %collective-permute-start.43) | collective-permute-done | bytes 131104 | tf_op jit(solution)/shard_map/ppermute | solution.py:552
  354.6 1.8 collective-permute-done.44.refs_3_
  356.5 3.3 project.3
  (75 shorter events, 19.3 us)
Async XLA Ops:
  0.0 10.9 %copy-start = (bf16[512,1024]{1,0:T(8,128)(2,1)S(1)}, bf16[512,1024]{1,0:T(8,128)(2,1)}, u32[]{:S(2)}) copy-start(bf16[512,1024]{1,0:T(8,128)(2,1)} %s_ref.1) | copy-start | bytes 3145732
  2.0 15.8 %collective-permute-start.9 = (bf16[576,256]{1,0:T(8,128)(2,1)}, bf16[576,256]{1,0:T(8,128)(2,1)S(1)}, u32[]{:S(2)}, u32[]{:S(2)}) collective-permute-start(bf16[576,256]{1,0:T(8,128)(2,1)} %pack.3.refs_0_), channel_id=1, source_target_pairs={{0,8},{4,12},{8,0},{12,4},{16,24},{20,28},{24,16},{28,20},{1,9},{5... | collective-permute-start | bytes 884744 | tf_op jit(solution)/shard_map/ppermute | solution.py:552
  5.1 23.6 %collective-permute-start.11 = (bf16[576,256]{1,0:T(8,128)(2,1)}, bf16[576,256]{1,0:T(8,128)(2,1)S(1)}, u32[]{:S(2)}, u32[]{:S(2)}) collective-permute-start(bf16[576,256]{1,0:T(8,128)(2,1)} %pack.3.refs_0_), channel_id=1, source_target_pairs={{0,16},{4,20},{8,24},{12,28},{16,0},{20,4},{24,8},{28,12},{1,17},{... | collective-permute-start | bytes 884744 | tf_op jit(solution)/shard_map/ppermute | solution.py:552
  7.7 22.5 %collective-permute-start.13 = (bf16[576,256]{1,0:T(8,128)(2,1)}, bf16[576,256]{1,0:T(8,128)(2,1)S(1)}, u32[]{:S(2)}, u32[]{:S(2)}) collective-permute-start(bf16[576,256]{1,0:T(8,128)(2,1)} %pack.3.refs_0_), channel_id=1, source_target_pairs={{0,24},{4,28},{8,16},{12,20},{16,8},{20,12},{24,0},{28,4},{1,25},{... | collective-permute-start | bytes 884744 | tf_op jit(solution)/shard_map/ppermute | solution.py:552
  7.7 23.1 %collective-permute-start.8 = (bf16[576,256]{1,0:T(8,128)(2,1)}, bf16[576,256]{1,0:T(8,128)(2,1)S(1)}, u32[]{:S(2)}, u32[]{:S(2)}) collective-permute-start(bf16[576,256]{1,0:T(8,128)(2,1)} %pack.3.refs_0_), channel_id=1, source_target_pairs={{0,4},{4,0},{8,12},{12,8},{16,20},{20,16},{24,28},{28,24},{1,5},{5... | collective-permute-start | bytes 884744 | tf_op jit(solution)/shard_map/ppermute | solution.py:552
  10.9 35.7 %copy-start.2 = (bf16[576,256]{1,0:T(8,128)(2,1)S(1)}, bf16[576,256]{1,0:T(8,128)(2,1)}, u32[]{:S(2)}) copy-start(bf16[576,256]{1,0:T(8,128)(2,1)} %pack.3.refs_0_) | copy-start | bytes 884740
  11.2 73.7 %collective-permute-start.17 = (bf16[512,1024]{1,0:T(8,128)(2,1)S(1)}, bf16[512,1024]{1,0:T(8,128)(2,1)}, u32[]{:S(2)}, u32[]{:S(2)}) collective-permute-start(bf16[512,1024]{1,0:T(8,128)(2,1)S(1)} %fusion.1.refs_0_), channel_id=1, source_target_pairs={{0,1},{1,0},{2,3},{3,2},{4,5},{5,4},{6,7},{7,6},{8,9},{9,8},{10,11... | collective-permute-start | bytes 3145736 | tf_op jit(solution)/shard_map/ppermute | solution.py:552
  17.9 68.4 %collective-permute-start.15 = (bf16[512,1024]{1,0:T(8,128)(2,1)S(1)}, bf16[512,1024]{1,0:T(8,128)(2,1)}, u32[]{:S(2)}, u32[]{:S(2)}) collective-permute-start(bf16[512,1024]{1,0:T(8,128)(2,1)S(1)} %fusion.1.refs_0_), channel_id=1, source_target_pairs={{0,2},{1,3},{2,0},{3,1},{4,6},{5,7},{6,4},{7,5},{8,10},{9,11},{10,... | collective-permute-start | bytes 3145736 | tf_op jit(solution)/shard_map/ppermute | solution.py:552
  28.7 9.6 %collective-permute-start.10 = (bf16[576,256]{1,0:T(8,128)(2,1)S(1)}, bf16[576,256]{1,0:T(8,128)(2,1)}, u32[]{:S(2)}, u32[]{:S(2)}) collective-permute-start(bf16[576,256]{1,0:T(8,128)(2,1)S(1)} %collective-permute-done.9.refs_2_), channel_id=1, source_target_pairs={{0,4},{4,0},{8,12},{12,8},{16,20},{20,16},{24,28},{28,24},{1,5},{5... | collective-permute-start | bytes 884744 | tf_op jit(solution)/shard_map/ppermute | solution.py:552
  30.2 11.3 %collective-permute-start.12 = (bf16[576,256]{1,0:T(8,128)(2,1)S(1)}, bf16[576,256]{1,0:T(8,128)(2,1)}, u32[]{:S(2)}, u32[]{:S(2)}) collective-permute-start(bf16[576,256]{1,0:T(8,128)(2,1)S(1)} %collective-permute-done.11.refs_4_), channel_id=1, source_target_pairs={{0,4},{4,0},{8,12},{12,8},{16,20},{20,16},{24,28},{28,24},{1,5},{5... | collective-permute-start | bytes 884744 | tf_op jit(solution)/shard_map/ppermute | solution.py:552
  30.8 0.7 copy-start.3
  31.5 13.8 %collective-permute-start.14 = (bf16[576,256]{1,0:T(8,128)(2,1)S(1)}, bf16[576,256]{1,0:T(8,128)(2,1)}, u32[]{:S(2)}, u32[]{:S(2)}) collective-permute-start(bf16[576,256]{1,0:T(8,128)(2,1)S(1)} %collective-permute-done.13.refs_6_), channel_id=1, source_target_pairs={{0,4},{4,0},{8,12},{12,8},{16,20},{20,16},{24,28},{28,24},{1,5},{5... | collective-permute-start | bytes 884744 | tf_op jit(solution)/shard_map/ppermute | solution.py:552
  33.6 52.8 %copy-start.6 = (s32[2]{0:T(128)S(1)}, s32[2]{0:T(128)}, u32[]{:S(2)}) copy-start(s32[2]{0:T(128)} %pad_add_fusion.refs_0_.ids_ref) | copy-start | bytes 28
  33.6 52.8 %copy-start.7 = (s32[1,2048]{1,0:T(1,128)S(1)}, s32[1,2048]{1,0:T(1,128)}, u32[]{:S(2)}) copy-start(s32[1,2048]{1,0:T(1,128)} %mask_ref.9) | copy-start | bytes 24580
  35.9 24.6 %copy-start.1 = (bf16[1088,256]{1,0:T(8,128)(2,1)S(1)}, bf16[1088,256]{1,0:T(8,128)(2,1)}, u32[]{:S(2)}) copy-start(bf16[1088,256]{1,0:T(8,128)(2,1)} %pack.2.refs_0_) | copy-start | bytes 1671172
  38.4 22.1 %collective-permute-start.1 = (bf16[1088,256]{1,0:T(8,128)(2,1)}, bf16[1088,256]{1,0:T(8,128)(2,1)S(1)}, u32[]{:S(2)}, u32[]{:S(2)}) collective-permute-start(bf16[1088,256]{1,0:T(8,128)(2,1)} %pack.2.refs_0_), channel_id=1, source_target_pairs={{0,8},{4,12},{8,0},{12,4},{16,24},{20,28},{24,16},{28,20},{1,9},{5... | collective-permute-start | bytes 1671176 | tf_op jit(solution)/shard_map/ppermute | solution.py:552
  41.5 41.3 %collective-permute-start.3 = (bf16[1088,256]{1,0:T(8,128)(2,1)}, bf16[1088,256]{1,0:T(8,128)(2,1)S(1)}, u32[]{:S(2)}, u32[]{:S(2)}) collective-permute-start(bf16[1088,256]{1,0:T(8,128)(2,1)} %pack.2.refs_0_), channel_id=1, source_target_pairs={{0,16},{4,20},{8,24},{12,28},{16,0},{20,4},{24,8},{28,12},{1,17},{... | collective-permute-start | bytes 1671176 | tf_op jit(solution)/shard_map/ppermute | solution.py:552
  45.2 39.1 %collective-permute-start.5 = (bf16[1088,256]{1,0:T(8,128)(2,1)}, bf16[1088,256]{1,0:T(8,128)(2,1)S(1)}, u32[]{:S(2)}, u32[]{:S(2)}) collective-permute-start(bf16[1088,256]{1,0:T(8,128)(2,1)} %pack.2.refs_0_), channel_id=1, source_target_pairs={{0,24},{4,28},{8,16},{12,20},{16,8},{20,12},{24,0},{28,4},{1,25},{... | collective-permute-start | bytes 1671176 | tf_op jit(solution)/shard_map/ppermute | solution.py:552
  46.6 1.0 copy-start.4
  47.6 0.6 copy-start.5
  60.5 60.4 %collective-permute-start = (bf16[1088,256]{1,0:T(8,128)(2,1)S(1)}, bf16[1088,256]{1,0:T(8,128)(2,1)S(1)}, u32[]{:S(2)}, u32[]{:S(2)}) collective-permute-start(bf16[1088,256]{1,0:T(8,128)(2,1)S(1)} %copy-done.1), channel_id=1, source_target_pairs={{0,4},{4,0},{8,12},{12,8},{16,20},{20,16},{24,28},{28,24},{1,5},{5... | collective-permute-start | bytes 1671176 | tf_op jit(solution)/shard_map/ppermute | solution.py:552
  82.8 38.7 %collective-permute-start.2 = (bf16[1088,256]{1,0:T(8,128)(2,1)S(1)}, bf16[1088,256]{1,0:T(8,128)(2,1)S(1)}, u32[]{:S(2)}, u32[]{:S(2)}) collective-permute-start(bf16[1088,256]{1,0:T(8,128)(2,1)S(1)} %collective-permute-done.1.refs_2_), channel_id=1, source_target_pairs={{0,4},{4,0},{8,12},{12,8},{16,20},{20,16},{24,28},{28,24},{1,5},{5... | collective-permute-start | bytes 1671176 | tf_op jit(solution)/shard_map/ppermute | solution.py:552
  84.3 39.1 %collective-permute-start.4 = (bf16[1088,256]{1,0:T(8,128)(2,1)S(1)}, bf16[1088,256]{1,0:T(8,128)(2,1)S(1)}, u32[]{:S(2)}, u32[]{:S(2)}) collective-permute-start(bf16[1088,256]{1,0:T(8,128)(2,1)S(1)} %collective-permute-done.3.refs_4_), channel_id=1, source_target_pairs={{0,4},{4,0},{8,12},{12,8},{16,20},{20,16},{24,28},{28,24},{1,5},{5... | collective-permute-start | bytes 1671176 | tf_op jit(solution)/shard_map/ppermute | solution.py:552
  84.8 38.6 %collective-permute-start.6 = (bf16[1088,256]{1,0:T(8,128)(2,1)S(1)}, bf16[1088,256]{1,0:T(8,128)(2,1)S(1)}, u32[]{:S(2)}, u32[]{:S(2)}) collective-permute-start(bf16[1088,256]{1,0:T(8,128)(2,1)S(1)} %collective-permute-done.5.refs_6_), channel_id=1, source_target_pairs={{0,4},{4,0},{8,12},{12,8},{16,20},{20,16},{24,28},{28,24},{1,5},{5... | collective-permute-start | bytes 1671176 | tf_op jit(solution)/shard_map/ppermute | solution.py:552
  86.3 14.2 %collective-permute-start.16 = (bf16[512,1024]{1,0:T(8,128)(2,1)}, bf16[512,1024]{1,0:T(8,128)(2,1)S(1)}, u32[]{:S(2)}, u32[]{:S(2)}) collective-permute-start(bf16[512,1024]{1,0:T(8,128)(2,1)} %collective-permute-done.15.refs_0_), channel_id=1, source_target_pairs={{0,1},{1,0},{2,3},{3,2},{4,5},{5,4},{6,7},{7,6},{8,9},{9,8},{10,11... | collective-permute-start | bytes 3145736 | tf_op jit(solution)/shard_map/ppermute | solution.py:552
  114.7 15.0 %collective-permute-start.18 = (bf16[192,512]{1,0:T(8,128)(2,1)S(1)}, bf16[192,512]{1,0:T(8,128)(2,1)S(1)}, u32[]{:S(2)}, u32[]{:S(2)}) collective-permute-start(bf16[192,512]{1,0:T(8,128)(2,1)S(1)} %get-tuple-element.65), channel_id=1, source_target_pairs={{0,8},{4,12},{8,0},{12,4},{16,24},{20,28},{24,16},{28,20},{1,9},{5... | collective-permute-start | bytes 589832 | tf_op jit(solution)/shard_map/ppermute | solution.py:552
  120.9 17.1 %collective-permute-start.19 = (bf16[192,512]{1,0:T(8,128)(2,1)S(1)}, bf16[192,512]{1,0:T(8,128)(2,1)S(1)}, u32[]{:S(2)}, u32[]{:S(2)}) collective-permute-start(bf16[192,512]{1,0:T(8,128)(2,1)S(1)} %get-tuple-element.66), channel_id=1, source_target_pairs={{0,16},{4,20},{8,24},{12,28},{16,0},{20,4},{24,8},{28,12},{1,17},{... | collective-permute-start | bytes 589832 | tf_op jit(solution)/shard_map/ppermute | solution.py:552
  121.5 16.6 %collective-permute-start.20 = (bf16[192,512]{1,0:T(8,128)(2,1)S(1)}, bf16[192,512]{1,0:T(8,128)(2,1)S(1)}, u32[]{:S(2)}, u32[]{:S(2)}) collective-permute-start(bf16[192,512]{1,0:T(8,128)(2,1)S(1)} %get-tuple-element.67), channel_id=1, source_target_pairs={{0,24},{4,28},{8,16},{12,20},{16,8},{20,12},{24,0},{28,4},{1,25},{... | collective-permute-start | bytes 589832 | tf_op jit(solution)/shard_map/ppermute | solution.py:552
  124.7 84.5 %collective-permute-start.7 = (bf16[2048,512]{1,0:T(8,128)(2,1)S(1)}, bf16[2048,512]{1,0:T(8,128)(2,1)S(1)}, u32[]{:S(2)}, u32[]{:S(2)}) collective-permute-start(bf16[2048,512]{1,0:T(8,128)(2,1)S(1)} %get-tuple-element.54.own_ref), channel_id=1, source_target_pairs={{0,1},{1,0},{2,3},{3,2},{4,5},{5,4},{6,7},{7,6},{8,9},{9,8},{10,11... | collective-permute-start | bytes 6291464 | tf_op jit(solution)/shard_map/ppermute | solution.py:552
  138.2 18.3 %collective-permute-start.21 = (bf16[192,512]{1,0:T(8,128)(2,1)S(1)}, bf16[192,512]{1,0:T(8,128)(2,1)S(1)}, u32[]{:S(2)}, u32[]{:S(2)}) collective-permute-start(bf16[192,512]{1,0:T(8,128)(2,1)S(1)} %add_convert_fusion.1.own_ref), channel_id=1, source_target_pairs={{0,4},{4,0},{8,12},{12,8},{16,20},{20,16},{24,28},{28,24},{1,5},{5... | collective-permute-start | bytes 589832 | tf_op jit(solution)/shard_map/ppermute | solution.py:552
  161.7 18.4 %collective-permute-start.23 = (bf16[192,512]{1,0:T(8,128)(2,1)S(1)}, bf16[192,512]{1,0:T(8,128)(2,1)S(1)}, u32[]{:S(2)}, u32[]{:S(2)}) collective-permute-start(bf16[192,512]{1,0:T(8,128)(2,1)S(1)} %newton.2.refs_0_), channel_id=1, source_target_pairs={{0,16},{4,20},{8,24},{12,28},{16,0},{20,4},{24,8},{28,12},{1,17},{... | collective-permute-start | bytes 589832 | tf_op jit(solution)/shard_map/ppermute | solution.py:552
  166.0 14.1 %collective-permute-start.24 = (bf16[192,512]{1,0:T(8,128)(2,1)S(1)}, bf16[192,512]{1,0:T(8,128)(2,1)S(1)}, u32[]{:S(2)}, u32[]{:S(2)}) collective-permute-start(bf16[192,512]{1,0:T(8,128)(2,1)S(1)} %newton.2.refs_0_), channel_id=1, source_target_pairs={{0,24},{4,28},{8,16},{12,20},{16,8},{20,12},{24,0},{28,4},{1,25},{... | collective-permute-start | bytes 589832 | tf_op jit(solution)/shard_map/ppermute | solution.py:552
  168.0 18.1 %collective-permute-start.22 = (bf16[192,512]{1,0:T(8,128)(2,1)S(1)}, bf16[192,512]{1,0:T(8,128)(2,1)S(1)}, u32[]{:S(2)}, u32[]{:S(2)}) collective-permute-start(bf16[192,512]{1,0:T(8,128)(2,1)S(1)} %newton.2.refs_0_), channel_id=1, source_target_pairs={{0,8},{4,12},{8,0},{12,4},{16,24},{20,28},{24,16},{28,20},{1,9},{5... | collective-permute-start | bytes 589832 | tf_op jit(solution)/shard_map/ppermute | solution.py:552
  184.4 16.1 %collective-permute-start.28 = (bf16[512,128]{1,0:T(8,128)(2,1)S(1)}, bf16[512,128]{1,0:T(8,128)(2,1)S(1)}, u32[]{:S(2)}, u32[]{:S(2)}) collective-permute-start(bf16[512,128]{1,0:T(8,128)(2,1)S(1)} %get-tuple-element.73), channel_id=1, source_target_pairs={{0,2},{1,3},{2,0},{3,1},{4,6},{5,7},{6,4},{7,5},{8,10},{9,11},{10,... | collective-permute-start | bytes 393224 | tf_op jit(solution)/shard_map/ppermute | solution.py:552
  198.2 10.9 %collective-permute-start.25 = (bf16[512,256]{1,0:T(8,128)(2,1)S(1)}, bf16[512,256]{1,0:T(8,128)(2,1)S(1)}, u32[]{:S(2)}, u32[]{:S(2)}) collective-permute-start(bf16[512,256]{1,0:T(8,128)(2,1)S(1)} %get-tuple-element.70), channel_id=1, source_target_pairs={{0,1},{1,0},{2,3},{3,2},{4,5},{5,4},{6,7},{7,6},{8,9},{9,8},{10,11... | collective-permute-start | bytes 786440 | tf_op jit(solution)/shard_map/ppermute | solution.py:552
  198.3 5.2 %collective-permute-start.29 = (bf16[512,128]{1,0:T(8,128)(2,1)S(1)}, bf16[512,128]{1,0:T(8,128)(2,1)S(1)}, u32[]{:S(2)}, u32[]{:S(2)}) collective-permute-start(bf16[512,128]{1,0:T(8,128)(2,1)S(1)} %get-tuple-element.74), channel_id=1, source_target_pairs={{0,3},{1,2},{2,1},{3,0},{4,7},{5,6},{6,5},{7,4},{8,11},{9,10},{10,... | collective-permute-start | bytes 393224 | tf_op jit(solution)/shard_map/ppermute | solution.py:552
  198.9 8.7 %collective-permute-start.26 = (bf16[512,128]{1,0:T(8,128)(2,1)S(1)}, bf16[512,128]{1,0:T(8,128)(2,1)S(1)}, u32[]{:S(2)}, u32[]{:S(2)}) collective-permute-start(bf16[512,128]{1,0:T(8,128)(2,1)S(1)} %get-tuple-element.71), channel_id=1, source_target_pairs={{0,2},{1,3},{2,0},{3,1},{4,6},{5,7},{6,4},{7,5},{8,10},{9,11},{10,... | collective-permute-start | bytes 393224 | tf_op jit(solution)/shard_map/ppermute | solution.py:552
  200.4 8.7 %collective-permute-start.27 = (bf16[512,128]{1,0:T(8,128)(2,1)S(1)}, bf16[512,128]{1,0:T(8,128)(2,1)S(1)}, u32[]{:S(2)}, u32[]{:S(2)}) collective-permute-start(bf16[512,128]{1,0:T(8,128)(2,1)S(1)} %get-tuple-element.72), channel_id=1, source_target_pairs={{0,3},{1,2},{2,1},{3,0},{4,7},{5,6},{6,5},{7,4},{8,11},{9,10},{10,... | collective-permute-start | bytes 393224 | tf_op jit(solution)/shard_map/ppermute | solution.py:552
  212.2 25.6 %collective-permute-start.34 = (bf16[512,1024]{1,0:T(8,128)(2,1)S(1)}, bf16[512,1024]{1,0:T(8,128)(2,1)S(1)}, u32[]{:S(2)}, u32[]{:S(2)}) collective-permute-start(bf16[512,1024]{1,0:T(8,128)(2,1)S(1)} %get-tuple-element.80.refs_0_), channel_id=1, source_target_pairs={{0,1},{1,0},{2,3},{3,2},{4,5},{5,4},{6,7},{7,6},{8,9},{9,8},{10,11... | collective-permute-start | bytes 3145736 | tf_op jit(solution)/shard_map/ppermute | solution.py:552
  212.7 14.8 %collective-permute-start.32 = (bf16[256,1024]{1,0:T(8,128)(2,1)S(1)}, bf16[256,1024]{1,0:T(8,128)(2,1)S(1)}, u32[]{:S(2)}, u32[]{:S(2)}) collective-permute-start(bf16[256,1024]{1,0:T(8,128)(2,1)S(1)} %get-tuple-element.79), channel_id=1, source_target_pairs={{0,2},{1,3},{2,0},{3,1},{4,6},{5,7},{6,4},{7,5},{8,10},{9,11},{10,... | collective-permute-start | bytes 1572872 | tf_op jit(solution)/shard_map/ppermute | solution.py:552
  213.1 24.7 %collective-permute-start.30 = (bf16[256,1024]{1,0:T(8,128)(2,1)S(1)}, bf16[256,1024]{1,0:T(8,128)(2,1)S(1)}, u32[]{:S(2)}, u32[]{:S(2)}) collective-permute-start(bf16[256,1024]{1,0:T(8,128)(2,1)S(1)} %get-tuple-element.78), channel_id=1, source_target_pairs={{0,2},{1,3},{2,0},{3,1},{4,6},{5,7},{6,4},{7,5},{8,10},{9,11},{10,... | collective-permute-start | bytes 1572872 | tf_op jit(solution)/shard_map/ppermute | solution.py:552
  227.5 23.6 %collective-permute-start.33 = (bf16[256,1024]{1,0:T(8,128)(2,1)S(1)}, bf16[256,1024]{1,0:T(8,128)(2,1)S(1)}, u32[]{:S(2)}, u32[]{:S(2)}) collective-permute-start(bf16[256,1024]{1,0:T(8,128)(2,1)S(1)} %collective-permute-done.32.refs_0_), channel_id=1, source_target_pairs={{0,1},{1,0},{2,3},{3,2},{4,5},{5,4},{6,7},{7,6},{8,9},{9,8},{10,11... | collective-permute-start | bytes 1572872 | tf_op jit(solution)/shard_map/ppermute | solution.py:552
  237.8 20.8 %collective-permute-start.31 = (bf16[256,1024]{1,0:T(8,128)(2,1)S(1)}, bf16[256,1024]{1,0:T(8,128)(2,1)S(1)}, u32[]{:S(2)}, u32[]{:S(2)}) collective-permute-start(bf16[256,1024]{1,0:T(8,128)(2,1)S(1)} %collective-permute-done.30.refs_0_), channel_id=1, source_target_pairs={{0,1},{1,0},{2,3},{3,2},{4,5},{5,4},{6,7},{7,6},{8,9},{9,8},{10,11... | collective-permute-start | bytes 1572872 | tf_op jit(solution)/shard_map/ppermute | solution.py:552
  266.5 12.2 %collective-permute-start.35 = (bf16[192,512]{1,0:T(8,128)(2,1)S(1)}, bf16[192,512]{1,0:T(8,128)(2,1)S(1)}, u32[]{:S(2)}, u32[]{:S(2)}) collective-permute-start(bf16[192,512]{1,0:T(8,128)(2,1)S(1)} %get-tuple-element.93), channel_id=1, source_target_pairs={{0,8},{4,12},{8,0},{12,4},{16,24},{20,28},{24,16},{28,20},{1,9},{5... | collective-permute-start | bytes 589832 | tf_op jit(solution)/shard_map/ppermute | solution.py:552
  269.6 17.1 %collective-permute-start.36 = (bf16[192,512]{1,0:T(8,128)(2,1)S(1)}, bf16[192,512]{1,0:T(8,128)(2,1)S(1)}, u32[]{:S(2)}, u32[]{:S(2)}) collective-permute-start(bf16[192,512]{1,0:T(8,128)(2,1)S(1)} %get-tuple-element.94), channel_id=1, source_target_pairs={{0,16},{4,20},{8,24},{12,28},{16,0},{20,4},{24,8},{28,12},{1,17},{... | collective-permute-start | bytes 589832 | tf_op jit(solution)/shard_map/ppermute | solution.py:552
  270.1 16.6 %collective-permute-start.37 = (bf16[192,512]{1,0:T(8,128)(2,1)S(1)}, bf16[192,512]{1,0:T(8,128)(2,1)S(1)}, u32[]{:S(2)}, u32[]{:S(2)}) collective-permute-start(bf16[192,512]{1,0:T(8,128)(2,1)S(1)} %get-tuple-element.95), channel_id=1, source_target_pairs={{0,24},{4,28},{8,16},{12,20},{16,8},{20,12},{24,0},{28,4},{1,25},{... | collective-permute-start | bytes 589832 | tf_op jit(solution)/shard_map/ppermute | solution.py:552
  286.9 17.3 %collective-permute-start.38 = (bf16[192,512]{1,0:T(8,128)(2,1)S(1)}, bf16[192,512]{1,0:T(8,128)(2,1)S(1)}, u32[]{:S(2)}, u32[]{:S(2)}) collective-permute-start(bf16[192,512]{1,0:T(8,128)(2,1)S(1)} %add_convert_fusion.own_ref), channel_id=1, source_target_pairs={{0,4},{4,0},{8,12},{12,8},{16,20},{20,16},{24,28},{28,24},{1,5},{5... | collective-permute-start | bytes 589832 | tf_op jit(solution)/shard_map/ppermute | solution.py:552
  309.5 12.1 %collective-permute-start.39 = (bf16[192,512]{1,0:T(8,128)(2,1)S(1)}, bf16[192,512]{1,0:T(8,128)(2,1)S(1)}, u32[]{:S(2)}, u32[]{:S(2)}) collective-permute-start(bf16[192,512]{1,0:T(8,128)(2,1)S(1)} %newton.3.refs_0_), channel_id=1, source_target_pairs={{0,8},{4,12},{8,0},{12,4},{16,24},{20,28},{24,16},{28,20},{1,9},{5... | collective-permute-start | bytes 589832 | tf_op jit(solution)/shard_map/ppermute | solution.py:552
  319.1 14.9 %collective-permute-start.40 = (bf16[192,512]{1,0:T(8,128)(2,1)S(1)}, bf16[192,512]{1,0:T(8,128)(2,1)S(1)}, u32[]{:S(2)}, u32[]{:S(2)}) collective-permute-start(bf16[192,512]{1,0:T(8,128)(2,1)S(1)} %newton.3.refs_0_), channel_id=1, source_target_pairs={{0,16},{4,20},{8,24},{12,28},{16,0},{20,4},{24,8},{28,12},{1,17},{... | collective-permute-start | bytes 589832 | tf_op jit(solution)/shard_map/ppermute | solution.py:552
  319.7 14.3 %collective-permute-start.41 = (bf16[192,512]{1,0:T(8,128)(2,1)S(1)}, bf16[192,512]{1,0:T(8,128)(2,1)S(1)}, u32[]{:S(2)}, u32[]{:S(2)}) collective-permute-start(bf16[192,512]{1,0:T(8,128)(2,1)S(1)} %newton.3.refs_0_), channel_id=1, source_target_pairs={{0,24},{4,28},{8,16},{12,20},{16,8},{20,12},{24,0},{28,4},{1,25},{... | collective-permute-start | bytes 589832 | tf_op jit(solution)/shard_map/ppermute | solution.py:552
  338.3 18.2 %collective-permute-start.42 = (bf16[512,256]{1,0:T(8,128)(2,1)S(1)}, bf16[512,256]{1,0:T(8,128)(2,1)S(1)}, u32[]{:S(2)}, u32[]{:S(2)}) collective-permute-start(bf16[512,256]{1,0:T(8,128)(2,1)S(1)} %get-tuple-element.98), channel_id=1, source_target_pairs={{0,1},{1,0},{2,3},{3,2},{4,5},{5,4},{6,7},{7,6},{8,9},{9,8},{10,11... | collective-permute-start | bytes 786440 | tf_op jit(solution)/shard_map/ppermute | solution.py:552
  342.6 6.4 %collective-permute-start.45 = (bf16[512,128]{1,0:T(8,128)(2,1)S(1)}, bf16[512,128]{1,0:T(8,128)(2,1)S(1)}, u32[]{:S(2)}, u32[]{:S(2)}) collective-permute-start(bf16[512,128]{1,0:T(8,128)(2,1)S(1)} %get-tuple-element.101), channel_id=1, source_target_pairs={{0,2},{1,3},{2,0},{3,1},{4,6},{5,7},{6,4},{7,5},{8,10},{9,11},{10,... | collective-permute-start | bytes 393224 | tf_op jit(solution)/shard_map/ppermute | solution.py:552
  343.1 7.7 %collective-permute-start.46 = (bf16[512,128]{1,0:T(8,128)(2,1)S(1)}, bf16[512,128]{1,0:T(8,128)(2,1)S(1)}, u32[]{:S(2)}, u32[]{:S(2)}) collective-permute-start(bf16[512,128]{1,0:T(8,128)(2,1)S(1)} %get-tuple-element.102), channel_id=1, source_target_pairs={{0,3},{1,2},{2,1},{3,0},{4,7},{5,6},{6,5},{7,4},{8,11},{9,10},{10,... | collective-permute-start | bytes 393224 | tf_op jit(solution)/shard_map/ppermute | solution.py:552
  344.5 10.2 %collective-permute-start.43 = (bf16[512,128]{1,0:T(8,128)(2,1)S(1)}, bf16[512,128]{1,0:T(8,128)(2,1)S(1)}, u32[]{:S(2)}, u32[]{:S(2)}) collective-permute-start(bf16[512,128]{1,0:T(8,128)(2,1)S(1)} %get-tuple-element.99), channel_id=1, source_target_pairs={{0,2},{1,3},{2,0},{3,1},{4,6},{5,7},{6,4},{7,5},{8,10},{9,11},{10,... | collective-permute-start | bytes 393224 | tf_op jit(solution)/shard_map/ppermute | solution.py:552
  345.0 11.5 %collective-permute-start.44 = (bf16[512,128]{1,0:T(8,128)(2,1)S(1)}, bf16[512,128]{1,0:T(8,128)(2,1)S(1)}, u32[]{:S(2)}, u32[]{:S(2)}) collective-permute-start(bf16[512,128]{1,0:T(8,128)(2,1)S(1)} %get-tuple-element.100), channel_id=1, source_target_pairs={{0,3},{1,2},{2,1},{3,0},{4,7},{5,6},{6,5},{7,4},{8,11},{9,10},{10,... | collective-permute-start | bytes 393224 | tf_op jit(solution)/shard_map/ppermute | solution.py:552
